TPU v7x, 32 devices: a whole 2x2x4 slice. The times are simulated.
32 devices in a mesh: site: 8 (over z, core), sector: 4 (over y, x).
Axes of the slice: x: 2, y: 2, z: 4, core: 2. Of those that a mesh axis runs over, the one named last changes fastest.
Arguments:
- site_tensor: float32 [8, 4, 16, 512, 512], P('site', None, 'sector'), may hold values from -0.25 to 0.25
- outcomes: int32 [6, 8, 128], P(None, 'site'), may hold values from 0 to 3
- in_flight: float32 [8, 128, 8192], P('site', None, 'sector'), may hold values from -6 to 6
- prior_logp: float32 [8, 128], P('site'), may hold values from -30 to 0
- entering: float32 [5, 128, 8192], P(None, None, 'sector'), may hold values from -6 to 6
Outputs:
- final_env: float32 [8, 128, 8192], P('site', None, 'sector')
- final_logp: float32 [8, 128], P('site')
All inputs are finite; a program needn't handle non-finite values.
Results may differ from a plain program's by a relative error of at most 0.0003.
Values sent between devices are 32-bit elements; how exact they have to be, the bound alone decides.
No kernel may reach another device: no remote copies, remote signals or barrier semaphores. Data moves between devices by JAX's collectives and lax.ppermute only.
A program may use at most 64 MiB of HBM per device.

v0:
```python
import jax
import jax.numpy as jnp
from jax import lax
from jax.sharding import PartitionSpec as P

EPSILON = 1e-06


def passed_along(value, axis, steps):
    count = lax.axis_size(axis)
    initial, last = (max(0, -steps), min(count, count - steps))
    return lax.ppermute(value, axis, [(source, source + steps) for source in range(initial, last)])


def sector_products(state_rows, weights, chosen):
    row_count = state_rows.shape[0]
    outcome_count = weights.shape[0]
    local_count = weights.shape[1]
    width = weights.shape[2]
    hop_count = (outcome_count - 2 + local_count) // local_count
    pieces = [state_rows]
    for hop in range(1, hop_count + 1):
        pieces.append(passed_along(state_rows, "sector", -hop))
    joined = jnp.concatenate(pieces, axis=1)
    stacked = jnp.stack(
        [
            joined[:, count * width : (count + local_count) * width]
            for count in range(outcome_count)
        ],
        axis=1,
    )
    stacked = stacked.reshape(row_count, outcome_count, local_count, width)
    amplitude = jnp.einsum("rnsi,nsij->rnsj", stacked, weights, precision=lax.Precision.HIGHEST)
    selector = (chosen[:, None] == jnp.arange(outcome_count, dtype=jnp.int32)[None, :]).astype(
        jnp.float32
    )
    powers = jnp.sum(amplitude * amplitude, axis=(2, 3))
    picked_part = jnp.sum(powers * selector, axis=1)
    total_part = jnp.sum(powers, axis=1)
    selected = jnp.sum(amplitude * selector[:, :, None, None], axis=1)
    return (selected.reshape(row_count, -1), picked_part, total_part)


def step_later(state_rows, log_weight, pending_picked, pending_total, chosen, weights, bond_size):
    picked_sum, total_sum = lax.psum((pending_picked, pending_total), "sector")
    picked_mean = picked_sum / bond_size + EPSILON
    total_mean = total_sum / bond_size + EPSILON
    log_weight = log_weight + jnp.log(picked_mean) - jnp.log(total_mean)
    selected, picked_part, total_part = sector_products(state_rows, weights, chosen)
    scale = lax.rsqrt(picked_mean)
    return (
        selected * scale[:, None],
        log_weight,
        picked_part / picked_mean,
        total_part / picked_mean,
    )


def per_device(site_tensor, outcomes, in_flight, prior_logp, entering):
    weights = site_tensor[0]
    at_start = lax.axis_index("site") == 0
    total_rows = in_flight.shape[1]
    batch_count = 1
    batch_rows = total_rows // batch_count
    bond_size = in_flight.shape[2] * lax.axis_size("sector")
    tick_count = outcomes.shape[0]
    starts = [0]
    states = [in_flight[0, row_start : row_start + batch_rows] for row_start in starts]
    weights_sum = [prior_logp[0, row_start : row_start + batch_rows] for row_start in starts]
    fresh_value = jnp.where(lax.axis_index("sector") == 0, bond_size * (1.0 - EPSILON), 0.0).astype(
        jnp.float32
    )
    fresh_rows = fresh_value * jnp.ones((batch_rows,), jnp.float32)
    pend_picked = [fresh_rows for row_start in starts]
    pend_total = [fresh_rows for row_start in starts]
    for tick_index in range(tick_count):
        batch_index = 0
        row_start = starts[batch_index]
        state_rows = states[batch_index]
        log_weight = weights_sum[batch_index]
        picked_rows = pend_picked[batch_index]
        total_sums = pend_total[batch_index]
        if tick_index > 0:
            state_rows, log_weight, picked_rows, total_sums = passed_along(
                (state_rows, log_weight, picked_rows, total_sums), "site", 1
            )
            state_rows = jnp.where(
                at_start, entering[tick_index - 1, row_start : row_start + batch_rows], state_rows
            )
            log_weight = jnp.where(at_start, jnp.zeros_like(log_weight), log_weight)
            picked_rows = jnp.where(at_start, fresh_rows, picked_rows)
            total_sums = jnp.where(at_start, fresh_rows, total_sums)
        chosen = outcomes[tick_index, 0, row_start : row_start + batch_rows]
        state_rows, log_weight, picked_rows, total_sums = step_later(
            state_rows, log_weight, picked_rows, total_sums, chosen, weights, bond_size
        )
        states[batch_index] = state_rows
        weights_sum[batch_index] = log_weight
        pend_picked[batch_index] = picked_rows
        pend_total[batch_index] = total_sums
    batch_index = 0
    final_picked, final_total = lax.psum(
        (pend_picked[batch_index], pend_total[batch_index]), "sector"
    )
    picked_mean = final_picked / bond_size + EPSILON
    total_mean = final_total / bond_size + EPSILON
    states[batch_index] = states[batch_index] * lax.rsqrt(picked_mean)[:, None]
    weights_sum[batch_index] = weights_sum[batch_index] + jnp.log(picked_mean) - jnp.log(total_mean)
    final_env = states[0][None]
    final_logp = weights_sum[0][None]
    return (final_env, final_logp)


def solution(mesh):
    return jax.shard_map(
        per_device,
        mesh=mesh,
        in_specs=(
            P("site", None, "sector", None, None),
            P(None, "site", None),
            P("site", None, "sector"),
            P("site", None),
            P(None, None, "sector"),
        ),
        out_specs=(P("site", None, "sector"), P("site", None)),
        check_vma=False,
    )
```

profile of v0, /device:TPU:1, one launch (start us, length us, event | category | flops | bytes accessed | tf_op | source)
XLA Modules:
  0.0 465.2 jit_solution(10045141854859963162)
XLA Ops:
  3.9 28.0 %psum.94 = f32[128]{0:T(128)S(1)} all-reduce(f32[128]{0:T(128)S(1)} %mul.159), channel_id=1, replica_groups=mesh['site'=8,'sector'=4] {'sector'}, use_global_device_ids=true, to_apply=%region_1.2 | all-reduce | flops 128 | bytes 1024 | tf_op jit(solution)/shard_map/psum | solution.py:45
  31.9 2.9 fusion.83
  36.8 2.6 copy.79
  39.3 15.5 %fusion.60 = (f32[128]{0:T(128)S(1)}, f32[128,4]{0,1:T(4,128)S(1)}, f32[128,4,512]{2,0,1:T(8,128)}) fusion(f32[128,4]{0,1:T(4,128)S(1)} %get-tuple-element.84, f32[1,4,4,512,512]{4,3,2,1,0:T(8,128)} %param.5, f32[128,1,4,512]{3,0,2,1:T(8,128)} %copy.79, f32[128,1,4,512]{3,0,2,1:T(8,128)S(1)} %copy.78, f32[128,1,4,512]{3,0,2,1:T(8,128)S(1)} %copy.77, ...), kind=kOutput, calls=%fused_computation.72 | convolution fusion | flops 6450576896 | bytes 22024704 | tf_op jit(solution)/shard_map/rnsi,nsij->rnsj/dot_general | solution.py:33
  57.4 5.8 %collective-permute-start.1 = (f32[128,2048]{0,1:T(8,128)}, f32[128,2048]{0,1:T(8,128)}, u32[]{:S(2)}, u32[]{:S(2)}) collective-permute-start(f32[128,2048]{0,1:T(8,128)} %bitcast_multiply_fusion.17), channel_id=1, source_target_pairs={{0,4},{4,8},{8,12},{12,16},{16,20},{20,24},{24,28},{1,5},{5,9},{9,... | collective-permute-start | bytes 3145736 | tf_op jit(solution)/shard_map/ppermute | solution.py:12
  63.3 4.5 fusion.127
  69.0 6.3 %collective-permute-done.1 = f32[128,2048]{0,1:T(8,128)} collective-permute-done((f32[128,2048]{0,1:T(8,128)}, f32[128,2048]{0,1:T(8,128)}, u32[]{:S(2)}, u32[]{:S(2)}) %collective-permute-start.1) | collective-permute-done | bytes 1048608 | tf_op jit(solution)/shard_map/ppermute | solution.py:12
  78.3 4.4 collective-permute-start.3
  83.4 15.8 %psum.95 = f32[128]{0:T(128)S(1)} all-reduce(f32[128]{0:T(128)S(1)} %broadcast_select_fusion.14), channel_id=1, replica_groups=mesh['site'=8,'sector'=4] {'sector'}, use_global_device_ids=true, to_apply=%region_5.6 | all-reduce | flops 128 | bytes 1024 | tf_op jit(solution)/shard_map/psum | solution.py:45
  100.5 3.2 fusion.81
  103.7 2.6 copy.82
  111.4 16.0 %fusion.62 = (f32[128]{0:T(128)S(1)}, f32[128,4]{0,1:T(4,128)S(1)}, f32[128,4,512]{2,0,1:T(8,128)}) fusion(f32[128,4]{0,1:T(4,128)S(1)} %get-tuple-element.83, f32[1,4,4,512,512]{4,3,2,1,0:T(8,128)} %param.5, f32[128,1,4,512]{3,0,2,1:T(8,128)} %copy.84, f32[128,1,4,512]{3,0,2,1:T(8,128)} %copy.83, f32[128,1,4,512]{3,0,2,1:T(8,128)} %copy.82, ...), kind=kOutput, calls=%fused_computation.74 | convolution fusion | flops 6450576896 | bytes 22024704 | tf_op jit(solution)/shard_map/rnsi,nsij->rnsj/dot_general | solution.py:33
  127.4 2.6 copy.85
  132.4 11.5 %collective-permute-start.4 = (f32[128,2048]{0,1:T(8,128)}, f32[128,2048]{0,1:T(8,128)}, u32[]{:S(2)}, u32[]{:S(2)}) collective-permute-start(f32[128,2048]{0,1:T(8,128)} %bitcast_multiply_fusion.16), channel_id=1, source_target_pairs={{0,4},{4,8},{8,12},{12,16},{16,20},{20,24},{24,28},{1,5},{5,9},{9,... | collective-permute-start | bytes 3145736 | tf_op jit(solution)/shard_map/ppermute | solution.py:12
  145.2 10.7 %collective-permute-done.4 = f32[128,2048]{0,1:T(8,128)} collective-permute-done((f32[128,2048]{0,1:T(8,128)}, f32[128,2048]{0,1:T(8,128)}, u32[]{:S(2)}, u32[]{:S(2)}) %collective-permute-start.4) | collective-permute-done | bytes 1048608 | tf_op jit(solution)/shard_map/ppermute | solution.py:12
  158.9 4.4 collective-permute-start.6
  164.0 12.5 %psum.96 = f32[128]{0:T(128)S(1)} all-reduce(f32[128]{0:T(128)S(1)} %broadcast_select_fusion.13), channel_id=1, replica_groups=mesh['site'=8,'sector'=4] {'sector'}, use_global_device_ids=true, to_apply=%region_9.10 | all-reduce | flops 128 | bytes 1024 | tf_op jit(solution)/shard_map/psum | solution.py:45
  177.9 3.1 fusion.79
  181.0 2.6 copy.87
  183.6 2.5 copy.88
  188.7 16.1 %fusion.64 = (f32[128]{0:T(128)S(1)}, f32[128,4]{0,1:T(4,128)S(1)}, f32[128,4,512]{2,0,1:T(8,128)}) fusion(f32[128,4]{0,1:T(4,128)S(1)} %get-tuple-element.82, f32[1,4,4,512,512]{4,3,2,1,0:T(8,128)} %param.5, f32[128,1,4,512]{3,0,2,1:T(8,128)} %copy.89, f32[128,1,4,512]{3,0,2,1:T(8,128)} %copy.88, f32[128,1,4,512]{3,0,2,1:T(8,128)} %copy.87, ...), kind=kOutput, calls=%fused_computation.76 | convolution fusion | flops 6450576896 | bytes 22024704 | tf_op jit(solution)/shard_map/rnsi,nsij->rnsj/dot_general | solution.py:33
  204.8 2.6 copy.90
  209.8 15.9 %collective-permute-start.7 = (f32[128,2048]{0,1:T(8,128)}, f32[128,2048]{0,1:T(8,128)}, u32[]{:S(2)}, u32[]{:S(2)}) collective-permute-start(f32[128,2048]{0,1:T(8,128)} %bitcast_multiply_fusion.15), channel_id=1, source_target_pairs={{0,4},{4,8},{8,12},{12,16},{16,20},{20,24},{24,28},{1,5},{5,9},{9,... | collective-permute-start | bytes 3145736 | tf_op jit(solution)/shard_map/ppermute | solution.py:12
  227.0 10.7 %collective-permute-done.7 = f32[128,2048]{0,1:T(8,128)} collective-permute-done((f32[128,2048]{0,1:T(8,128)}, f32[128,2048]{0,1:T(8,128)}, u32[]{:S(2)}, u32[]{:S(2)}) %collective-permute-start.7) | collective-permute-done | bytes 1048608 | tf_op jit(solution)/shard_map/ppermute | solution.py:12
  240.7 4.4 collective-permute-start.9
  245.8 11.5 %psum.97 = f32[128]{0:T(128)S(1)} all-reduce(f32[128]{0:T(128)S(1)} %broadcast_select_fusion.12), channel_id=1, replica_groups=mesh['site'=8,'sector'=4] {'sector'}, use_global_device_ids=true, to_apply=%region_13.14 | all-reduce | flops 128 | bytes 1024 | tf_op jit(solution)/shard_map/psum | solution.py:45
  258.6 3.1 fusion.77
  261.7 2.6 copy.92
  264.3 2.6 copy.93
  269.4 16.1 %fusion.66 = (f32[128]{0:T(128)S(1)}, f32[128,4]{0,1:T(4,128)S(1)}, f32[128,4,512]{2,0,1:T(8,128)}) fusion(f32[128,4]{0,1:T(4,128)S(1)} %get-tuple-element.81, f32[1,4,4,512,512]{4,3,2,1,0:T(8,128)} %param.5, f32[128,1,4,512]{3,0,2,1:T(8,128)} %copy.94, f32[128,1,4,512]{3,0,2,1:T(8,128)} %copy.93, f32[128,1,4,512]{3,0,2,1:T(8,128)} %copy.92, ...), kind=kOutput, calls=%fused_computation.78 | convolution fusion | flops 6450576896 | bytes 22024704 | tf_op jit(solution)/shard_map/rnsi,nsij->rnsj/dot_general | solution.py:33
  288.2 11.8 %collective-permute-start.10 = (f32[128,2048]{0,1:T(8,128)}, f32[128,2048]{0,1:T(8,128)}, u32[]{:S(2)}, u32[]{:S(2)}) collective-permute-start(f32[128,2048]{0,1:T(8,128)} %bitcast_multiply_fusion.14), channel_id=1, source_target_pairs={{0,4},{4,8},{8,12},{12,16},{16,20},{20,24},{24,28},{1,5},{5,9},{9,... | collective-permute-start | bytes 3145736 | tf_op jit(solution)/shard_map/ppermute | solution.py:12
  300.3 11.7 %collective-permute-done.10 = f32[128,2048]{0,1:T(8,128)} collective-permute-done((f32[128,2048]{0,1:T(8,128)}, f32[128,2048]{0,1:T(8,128)}, u32[]{:S(2)}, u32[]{:S(2)}) %collective-permute-start.10) | collective-permute-done | bytes 1048608 | tf_op jit(solution)/shard_map/ppermute | solution.py:12
  314.7 4.4 collective-permute-start.12
  319.8 12.4 %psum.98 = f32[128]{0:T(128)S(1)} all-reduce(f32[128]{0:T(128)S(1)} %broadcast_select_fusion.11), channel_id=1, replica_groups=mesh['site'=8,'sector'=4] {'sector'}, use_global_device_ids=true, to_apply=%region_17.18 | all-reduce | flops 128 | bytes 1024 | tf_op jit(solution)/shard_map/psum | solution.py:45
  332.6 3.2 fusion.75
  337.3 2.5 copy.98
  342.3 15.8 %fusion.68 = (f32[128]{0:T(128)S(1)}, f32[128,4]{0,1:T(4,128)S(1)}, f32[128,4,512]{2,0,1:T(8,128)}) fusion(f32[128,4]{0,1:T(4,128)S(1)} %get-tuple-element.80, f32[1,4,4,512,512]{4,3,2,1,0:T(8,128)} %param.5, f32[128,1,4,512]{3,0,2,1:T(8,128)} %copy.99, f32[128,1,4,512]{3,0,2,1:T(8,128)} %copy.98, f32[128,1,4,512]{3,0,2,1:T(8,128)S(1)} %copy.97, ...), kind=kOutput, calls=%fused_computation.80 | convolution fusion | flops 6450576896 | bytes 22024704 | tf_op jit(solution)/shard_map/rnsi,nsij->rnsj/dot_general | solution.py:33
  359.8 7.6 %collective-permute-start.13 = (f32[128,2048]{0,1:T(8,128)S(1)}, f32[128,2048]{0,1:T(8,128)}, u32[]{:S(2)}, u32[]{:S(2)}) collective-permute-start(f32[128,2048]{0,1:T(8,128)S(1)} %bitcast_multiply_fusion.13), channel_id=1, source_target_pairs={{0,4},{4,8},{8,12},{12,16},{16,20},{20,24},{24,28},{1,5},{5,9},{9,... | collective-permute-start | bytes 3145736 | tf_op jit(solution)/shard_map/ppermute | solution.py:12
  371.6 7.6 %collective-permute-done.17 = f32[128]{0:T(128)S(1)} collective-permute-done((f32[128]{0:T(128)S(1)}, f32[128]{0:T(128)S(1)}, u32[]{:S(2)}, u32[]{:S(2)}) %collective-permute-start.17) | collective-permute-done | bytes 544 | tf_op jit(solution)/shard_map/ppermute | solution.py:12
  379.2 4.4 collective-permute-start.19
  392.1 2.9 collective-permute-start.25
  395.1 20.9 %psum.99 = f32[128]{0:T(128)S(1)} all-reduce(f32[128]{0:T(128)S(1)} %broadcast_select_fusion.10), channel_id=1, replica_groups=mesh['site'=8,'sector'=4] {'sector'}, use_global_device_ids=true, to_apply=%region_21.22 | all-reduce | flops 128 | bytes 1024 | tf_op jit(solution)/shard_map/psum | solution.py:45
  419.8 2.5 copy.103
  423.6 14.8 %fusion.70 = (f32[128]{0:T(128)S(1)}, f32[128,4]{0,1:T(4,128)S(1)}, f32[128,4,512]{2,0,1:T(8,128)S(1)}) fusion(f32[128,4]{0,1:T(4,128)S(1)} %get-tuple-element.79, f32[1,4,4,512,512]{4,3,2,1,0:T(8,128)} %param.5, f32[128,1,4,512]{3,0,2,1:T(8,128)} %copy.104, f32[128,1,4,512]{3,0,2,1:T(8,128)} %copy.103, f32[128,1,4,512]{3,0,2,1:T(8,128)S(1)} %copy.102, ...), kind=kOutput, calls=%fused_computation.82 | convolution fusion | flops 6450576896 | bytes 22024704 | tf_op jit(solution)/shard_map/rnsi,nsij->rnsj/dot_general | solution.py:33
  438.5 6.9 %all-reduce = (f32[128]{0:T(128)S(1)}, f32[128]{0:T(128)S(1)}, f32[128]{0:T(128)S(1)}, f32[128]{0:T(128)S(1)}, f32[128]{0:T(128)S(1)}, /*index=5*/f32[128]{0:T(128)S(1)}, f32[128]{0:T(128)S(1)}) all-reduce(f32[128]{0:T(128)S(1)} %get-tuple-element.78, ...), channel_id=1, replica_groups=mesh['site'=8,'sector'=4] {'sector'}, use_global_device_ids=true, to_apply=%region_24.25 | all-reduce | flops 896 | bytes 7168 | tf_op jit(solution)/shard_map/psum | solution.py:102
  447.3 3.3 collective-permute-done.18
  453.6 3.8 collective-permute-start.22
  458.1 4.2 collective-permute-start.24
  (120 shorter events, 79.8 us)
Async XLA Ops:
  0.6 31.2 %copy-start.6 = (s32[6,1,128]{2,1,0:T(1,128)S(1)}, s32[6,1,128]{2,1,0:T(1,128)}, u32[]{:S(2)}) copy-start(s32[6,1,128]{2,1,0:T(1,128)} %param.6) | copy-start | bytes 9220
  2.2 29.7 %collective-permute-start = (f32[128,2048]{0,1:T(8,128)S(1)}, f32[128,2048]{0,1:T(8,128)}, u32[]{:S(2)}, u32[]{:S(2)}) collective-permute-start(f32[128,2048]{0,1:T(8,128)S(1)} %bitcast.145), channel_id=1, source_target_pairs={{1,0},{2,1},{3,2},{5,4},{6,5},{7,6},{9,8},{10,9},{11,10},{13,12},{... | collective-permute-start | bytes 3145736 | tf_op jit(solution)/shard_map/ppermute | solution.py:12
  39.3 17.1 %copy-start.7 = (f32[1,128]{1,0:T(1,128)S(1)}, f32[1,128]{1,0:T(1,128)}, u32[]{:S(2)}) copy-start(f32[1,128]{1,0:T(1,128)} %param.8) | copy-start | bytes 1540
  57.4 17.9 %collective-permute-start.1 = (f32[128,2048]{0,1:T(8,128)}, f32[128,2048]{0,1:T(8,128)}, u32[]{:S(2)}, u32[]{:S(2)}) collective-permute-start(f32[128,2048]{0,1:T(8,128)} %bitcast_multiply_fusion.17), channel_id=1, source_target_pairs={{0,4},{4,8},{8,12},{12,16},{16,20},{20,24},{24,28},{1,5},{5,9},{9,... | collective-permute-start | bytes 3145736 | tf_op jit(solution)/shard_map/ppermute | solution.py:12
  77.0 23.6 %collective-permute-start.2 = (f32[128,2048]{0,1:T(8,128)S(1)}, f32[128,2048]{0,1:T(8,128)}, u32[]{:S(2)}, u32[]{:S(2)}) collective-permute-start(f32[128,2048]{0,1:T(8,128)S(1)} %bitcast_select_fusion), channel_id=1, source_target_pairs={{1,0},{2,1},{3,2},{5,4},{6,5},{7,6},{9,8},{10,9},{11,10},{13,12},{... | collective-permute-start | bytes 3145736 | tf_op jit(solution)/shard_map/ppermute | solution.py:12
  78.3 5.1 %collective-permute-start.3 = (f32[128]{0:T(128)S(1)}, f32[128]{0:T(128)S(1)}, u32[]{:S(2)}, u32[]{:S(2)}) collective-permute-start(f32[128]{0:T(128)S(1)} %get-tuple-element.62), channel_id=1, source_target_pairs={{0,4},{4,8},{8,12},{12,16},{16,20},{20,24},{24,28},{1,5},{5,9},{9,... | collective-permute-start | bytes 1544 | tf_op jit(solution)/shard_map/ppermute | solution.py:12
  103.7 7.7 %copy-start.2 = (f32[128,1,4,512]{3,0,2,1:T(8,128)S(1)}, f32[128,1,4,512]{3,0,2,1:T(8,128)}, u32[]{:S(2)}) copy-start(f32[128,1,4,512]{3,0,2,1:T(8,128)} %copy.81) | copy-start | bytes 3145732
  127.4 16.5 %copy-start.1 = (f32[1,128,2048]{2,1,0:T(8,128)S(1)}, f32[1,128,2048]{2,1,0:T(8,128)}, u32[]{:S(2)}) copy-start(f32[1,128,2048]{2,1,0:T(8,128)} %get-tuple-element.30) | copy-start | bytes 3145732
  132.4 23.6 %collective-permute-start.4 = (f32[128,2048]{0,1:T(8,128)}, f32[128,2048]{0,1:T(8,128)}, u32[]{:S(2)}, u32[]{:S(2)}) collective-permute-start(f32[128,2048]{0,1:T(8,128)} %bitcast_multiply_fusion.16), channel_id=1, source_target_pairs={{0,4},{4,8},{8,12},{12,16},{16,20},{20,24},{24,28},{1,5},{5,9},{9,... | collective-permute-start | bytes 3145736 | tf_op jit(solution)/shard_map/ppermute | solution.py:12
  157.6 20.3 %collective-permute-start.5 = (f32[128,2048]{0,1:T(8,128)S(1)}, f32[128,2048]{0,1:T(8,128)}, u32[]{:S(2)}, u32[]{:S(2)}) collective-permute-start(f32[128,2048]{0,1:T(8,128)S(1)} %bitcast_select_fusion.1), channel_id=1, source_target_pairs={{1,0},{2,1},{3,2},{5,4},{6,5},{7,6},{9,8},{10,9},{11,10},{13,12},{... | collective-permute-start | bytes 3145736 | tf_op jit(solution)/shard_map/ppermute | solution.py:12
  158.9 5.1 %collective-permute-start.6 = (f32[128]{0:T(128)S(1)}, f32[128]{0:T(128)S(1)}, u32[]{:S(2)}, u32[]{:S(2)}) collective-permute-start(f32[128]{0:T(128)S(1)} %get-tuple-element.72), channel_id=1, source_target_pairs={{0,4},{4,8},{8,12},{12,16},{16,20},{20,24},{24,28},{1,5},{5,9},{9,... | collective-permute-start | bytes 1544 | tf_op jit(solution)/shard_map/ppermute | solution.py:12
  181.0 7.7 %copy-start.4 = (f32[128,1,4,512]{3,0,2,1:T(8,128)S(1)}, f32[128,1,4,512]{3,0,2,1:T(8,128)}, u32[]{:S(2)}) copy-start(f32[128,1,4,512]{3,0,2,1:T(8,128)} %copy.86) | copy-start | bytes 3145732
  204.8 20.9 %copy-start = (f32[1,128,2048]{2,1,0:T(8,128)S(1)}, f32[1,128,2048]{2,1,0:T(8,128)}, u32[]{:S(2)}) copy-start(f32[1,128,2048]{2,1,0:T(8,128)} %get-tuple-element.31) | copy-start | bytes 3145732
  209.8 27.9 %collective-permute-start.7 = (f32[128,2048]{0,1:T(8,128)}, f32[128,2048]{0,1:T(8,128)}, u32[]{:S(2)}, u32[]{:S(2)}) collective-permute-start(f32[128,2048]{0,1:T(8,128)} %bitcast_multiply_fusion.15), channel_id=1, source_target_pairs={{0,4},{4,8},{8,12},{12,16},{16,20},{20,24},{24,28},{1,5},{5,9},{9,... | collective-permute-start | bytes 3145736 | tf_op jit(solution)/shard_map/ppermute | solution.py:12
  239.4 19.2 %collective-permute-start.8 = (f32[128,2048]{0,1:T(8,128)S(1)}, f32[128,2048]{0,1:T(8,128)}, u32[]{:S(2)}, u32[]{:S(2)}) collective-permute-start(f32[128,2048]{0,1:T(8,128)S(1)} %bitcast_select_fusion.2), channel_id=1, source_target_pairs={{1,0},{2,1},{3,2},{5,4},{6,5},{7,6},{9,8},{10,9},{11,10},{13,12},{... | collective-permute-start | bytes 3145736 | tf_op jit(solution)/shard_map/ppermute | solution.py:12
  240.7 5.1 %collective-permute-start.9 = (f32[128]{0:T(128)S(1)}, f32[128]{0:T(128)S(1)}, u32[]{:S(2)}, u32[]{:S(2)}) collective-permute-start(f32[128]{0:T(128)S(1)} %get-tuple-element.69), channel_id=1, source_target_pairs={{0,4},{4,8},{8,12},{12,16},{16,20},{20,24},{24,28},{1,5},{5,9},{9,... | collective-permute-start | bytes 1544 | tf_op jit(solution)/shard_map/ppermute | solution.py:12
  261.7 7.8 %copy-start.3 = (f32[128,1,4,512]{3,0,2,1:T(8,128)S(1)}, f32[128,1,4,512]{3,0,2,1:T(8,128)}, u32[]{:S(2)}) copy-start(f32[128,1,4,512]{3,0,2,1:T(8,128)} %copy.91) | copy-start | bytes 3145732
  288.2 23.9 %collective-permute-start.10 = (f32[128,2048]{0,1:T(8,128)}, f32[128,2048]{0,1:T(8,128)}, u32[]{:S(2)}, u32[]{:S(2)}) collective-permute-start(f32[128,2048]{0,1:T(8,128)} %bitcast_multiply_fusion.14), channel_id=1, source_target_pairs={{0,4},{4,8},{8,12},{12,16},{16,20},{20,24},{24,28},{1,5},{5,9},{9,... | collective-permute-start | bytes 3145736 | tf_op jit(solution)/shard_map/ppermute | solution.py:12
  313.4 19.2 %collective-permute-start.11 = (f32[128,2048]{0,1:T(8,128)S(1)}, f32[128,2048]{0,1:T(8,128)}, u32[]{:S(2)}, u32[]{:S(2)}) collective-permute-start(f32[128,2048]{0,1:T(8,128)S(1)} %bitcast_select_fusion.3), channel_id=1, source_target_pairs={{1,0},{2,1},{3,2},{5,4},{6,5},{7,6},{9,8},{10,9},{11,10},{13,12},{... | collective-permute-start | bytes 3145736 | tf_op jit(solution)/shard_map/ppermute | solution.py:12
  314.7 5.1 %collective-permute-start.12 = (f32[128]{0:T(128)S(1)}, f32[128]{0:T(128)S(1)}, u32[]{:S(2)}, u32[]{:S(2)}) collective-permute-start(f32[128]{0:T(128)S(1)} %get-tuple-element.66), channel_id=1, source_target_pairs={{0,4},{4,8},{8,12},{12,16},{16,20},{20,24},{24,28},{1,5},{5,9},{9,... | collective-permute-start | bytes 1544 | tf_op jit(solution)/shard_map/ppermute | solution.py:12
  359.8 25.7 %collective-permute-start.13 = (f32[128,2048]{0,1:T(8,128)S(1)}, f32[128,2048]{0,1:T(8,128)}, u32[]{:S(2)}, u32[]{:S(2)}) collective-permute-start(f32[128,2048]{0,1:T(8,128)S(1)} %bitcast_multiply_fusion.13), channel_id=1, source_target_pairs={{0,4},{4,8},{8,12},{12,16},{16,20},{20,24},{24,28},{1,5},{5,9},{9,... | collective-permute-start | bytes 3145736 | tf_op jit(solution)/shard_map/ppermute | solution.py:12
  367.4 11.8 %collective-permute-start.17 = (f32[128]{0:T(128)S(1)}, f32[128]{0:T(128)S(1)}, u32[]{:S(2)}, u32[]{:S(2)}) collective-permute-start(f32[128]{0:T(128)S(1)} %get-tuple-element.63), channel_id=1, source_target_pairs={{0,4},{4,8},{8,12},{12,16},{16,20},{20,24},{24,28},{1,5},{5,9},{9,... | collective-permute-start | bytes 1544 | tf_op jit(solution)/shard_map/ppermute | solution.py:12
  369.7 75.7 %collective-permute-start.16 = (f32[128]{0:T(128)S(1)}, f32[128]{0:T(128)S(1)}, u32[]{:S(2)}, u32[]{:S(2)}) collective-permute-start(f32[128]{0:T(128)S(1)} %get-tuple-element.61), channel_id=1, source_target_pairs={{0,4},{4,8},{8,12},{12,16},{16,20},{20,24},{24,28},{1,5},{5,9},{9,... | collective-permute-start | bytes 1544 | tf_op jit(solution)/shard_map/ppermute | solution.py:12
  379.2 9.0 %collective-permute-start.19 = (f32[128]{0:T(128)S(1)}, f32[128]{0:T(128)S(1)}, u32[]{:S(2)}, u32[]{:S(2)}) collective-permute-start(f32[128]{0:T(128)S(1)} %get-tuple-element.71), channel_id=1, source_target_pairs={{0,4},{4,8},{8,12},{12,16},{16,20},{20,24},{24,28},{1,5},{5,9},{9,... | collective-permute-start | bytes 1544 | tf_op jit(solution)/shard_map/ppermute | solution.py:12
  383.6 6.5 %collective-permute-start.21 = (f32[128]{0:T(128)S(1)}, f32[128]{0:T(128)S(1)}, u32[]{:S(2)}, u32[]{:S(2)}) collective-permute-start(f32[128]{0:T(128)S(1)} %get-tuple-element.68), channel_id=1, source_target_pairs={{0,4},{4,8},{8,12},{12,16},{16,20},{20,24},{24,28},{1,5},{5,9},{9,... | collective-permute-start | bytes 1544 | tf_op jit(solution)/shard_map/ppermute | solution.py:12
  386.9 29.4 %collective-permute-start.14 = (f32[128,2048]{0,1:T(8,128)S(1)}, f32[128,2048]{0,1:T(8,128)S(1)}, u32[]{:S(2)}, u32[]{:S(2)}) collective-permute-start(f32[128,2048]{0,1:T(8,128)S(1)} %bitcast_select_fusion.4), channel_id=1, source_target_pairs={{1,0},{2,1},{3,2},{5,4},{6,5},{7,6},{9,8},{10,9},{11,10},{13,12},{... | collective-permute-start | bytes 3145736 | tf_op jit(solution)/shard_map/ppermute | solution.py:12
  388.2 3.9 collective-permute-start.23
  390.2 4.9 %collective-permute-start.15 = (f32[128]{0:T(128)S(1)}, f32[128]{0:T(128)S(1)}, u32[]{:S(2)}, u32[]{:S(2)}) collective-permute-start(f32[128]{0:T(128)S(1)} %get-tuple-element.75), channel_id=1, source_target_pairs={{0,4},{4,8},{8,12},{12,16},{16,20},{20,24},{24,28},{1,5},{5,9},{9,... | collective-permute-start | bytes 1544 | tf_op jit(solution)/shard_map/ppermute | solution.py:12
  392.1 23.8 %collective-permute-start.25 = (f32[128]{0:T(128)S(1)}, f32[128]{0:T(128)S(1)}, u32[]{:S(2)}, u32[]{:S(2)}) collective-permute-start(f32[128]{0:T(128)S(1)} %get-tuple-element.74), channel_id=1, source_target_pairs={{0,4},{4,8},{8,12},{12,16},{16,20},{20,24},{24,28},{1,5},{5,9},{9,... | collective-permute-start | bytes 1544 | tf_op jit(solution)/shard_map/ppermute | solution.py:12
  418.1 4.2 copy-start.5
  445.4 5.2 %collective-permute-start.18 = (f32[128]{0:T(128)S(1)}, f32[128]{0:T(128)S(1)}, u32[]{:S(2)}, u32[]{:S(2)}) collective-permute-start(f32[128]{0:T(128)S(1)} %fusion.92), channel_id=1, source_target_pairs={{0,4},{4,8},{8,12},{12,16},{16,20},{20,24},{24,28},{1,5},{5,9},{9,... | collective-permute-start | bytes 1544 | tf_op jit(solution)/shard_map/ppermute | solution.py:12
  450.6 3.1 collective-permute-start.20
  453.6 4.5 collective-permute-start.22
  458.1 4.9 %collective-permute-start.24 = (f32[128]{0:T(128)S(1)}, f32[128]{0:T(128)S(1)}, u32[]{:S(2)}, u32[]{:S(2)}) collective-permute-start(f32[128]{0:T(128)S(1)} %fusion.98), channel_id=1, source_target_pairs={{0,4},{4,8},{8,12},{12,16},{16,20},{20,24},{24,28},{1,5},{5,9},{9,... | collective-permute-start | bytes 1544 | tf_op jit(solution)/shard_map/ppermute | solution.py:12
where the time goes:
time: 473 us; the launch traced here: 465 us
  blocking collectives  108 us (23%)
  starting transfers between devices  107 us (23%)
  matrix products  94.4 us (20%)
  local copies, waits for them, and re-layouts  66.9 us (14%)
  waiting for transfers between devices  55.3 us (12%)
  other arithmetic  32.6 us (7%)
    ppermute x26, starting transfers between devices, passed_along(): lax.ppermute(value, axis, [(source, source + steps) for source in range(i...  107 us
    psum x6, blocking collectives, step_later(): picked_sum, total_sum = lax.psum((pending_picked, pending_total), 'sector')  101 us
    dot_general x6, matrix products, sector_products(): jnp.einsum('rnsi,nsij->rnsj', stacked, weights, precision=lax.Precision.H...  94.4 us
    ppermute x26, waiting for transfers between devices, passed_along(): lax.ppermute(value, axis, [(source, source + steps) for source in range(i...  55.3 us
    another operation x24, local copies, waits for them, and re-layouts, sector_products(): jnp.stack([joined[:, count * width:(count + local_count) * width] for cou...  44.7 us
    concatenate x6, other arithmetic, sector_products(): joined = jnp.concatenate(pieces, axis=1)  17.3 us
    reduce_sum x6, local copies, waits for them, and re-layouts, sector_products(): selected = jnp.sum(amplitude * selector[:, :, None, None], axis=1)  10.2 us
  transfers between devices with their start and end apart: 26, of which 13 were waited for; matrix products, arithmetic and copies ran while one was open for 8% of the time, Pallas kernels for 0%

commit v1 on v0

v1 whole, which is shorter than its diff:
```python
import functools
import jax
import jax.numpy as jnp
from jax import lax
from jax.experimental import pallas as pl
from jax.experimental.pallas import tpu as pltpu
from jax.sharding import PartitionSpec as P

EPSILON = 1e-06
SCALE = 256.0
LANES = 128
CHUNKS = 2
BF = jnp.bfloat16
F32 = jnp.float32
AXES = ("site", "sector")


def split_kernel(w_ref, hi_ref, lo_ref):
    w = w_ref[...]
    hi = w.astype(BF)
    hi_ref[...] = hi
    lo_ref[...] = (w - hi.astype(F32)).astype(BF)


def split_weights(w):
    count, width, _ = w.shape
    spec = pl.BlockSpec((1, width, width), lambda i: (i, 0, 0))
    shape = jax.ShapeDtypeStruct(w.shape, BF)
    return pl.pallas_call(
        split_kernel,
        grid=(count,),
        in_specs=[spec],
        out_specs=[spec, spec],
        out_shape=[shape, shape],
        name="split_weights",
        cost_estimate=pl.CostEstimate(flops=w.size, bytes_accessed=8 * w.size, transcendentals=0),
    )(w)


def step_kernel(dims, tick, first, last, flags, *refs):
    n_out, local, width, rows, halo = dims
    refs = list(refs)
    choice_ref = refs.pop(0)
    main_ref = refs.pop(0)
    halo_refs = [refs.pop(0) for _ in halo]
    start_ref = None if first else refs.pop(0)
    next_ref = None if last else refs.pop(0)
    hi_ref, lo_ref = refs.pop(0), refs.pop(0)
    out_ref = refs.pop(0)
    part_ref = refs.pop(0) if last else None
    edge_ref = None if last else refs.pop(0)
    stack = refs.pop(0)
    s = pl.program_id(0)

    @pl.when(s == 0)
    def _():
        def put(index, value):
            hi = value.astype(BF)
            stack[index, :rows] = hi
            stack[index, rows:] = (value - hi.astype(F32)).astype(BF)

        for q in range(local):
            cols = slice(q * width, (q + 1) * width)
            if first:
                value = main_ref[:, cols] * SCALE
            else:
                value = jnp.where(flags[0] == 1, start_ref[:, cols] * SCALE, main_ref[:, cols])
            put(q, value)
        index = local
        for ref, blocks in zip(halo_refs, halo):
            for q in range(blocks):
                value = ref[:, q * width : (q + 1) * width]
                if first:
                    value = value * SCALE
                put(index, value)
                index += 1

    choice = choice_ref[:, tick : tick + 1]
    selected = None
    picked = jnp.zeros((rows, 1), F32)
    total = jnp.zeros((rows, 1), F32)
    for n in range(n_out):
        both = stack[s + n]
        top = both[:rows]
        wide = jnp.dot(both, hi_ref[n, 0], preferred_element_type=F32)
        value = wide[:rows] + wide[rows:]
        value = value + jnp.dot(top, lo_ref[n, 0], preferred_element_type=F32)
        power = jnp.sum(value * value, axis=1, keepdims=True)
        mine = choice == n
        total = total + power
        picked = jnp.where(mine, power, picked)
        selected = jnp.where(mine, value, 0.0) if n == 0 else jnp.where(mine, value, selected)
    base = pl.multiple_of(s * width, LANES)
    out_ref[:, pl.ds(base, width)] = selected
    if not last:
        for q in range(halo[0]):

            @pl.when(s == q)
            def _():
                cols = slice(q * width, (q + 1) * width)
                edge_ref[:, cols] = jnp.where(flags[1] == 1, next_ref[:, cols] * SCALE, selected)

    lane = lax.broadcasted_iota(jnp.int32, (rows, LANES), 1)
    new = jnp.where(lane == 2 * tick, picked, jnp.where(lane == 2 * tick + 1, total, 0.0))
    dest = part_ref if last else out_ref
    where = slice(None) if last else slice(local * width, local * width + LANES)

    @pl.when(s == 0)
    def _():
        if first:
            old = jnp.zeros((rows, LANES), F32)
        else:
            old = main_ref[:, local * width : local * width + LANES]
            old = jnp.where(flags[0] == 1, 0.0, old)
        dest[:, where] = old + new

    @pl.when(s > 0)
    def _():
        dest[:, where] = dest[:, where] + new


def step(dims, tick, ticks, flags, choice, main, halos, entering, chunk, weights):
    n_out, local, width, rows, halo = dims
    first, last = tick == 0, tick == ticks - 1
    span = local * width
    whole = lambda shape: pl.BlockSpec(shape, lambda s, f: (0,) * len(shape))
    row_block = lambda cols: pl.BlockSpec((rows, cols), lambda s, f: (chunk, 0))
    operands = [choice, main]
    specs = [row_block(choice.shape[1])]
    if first:
        specs.append(row_block(span))
    else:
        specs.append(whole(main.shape))
    for value in halos:
        operands.append(value)
        specs.append(whole(value.shape))
    if not first:
        operands.append(entering)
        specs.append(pl.BlockSpec((None, rows, span), lambda s, f, t=tick - 1: (t, chunk, 0)))
    if not last:
        operands.append(entering)
        specs.append(pl.BlockSpec((None, rows, halo[0] * width), lambda s, f, t=tick: (t, chunk, 0)))
    for value in weights:
        operands.append(value)
        specs.append(pl.BlockSpec((n_out, 1, width, width), lambda s, f: (0, s, 0, 0)))
    if last:
        shapes = [(rows, span), (rows, LANES)]
    else:
        shapes = [(rows, span + LANES), (rows, halo[0] * width)]
    blocks = local + sum(halo)
    return pl.pallas_call(
        functools.partial(step_kernel, dims, tick, first, last),
        grid_spec=pltpu.PrefetchScalarGridSpec(
            num_scalar_prefetch=1,
            grid=(local,),
            in_specs=specs,
            out_specs=[whole(shape) for shape in shapes],
            scratch_shapes=[pltpu.VMEM((blocks, 2 * rows, width), BF)],
        ),
        out_shape=[jax.ShapeDtypeStruct(shape, F32) for shape in shapes],
        name=f"step_{tick}_{chunk}",
        cost_estimate=pl.CostEstimate(
            flops=6 * rows * n_out * local * width * width,
            bytes_accessed=4 * n_out * local * width * width,
            transcendentals=0,
        ),
    )(flags, *operands)


def final_kernel(ticks, bond, chunks, *refs):
    state_refs = refs[:chunks]
    part_refs = refs[chunks : 2 * chunks]
    prior_ref, env_ref, logp_ref = refs[2 * chunks :]
    rows = state_refs[0].shape[0]
    scale = 1.0 / (bond * SCALE * SCALE)
    for c in range(chunks):
        sums = part_refs[c][...].T * scale
        own = slice(c * rows, (c + 1) * rows)
        log_weight = prior_ref[:, own]
        factor = jnp.ones((1, rows), F32)
        for t in range(ticks):
            picked = sums[2 * t : 2 * t + 1] * factor * factor + EPSILON
            total = sums[2 * t + 1 : 2 * t + 2] * factor * factor + EPSILON
            log_weight = log_weight + jnp.log(picked) - jnp.log(total)
            factor = factor * lax.rsqrt(picked)
        logp_ref[:, own] = log_weight
        column = jnp.broadcast_to(factor, (LANES, rows)).T[:, :1]
        env_ref[0, own] = state_refs[c][...] * (column * (1.0 / SCALE))


def finish(states, parts, prior, ticks, bond):
    rows = sum(value.shape[0] for value in states)
    span = states[0].shape[1]
    return pl.pallas_call(
        functools.partial(final_kernel, ticks, float(bond), len(states)),
        out_shape=[
            jax.ShapeDtypeStruct((1, rows, span), F32),
            jax.ShapeDtypeStruct((1, rows), F32),
        ],
        name="finish",
    )(*states, *parts, prior)


def per_device(sites, sectors, site_tensor, outcomes, in_flight, prior_logp, entering):
    weights = site_tensor[0]
    n_out, local, width = weights.shape[:3]
    span = in_flight.shape[2]
    total_rows = in_flight.shape[1]
    ticks = outcomes.shape[0]
    rows = total_rows // CHUNKS
    need = n_out - 1
    halo = []
    while need > 0:
        halo.append(min(local, need))
        need -= halo[-1]
    dims = (n_out, local, width, rows, tuple(halo))
    place = lambda k, d: k * sectors + d
    main_pairs = [(place(k, d), place(k + 1, d)) for k in range(sites - 1) for d in range(sectors)]

    def halo_pairs(hop, shift):
        return [
            (place(k, d + hop), place((k + shift) % sites, d))
            for k in range(sites)
            for d in range(sectors - hop)
        ]

    def halo_moved(edge, shift):
        return [
            lax.ppermute(edge[:, : blocks * width], AXES, halo_pairs(hop + 1, shift))
            for hop, blocks in enumerate(halo)
        ]

    site = lax.axis_index("site")
    flags = jnp.stack([site == 0, site == sites - 1]).astype(jnp.int32)
    choice = outcomes[:, 0].T
    prior = lax.ppermute(
        prior_logp, "site", [(k, k + ticks - 1) for k in range(sites - ticks + 1)]
    )
    halos = [
        halo_moved(in_flight[0, c * rows : (c + 1) * rows, : halo[0] * width], 0)
        for c in range(CHUNKS)
    ]
    split = split_weights(weights.reshape(n_out * local, width, width))
    split = [value.reshape(weights.shape) for value in split]
    mains = [in_flight[0]] * CHUNKS
    parts = [None] * CHUNKS
    for tick in range(ticks):
        for c in range(CHUNKS):
            main, other = step(
                dims, tick, ticks, flags, choice, mains[c], halos[c], entering, c, split
            )
            if tick < ticks - 1:
                mains[c] = lax.ppermute(main, AXES, main_pairs)
                halos[c] = halo_moved(other, 1)
            else:
                mains[c] = main
                parts[c] = lax.psum(other, "sector")
    return tuple(finish(mains, parts, prior, ticks, span * sectors))


def solution(mesh):
    sizes = (mesh.shape["site"], mesh.shape["sector"])
    return jax.shard_map(
        functools.partial(per_device, *sizes),
        mesh=mesh,
        in_specs=(
            P("site", None, "sector", None, None),
            P(None, "site", None),
            P("site", None, "sector"),
            P("site", None),
            P(None, None, "sector"),
        ),
        out_specs=(P("site", None, "sector"), P("site", None)),
        check_vma=False,
    )
```

time: 473 us -> 339 us (0.72); the launches traced: 465 us -> 337 us
  Pallas kernels: 0 us -> 141 us
  blocking collectives: 108 us -> 0 us
  matrix products: 94.4 us -> 0 us
  starting transfers between devices: 107 us -> 40.9 us
  waiting for transfers between devices: 55.3 us -> 120 us
  local copies, waits for them, and re-layouts: 66.9 us -> 19.7 us
  other arithmetic: 32.6 us -> 0.59 us
  between operations: 1.45 us -> 14.4 us
    pallas_call x0 -> x14, Pallas kernels: none -> 141 us  [the longest x12 121 us: step(): pl.pallas_call(functools.partial(step_kernel, dims, tick, first, last), g...]
    psum x7 -> x0, blocking collectives: 108 us -> none  [the longest x6 101 us: step_later(): picked_sum, total_sum = lax.psum((pending_picked, pending_total), 'sector')]
    dot_general x6 -> x0, matrix products: 94.4 us -> none  [sector_products(): jnp.einsum('rnsi,nsij->rnsj', stacked, weights, precision=lax.Precision.H...]
    ppermute x26 -> x23, starting transfers between devices: 107 us -> 40.8 us  [the longest x10 24 us: per_device(): mains[c] = lax.ppermute(main, AXES, main_pairs)]
    another operation x24 -> x0, local copies, waits for them, and re-layouts: 44.7 us -> none  [sector_products(): jnp.stack([joined[:, count * width:(count + local_count) * width] for cou...]
    psum x0 -> x1, waiting for transfers between devices: none -> 37.4 us  [per_device(): parts[c] = lax.psum(other, 'sector')]
    ppermute x26 -> x23, waiting for transfers between devices: 55.3 us -> 82.7 us  [the longest x12 82 us: halo_moved(): lax.ppermute(edge[:, :blocks * width], AXES, halo_pairs(hop + 1, shift))]
    concatenate x6 -> x0, other arithmetic: 17.3 us -> none  [sector_products(): joined = jnp.concatenate(pieces, axis=1)]
  transfers between devices with their start and end apart: 26 -> 24, of which waited for: 13 -> 7; matrix products, arithmetic and copies ran while one was open for 8% -> 1% of each run, Pallas kernels for 0% -> 38%
where the time goes in v1:
time: 339 us; the launch traced here: 337 us
  Pallas kernels  141 us (42%)
  waiting for transfers between devices  120 us (35%)
  starting transfers between devices  40.9 us (12%)
  local copies, waits for them, and re-layouts  19.7 us (6%)
  between operations  14.4 us (4%)
    pallas_call x12, Pallas kernels, step(): pl.pallas_call(functools.partial(step_kernel, dims, tick, first, last), g...  121 us
    ppermute x12, waiting for transfers between devices, halo_moved(): lax.ppermute(edge[:, :blocks * width], AXES, halo_pairs(hop + 1, shift))  82 us
    psum x1, waiting for transfers between devices, per_device(): parts[c] = lax.psum(other, 'sector')  37.4 us
    ppermute x10, starting transfers between devices, per_device(): mains[c] = lax.ppermute(main, AXES, main_pairs)  24 us
    unnamed x59, local copies, waits for them, and re-layouts  18.5 us
    pallas_call x1, Pallas kernels, split_weights(): pl.pallas_call(split_kernel, grid=(count,), in_specs=[spec], out_specs=[s...  17.3 us
    ppermute x12, starting transfers between devices, halo_moved(): lax.ppermute(edge[:, :blocks * width], AXES, halo_pairs(hop + 1, shift))  15.5 us
  transfers between devices with their start and end apart: 24, of which 7 were waited for; matrix products, arithmetic and copies ran while one was open for 1% of the time, Pallas kernels for 38%

profile of v1, /device:TPU:1, one launch (start us, length us, event | category | flops | bytes accessed | tf_op | source)
XLA Modules:
  0.0 337.0 jit_solution(13832880270459386939)
XLA Ops:
  7.2 1.2 slice_bitcast_fusion
  8.4 1.3 collective-permute-start.11
  9.7 1.3 collective-permute-start
  11.0 1.4 copy.7
  12.4 17.3 %split_weights.1 = (bf16[16,512,512]{2,1,0:T(8,128)(2,1)}, bf16[16,512,512]{2,1,0:T(8,128)(2,1)}) custom-call(f32[16,512,512]{2,1,0:T(8,128)} %bitcast.37), custom_call_target="tpu_custom_call" | custom-call | flops 4194304 | bytes 33554432 | tf_op jit(solution)/shard_map/split_weights/pallas_call | solution.py:29
  31.1 10.1 %step_0_1.1 = (f32[64,2176]{1,0:T(8,128)}, f32[64,1536]{1,0:T(8,128)}) custom-call(s32[2]{0:T(128)} %add_convert_fusion.flags, s32[128,6]{1,0:T(8,128)} %bitcast.38, f32[128,2048]{1,0:T(8,128)} %bitcast.50, f32[64,1536]{1,0:T(8,128)} %copy-done.11, f32[5,128,2048]{2,1,0:T(8,128)} %refs_3_.23, bf16[4,4,512,512]{3,2,1,0:T(8,128)(2,1)} %bitcast.13, ...), custom_call_target="tpu_custom_call" | custom-call | flops 1610612736 | bytes 16777216 | tf_op jit(solution)/shard_map/step_0_1/pallas_call | solution.py:151
  41.2 4.7 %collective-permute-start.12 = (f32[64,2176]{1,0:T(8,128)}, f32[64,2176]{1,0:T(8,128)S(1)}, u32[]{:S(2)}, u32[]{:S(2)}) collective-permute-start(f32[64,2176]{1,0:T(8,128)} %get-tuple-element.41), channel_id=1, source_target_pairs={{0,4},{1,5},{2,6},{3,7},{4,8},{5,9},{6,10},{7,11},{8,12},{9,13},{1... | collective-permute-start | bytes 1671176 | tf_op jit(solution)/shard_map/ppermute | solution.py:253
  46.6 10.0 %step_0_0.1 = (f32[64,2176]{1,0:T(8,128)}, f32[64,1536]{1,0:T(8,128)}) custom-call(s32[2]{0:T(128)} %add_convert_fusion.flags, s32[128,6]{1,0:T(8,128)} %bitcast.39, f32[128,2048]{1,0:T(8,128)} %bitcast.51, f32[64,1536]{1,0:T(8,128)} %copy-done.10, f32[5,128,2048]{2,1,0:T(8,128)} %refs_3_.23, bf16[4,4,512,512]{3,2,1,0:T(8,128)(2,1)} %bitcast.14, ...), custom_call_target="tpu_custom_call" | custom-call | flops 1610612736 | bytes 16777216 | tf_op jit(solution)/shard_map/step_0_0/pallas_call | solution.py:151
  56.6 1.9 collective-permute-start.1
  58.6 1.3 collective-permute-start.13
  59.9 1.3 collective-permute-start.2
  61.2 16.6 %collective-permute-done.13.refs_2_ = f32[64,1536]{1,0:T(8,128)S(1)} collective-permute-done((f32[64,1536]{1,0:T(8,128)S(1)}, f32[64,1536]{1,0:T(8,128)S(1)}, u32[]{:S(2)}, u32[]{:S(2)}) %collective-permute-start.13) | collective-permute-done | bytes 393248 | tf_op jit(solution)/shard_map/ppermute | solution.py:229
  78.5 0.8 copy-done.9
  79.3 10.2 %step_1_1.1 = (f32[64,2176]{1,0:T(8,128)}, f32[64,1536]{1,0:T(8,128)}) custom-call(s32[2]{0:T(128)} %add_convert_fusion.flags, s32[128,6]{1,0:T(8,128)} %bitcast.40, f32[64,2176]{1,0:T(8,128)} %copy-done.9, f32[64,1536]{1,0:T(8,128)} %copy-done.17, f32[5,128,2048]{2,1,0:T(8,128)} %refs_3_.23, f32[5,128,2048]{2,1,0:T(8,128)} %refs_3_.23, ...), custom_call_target="tpu_custom_call" | custom-call | flops 1610612736 | bytes 16777216 | tf_op jit(solution)/shard_map/step_1_1/pallas_call | solution.py:151
  89.5 2.0 collective-permute-start.14
  92.3 0.8 copy-done
  93.1 10.2 %step_1_0.1 = (f32[64,2176]{1,0:T(8,128)}, f32[64,1536]{1,0:T(8,128)}) custom-call(s32[2]{0:T(128)} %add_convert_fusion.flags, s32[128,6]{1,0:T(8,128)} %bitcast.41, f32[64,2176]{1,0:T(8,128)} %copy-done, f32[64,1536]{1,0:T(8,128)} %copy-done.12, f32[5,128,2048]{2,1,0:T(8,128)} %refs_3_.23, f32[5,128,2048]{2,1,0:T(8,128)} %refs_3_.23, ...), custom_call_target="tpu_custom_call" | custom-call | flops 1610612736 | bytes 16777216 | tf_op jit(solution)/shard_map/step_1_0/pallas_call | solution.py:151
  103.3 3.5 %collective-permute-start.3 = (f32[64,2176]{1,0:T(8,128)}, f32[64,2176]{1,0:T(8,128)S(1)}, u32[]{:S(2)}, u32[]{:S(2)}) collective-permute-start(f32[64,2176]{1,0:T(8,128)} %get-tuple-element.32), channel_id=1, source_target_pairs={{0,4},{1,5},{2,6},{3,7},{4,8},{5,9},{6,10},{7,11},{8,12},{9,13},{1... | collective-permute-start | bytes 1671176 | tf_op jit(solution)/shard_map/ppermute | solution.py:253
  106.9 1.3 collective-permute-start.15
  108.2 1.3 collective-permute-start.4
  109.5 14.9 %collective-permute-done.15.refs_2_ = f32[64,1536]{1,0:T(8,128)S(1)} collective-permute-done((f32[64,1536]{1,0:T(8,128)S(1)}, f32[64,1536]{1,0:T(8,128)S(1)}, u32[]{:S(2)}, u32[]{:S(2)}) %collective-permute-start.15) | collective-permute-done | bytes 393248 | tf_op jit(solution)/shard_map/ppermute | solution.py:229
  125.2 0.8 copy-done.1
  126.0 10.2 %step_2_1.1 = (f32[64,2176]{1,0:T(8,128)}, f32[64,1536]{1,0:T(8,128)}) custom-call(s32[2]{0:T(128)} %add_convert_fusion.flags, s32[128,6]{1,0:T(8,128)} %bitcast.42, f32[64,2176]{1,0:T(8,128)} %copy-done.1, f32[64,1536]{1,0:T(8,128)} %copy-done.18, f32[5,128,2048]{2,1,0:T(8,128)} %refs_3_.23, f32[5,128,2048]{2,1,0:T(8,128)} %refs_3_.23, ...), custom_call_target="tpu_custom_call" | custom-call | flops 1610612736 | bytes 16777216 | tf_op jit(solution)/shard_map/step_2_1/pallas_call | solution.py:151
  136.2 2.0 collective-permute-start.16
  139.8 10.2 %step_2_0.1 = (f32[64,2176]{1,0:T(8,128)}, f32[64,1536]{1,0:T(8,128)}) custom-call(s32[2]{0:T(128)} %add_convert_fusion.flags, s32[128,6]{1,0:T(8,128)} %bitcast.43, f32[64,2176]{1,0:T(8,128)} %copy-done.2, f32[64,1536]{1,0:T(8,128)} %copy-done.13, f32[5,128,2048]{2,1,0:T(8,128)} %refs_3_.23, f32[5,128,2048]{2,1,0:T(8,128)} %refs_3_.23, ...), custom_call_target="tpu_custom_call" | custom-call | flops 1610612736 | bytes 16777216 | tf_op jit(solution)/shard_map/step_2_0/pallas_call | solution.py:151
  150.0 1.9 collective-permute-start.5
  151.9 1.3 collective-permute-start.17
  153.2 1.3 collective-permute-start.6
  154.5 17.2 %collective-permute-done.17.refs_2_ = f32[64,1536]{1,0:T(8,128)S(1)} collective-permute-done((f32[64,1536]{1,0:T(8,128)S(1)}, f32[64,1536]{1,0:T(8,128)S(1)}, u32[]{:S(2)}, u32[]{:S(2)}) %collective-permute-start.17) | collective-permute-done | bytes 393248 | tf_op jit(solution)/shard_map/ppermute | solution.py:229
  173.3 10.2 %step_3_1.1 = (f32[64,2176]{1,0:T(8,128)}, f32[64,1536]{1,0:T(8,128)}) custom-call(s32[2]{0:T(128)} %add_convert_fusion.flags, s32[128,6]{1,0:T(8,128)} %bitcast.44, f32[64,2176]{1,0:T(8,128)} %copy-done.3, f32[64,1536]{1,0:T(8,128)} %copy-done.19, f32[5,128,2048]{2,1,0:T(8,128)} %refs_3_.23, f32[5,128,2048]{2,1,0:T(8,128)} %refs_3_.23, ...), custom_call_target="tpu_custom_call" | custom-call | flops 1610612736 | bytes 16777216 | tf_op jit(solution)/shard_map/step_3_1/pallas_call | solution.py:151
  183.4 2.0 collective-permute-start.18
  187.1 10.2 %step_3_0.1 = (f32[64,2176]{1,0:T(8,128)}, f32[64,1536]{1,0:T(8,128)}) custom-call(s32[2]{0:T(128)} %add_convert_fusion.flags, s32[128,6]{1,0:T(8,128)} %bitcast.45, f32[64,2176]{1,0:T(8,128)} %copy-done.4, f32[64,1536]{1,0:T(8,128)} %copy-done.14, f32[5,128,2048]{2,1,0:T(8,128)} %refs_3_.23, f32[5,128,2048]{2,1,0:T(8,128)} %refs_3_.23, ...), custom_call_target="tpu_custom_call" | custom-call | flops 1610612736 | bytes 16777216 | tf_op jit(solution)/shard_map/step_3_0/pallas_call | solution.py:151
  197.3 1.9 collective-permute-start.7
  199.2 1.3 collective-permute-start.19
  200.5 1.3 collective-permute-start.8
  201.8 17.5 %collective-permute-done.19.refs_2_ = f32[64,1536]{1,0:T(8,128)S(1)} collective-permute-done((f32[64,1536]{1,0:T(8,128)S(1)}, f32[64,1536]{1,0:T(8,128)S(1)}, u32[]{:S(2)}, u32[]{:S(2)}) %collective-permute-start.19) | collective-permute-done | bytes 393248 | tf_op jit(solution)/shard_map/ppermute | solution.py:229
  220.8 10.2 %step_4_1.1 = (f32[64,2176]{1,0:T(8,128)}, f32[64,1536]{1,0:T(8,128)}) custom-call(s32[2]{0:T(128)} %add_convert_fusion.flags, s32[128,6]{1,0:T(8,128)} %bitcast.46, f32[64,2176]{1,0:T(8,128)} %copy-done.5, f32[64,1536]{1,0:T(8,128)} %copy-done.20, f32[5,128,2048]{2,1,0:T(8,128)} %refs_3_.23, f32[5,128,2048]{2,1,0:T(8,128)} %refs_3_.23, ...), custom_call_target="tpu_custom_call" | custom-call | flops 1610612736 | bytes 16777216 | tf_op jit(solution)/shard_map/step_4_1/pallas_call | solution.py:151
  231.0 2.0 collective-permute-start.20
  234.6 10.2 %step_4_0.1 = (f32[64,2176]{1,0:T(8,128)}, f32[64,1536]{1,0:T(8,128)}) custom-call(s32[2]{0:T(128)} %add_convert_fusion.flags, s32[128,6]{1,0:T(8,128)} %bitcast.47, f32[64,2176]{1,0:T(8,128)} %copy-done.6, f32[64,1536]{1,0:T(8,128)} %copy-done.15, f32[5,128,2048]{2,1,0:T(8,128)} %refs_3_.23, f32[5,128,2048]{2,1,0:T(8,128)} %refs_3_.23, ...), custom_call_target="tpu_custom_call" | custom-call | flops 1610612736 | bytes 16777216 | tf_op jit(solution)/shard_map/step_4_0/pallas_call | solution.py:151
  244.8 1.9 collective-permute-start.9
  246.8 1.3 collective-permute-start.21
  248.1 1.3 collective-permute-start.10
  249.4 15.9 %collective-permute-done.21.refs_2_ = f32[64,1536]{1,0:T(8,128)S(1)} collective-permute-done((f32[64,1536]{1,0:T(8,128)S(1)}, f32[64,1536]{1,0:T(8,128)S(1)}, u32[]{:S(2)}, u32[]{:S(2)}) %collective-permute-start.21) | collective-permute-done | bytes 393248 | tf_op jit(solution)/shard_map/ppermute | solution.py:229
  266.8 9.9 %step_5_1.1 = (f32[64,2048]{1,0:T(8,128)}, f32[64,128]{1,0:T(8,128)}) custom-call(s32[2]{0:T(128)} %add_convert_fusion.flags, s32[128,6]{1,0:T(8,128)} %bitcast.48, f32[64,2176]{1,0:T(8,128)} %copy-done.7, f32[64,1536]{1,0:T(8,128)} %copy-done.21, f32[5,128,2048]{2,1,0:T(8,128)} %refs_3_.23, bf16[4,4,512,512]{3,2,1,0:T(8,128)(2,1)} %bitcast.23, ...), custom_call_target="tpu_custom_call" | custom-call | flops 1610612736 | bytes 16777216 | tf_op jit(solution)/shard_map/step_5_1/pallas_call | solution.py:151
  278.2 9.9 %step_5_0.1 = (f32[64,2048]{1,0:T(8,128)}, f32[64,128]{1,0:T(8,128)}) custom-call(s32[2]{0:T(128)} %add_convert_fusion.flags, s32[128,6]{1,0:T(8,128)} %bitcast.49, f32[64,2176]{1,0:T(8,128)} %copy-done.8, f32[64,1536]{1,0:T(8,128)} %copy-done.16, f32[5,128,2048]{2,1,0:T(8,128)} %refs_3_.23, bf16[4,4,512,512]{3,2,1,0:T(8,128)(2,1)} %bitcast.24, ...), custom_call_target="tpu_custom_call" | custom-call | flops 1610612736 | bytes 16777216 | tf_op jit(solution)/shard_map/step_5_0/pallas_call | solution.py:151
  288.2 1.3 collective-permute-start.22
  290.2 37.4 %all-reduce.3.cloned.1.call-done = (f32[64,128]{1,0:T(8,128)}, f32[64,128]{1,0:T(8,128)}) async-done(((f32[64,128]{1,0:T(8,128)}, f32[64,128]{1,0:T(8,128)}), (f32[64,128]{1,0:T(8,128)}, f32[64,128]{1,0:T(8,128)})) %all-reduce.3.cloned.1.call-update) | async-done | bytes 65552 | tf_op jit(solution)/shard_map/psum | solution.py:257
  327.5 2.6 finish.1
  (76 shorter events, 16.1 us)
Async XLA Ops:
  7.2 320.4 %all-reduce.3.cloned.1.call-start = ((), (), s32[]{:S(2)}) async-start(), calls=%async_computation | async-start | bytes 131072 | tf_op jit(solution)/shard_map/psum | solution.py:257
  8.4 21.9 %collective-permute-start.11 = (f32[64,1536]{1,0:T(8,128)S(1)}, f32[64,1536]{1,0:T(8,128)S(1)}, u32[]{:S(2)}, u32[]{:S(2)}) collective-permute-start(f32[64,1536]{1,0:T(8,128)S(1)} %get-tuple-element.56), channel_id=1, source_target_pairs={{1,0},{2,1},{3,2},{5,4},{6,5},{7,6},{9,8},{10,9},{11,10},{13,12},{... | collective-permute-start | bytes 1179656 | tf_op jit(solution)/shard_map/ppermute | solution.py:229
  9.7 36.2 %collective-permute-start = (f32[64,1536]{1,0:T(8,128)S(1)}, f32[64,1536]{1,0:T(8,128)S(1)}, u32[]{:S(2)}, u32[]{:S(2)}) collective-permute-start(f32[64,1536]{1,0:T(8,128)S(1)} %get-tuple-element.57), channel_id=1, source_target_pairs={{1,0},{2,1},{3,2},{5,4},{6,5},{7,6},{9,8},{10,9},{11,10},{13,12},{... | collective-permute-start | bytes 1179656 | tf_op jit(solution)/shard_map/ppermute | solution.py:229
  41.2 17.4 %copy-start.27 = (f32[64,1536]{1,0:T(8,128)S(1)}, f32[64,1536]{1,0:T(8,128)}, u32[]{:S(2)}) copy-start(f32[64,1536]{1,0:T(8,128)} %get-tuple-element.42) | copy-start | bytes 1179652
  41.2 36.6 %collective-permute-start.12 = (f32[64,2176]{1,0:T(8,128)}, f32[64,2176]{1,0:T(8,128)S(1)}, u32[]{:S(2)}, u32[]{:S(2)}) collective-permute-start(f32[64,2176]{1,0:T(8,128)} %get-tuple-element.41), channel_id=1, source_target_pairs={{0,4},{1,5},{2,6},{3,7},{4,8},{5,9},{6,10},{7,11},{8,12},{9,13},{1... | collective-permute-start | bytes 1671176 | tf_op jit(solution)/shard_map/ppermute | solution.py:253
  56.6 34.9 %collective-permute-start.1 = (f32[64,2176]{1,0:T(8,128)}, f32[64,2176]{1,0:T(8,128)S(1)}, u32[]{:S(2)}, u32[]{:S(2)}) collective-permute-start(f32[64,2176]{1,0:T(8,128)} %get-tuple-element.30), channel_id=1, source_target_pairs={{0,4},{1,5},{2,6},{3,7},{4,8},{5,9},{6,10},{7,11},{8,12},{9,13},{1... | collective-permute-start | bytes 1671176 | tf_op jit(solution)/shard_map/ppermute | solution.py:253
  58.6 19.2 %collective-permute-start.13 = (f32[64,1536]{1,0:T(8,128)S(1)}, f32[64,1536]{1,0:T(8,128)S(1)}, u32[]{:S(2)}, u32[]{:S(2)}) collective-permute-start(f32[64,1536]{1,0:T(8,128)S(1)} %copy-done.27), channel_id=1, source_target_pairs={{1,4},{2,5},{3,6},{5,8},{6,9},{7,10},{9,12},{10,13},{11,14},{13,16... | collective-permute-start | bytes 1179656 | tf_op jit(solution)/shard_map/ppermute | solution.py:229
  59.9 31.7 %collective-permute-start.2 = (f32[64,1536]{1,0:T(8,128)}, f32[64,1536]{1,0:T(8,128)S(1)}, u32[]{:S(2)}, u32[]{:S(2)}) collective-permute-start(f32[64,1536]{1,0:T(8,128)} %get-tuple-element.31), channel_id=1, source_target_pairs={{1,4},{2,5},{3,6},{5,8},{6,9},{7,10},{9,12},{10,13},{11,14},{13,16... | collective-permute-start | bytes 1179656 | tf_op jit(solution)/shard_map/ppermute | solution.py:229
  77.7 0.8 copy-start.17
  78.5 0.8 copy-start.9
  89.5 17.4 %copy-start.23 = (f32[64,1536]{1,0:T(8,128)S(1)}, f32[64,1536]{1,0:T(8,128)}, u32[]{:S(2)}) copy-start(f32[64,1536]{1,0:T(8,128)} %get-tuple-element.44) | copy-start | bytes 1179652
  89.5 34.9 %collective-permute-start.14 = (f32[64,2176]{1,0:T(8,128)}, f32[64,2176]{1,0:T(8,128)S(1)}, u32[]{:S(2)}, u32[]{:S(2)}) collective-permute-start(f32[64,2176]{1,0:T(8,128)} %get-tuple-element.43), channel_id=1, source_target_pairs={{0,4},{1,5},{2,6},{3,7},{4,8},{5,9},{6,10},{7,11},{8,12},{9,13},{1... | collective-permute-start | bytes 1671176 | tf_op jit(solution)/shard_map/ppermute | solution.py:253
  91.6 0.8 copy-start.12
  92.3 0.8 copy-start
  103.3 34.9 %collective-permute-start.3 = (f32[64,2176]{1,0:T(8,128)}, f32[64,2176]{1,0:T(8,128)S(1)}, u32[]{:S(2)}, u32[]{:S(2)}) collective-permute-start(f32[64,2176]{1,0:T(8,128)} %get-tuple-element.32), channel_id=1, source_target_pairs={{0,4},{1,5},{2,6},{3,7},{4,8},{5,9},{6,10},{7,11},{8,12},{9,13},{1... | collective-permute-start | bytes 1671176 | tf_op jit(solution)/shard_map/ppermute | solution.py:253
  106.9 17.5 %collective-permute-start.15 = (f32[64,1536]{1,0:T(8,128)S(1)}, f32[64,1536]{1,0:T(8,128)S(1)}, u32[]{:S(2)}, u32[]{:S(2)}) collective-permute-start(f32[64,1536]{1,0:T(8,128)S(1)} %copy-done.23), channel_id=1, source_target_pairs={{1,4},{2,5},{3,6},{5,8},{6,9},{7,10},{9,12},{10,13},{11,14},{13,16... | collective-permute-start | bytes 1179656 | tf_op jit(solution)/shard_map/ppermute | solution.py:229
  108.2 30.0 %collective-permute-start.4 = (f32[64,1536]{1,0:T(8,128)}, f32[64,1536]{1,0:T(8,128)S(1)}, u32[]{:S(2)}, u32[]{:S(2)}) collective-permute-start(f32[64,1536]{1,0:T(8,128)} %get-tuple-element.33), channel_id=1, source_target_pairs={{1,4},{2,5},{3,6},{5,8},{6,9},{7,10},{9,12},{10,13},{11,14},{13,16... | collective-permute-start | bytes 1179656 | tf_op jit(solution)/shard_map/ppermute | solution.py:229
  124.4 0.8 copy-start.18
  125.2 0.8 copy-start.1
  136.2 15.7 %copy-start.24 = (f32[64,1536]{1,0:T(8,128)S(1)}, f32[64,1536]{1,0:T(8,128)}, u32[]{:S(2)}) copy-start(f32[64,1536]{1,0:T(8,128)} %get-tuple-element.46) | copy-start | bytes 1179652
  136.2 35.5 %collective-permute-start.16 = (f32[64,2176]{1,0:T(8,128)}, f32[64,2176]{1,0:T(8,128)S(1)}, u32[]{:S(2)}, u32[]{:S(2)}) collective-permute-start(f32[64,2176]{1,0:T(8,128)} %get-tuple-element.45), channel_id=1, source_target_pairs={{0,4},{1,5},{2,6},{3,7},{4,8},{5,9},{6,10},{7,11},{8,12},{9,13},{1... | collective-permute-start | bytes 1671176 | tf_op jit(solution)/shard_map/ppermute | solution.py:253
  138.2 0.8 copy-start.13
  139.0 0.8 copy-start.2
  150.0 35.5 %collective-permute-start.5 = (f32[64,2176]{1,0:T(8,128)}, f32[64,2176]{1,0:T(8,128)S(1)}, u32[]{:S(2)}, u32[]{:S(2)}) collective-permute-start(f32[64,2176]{1,0:T(8,128)} %get-tuple-element.34), channel_id=1, source_target_pairs={{0,4},{1,5},{2,6},{3,7},{4,8},{5,9},{6,10},{7,11},{8,12},{9,13},{1... | collective-permute-start | bytes 1671176 | tf_op jit(solution)/shard_map/ppermute | solution.py:253
  151.9 19.8 %collective-permute-start.17 = (f32[64,1536]{1,0:T(8,128)S(1)}, f32[64,1536]{1,0:T(8,128)S(1)}, u32[]{:S(2)}, u32[]{:S(2)}) collective-permute-start(f32[64,1536]{1,0:T(8,128)S(1)} %copy-done.24), channel_id=1, source_target_pairs={{1,4},{2,5},{3,6},{5,8},{6,9},{7,10},{9,12},{10,13},{11,14},{13,16... | collective-permute-start | bytes 1179656 | tf_op jit(solution)/shard_map/ppermute | solution.py:229
  153.2 32.3 %collective-permute-start.6 = (f32[64,1536]{1,0:T(8,128)}, f32[64,1536]{1,0:T(8,128)S(1)}, u32[]{:S(2)}, u32[]{:S(2)}) collective-permute-start(f32[64,1536]{1,0:T(8,128)} %get-tuple-element.35), channel_id=1, source_target_pairs={{1,4},{2,5},{3,6},{5,8},{6,9},{7,10},{9,12},{10,13},{11,14},{13,16... | collective-permute-start | bytes 1179656 | tf_op jit(solution)/shard_map/ppermute | solution.py:229
  171.7 0.8 copy-start.19
  172.5 0.8 copy-start.3
  183.4 15.7 %copy-start.25 = (f32[64,1536]{1,0:T(8,128)S(1)}, f32[64,1536]{1,0:T(8,128)}, u32[]{:S(2)}) copy-start(f32[64,1536]{1,0:T(8,128)} %get-tuple-element.48) | copy-start | bytes 1179652
  183.4 35.8 %collective-permute-start.18 = (f32[64,2176]{1,0:T(8,128)}, f32[64,2176]{1,0:T(8,128)S(1)}, u32[]{:S(2)}, u32[]{:S(2)}) collective-permute-start(f32[64,2176]{1,0:T(8,128)} %get-tuple-element.47), channel_id=1, source_target_pairs={{0,4},{1,5},{2,6},{3,7},{4,8},{5,9},{6,10},{7,11},{8,12},{9,13},{1... | collective-permute-start | bytes 1671176 | tf_op jit(solution)/shard_map/ppermute | solution.py:253
  185.5 0.8 copy-start.14
  186.3 0.8 copy-start.4
  197.3 35.8 %collective-permute-start.7 = (f32[64,2176]{1,0:T(8,128)}, f32[64,2176]{1,0:T(8,128)S(1)}, u32[]{:S(2)}, u32[]{:S(2)}) collective-permute-start(f32[64,2176]{1,0:T(8,128)} %get-tuple-element.36), channel_id=1, source_target_pairs={{0,4},{1,5},{2,6},{3,7},{4,8},{5,9},{6,10},{7,11},{8,12},{9,13},{1... | collective-permute-start | bytes 1671176 | tf_op jit(solution)/shard_map/ppermute | solution.py:253
  199.2 20.1 %collective-permute-start.19 = (f32[64,1536]{1,0:T(8,128)S(1)}, f32[64,1536]{1,0:T(8,128)S(1)}, u32[]{:S(2)}, u32[]{:S(2)}) collective-permute-start(f32[64,1536]{1,0:T(8,128)S(1)} %copy-done.25), channel_id=1, source_target_pairs={{1,4},{2,5},{3,6},{5,8},{6,9},{7,10},{9,12},{10,13},{11,14},{13,16... | collective-permute-start | bytes 1179656 | tf_op jit(solution)/shard_map/ppermute | solution.py:229
  200.5 32.6 %collective-permute-start.8 = (f32[64,1536]{1,0:T(8,128)}, f32[64,1536]{1,0:T(8,128)S(1)}, u32[]{:S(2)}, u32[]{:S(2)}) collective-permute-start(f32[64,1536]{1,0:T(8,128)} %get-tuple-element.37), channel_id=1, source_target_pairs={{1,4},{2,5},{3,6},{5,8},{6,9},{7,10},{9,12},{10,13},{11,14},{13,16... | collective-permute-start | bytes 1179656 | tf_op jit(solution)/shard_map/ppermute | solution.py:229
  220.0 0.8 copy-start.5
  231.0 15.7 %copy-start.26 = (f32[64,1536]{1,0:T(8,128)S(1)}, f32[64,1536]{1,0:T(8,128)}, u32[]{:S(2)}) copy-start(f32[64,1536]{1,0:T(8,128)} %get-tuple-element.50) | copy-start | bytes 1179652
  231.0 34.2 %collective-permute-start.20 = (f32[64,2176]{1,0:T(8,128)}, f32[64,2176]{1,0:T(8,128)S(1)}, u32[]{:S(2)}, u32[]{:S(2)}) collective-permute-start(f32[64,2176]{1,0:T(8,128)} %get-tuple-element.49), channel_id=1, source_target_pairs={{0,4},{1,5},{2,6},{3,7},{4,8},{5,9},{6,10},{7,11},{8,12},{9,13},{1... | collective-permute-start | bytes 1671176 | tf_op jit(solution)/shard_map/ppermute | solution.py:253
  233.1 0.8 copy-start.15
  233.8 0.8 copy-start.6
  244.8 31.9 %collective-permute-start.9 = (f32[64,2176]{1,0:T(8,128)}, f32[64,2176]{1,0:T(8,128)S(1)}, u32[]{:S(2)}, u32[]{:S(2)}) collective-permute-start(f32[64,2176]{1,0:T(8,128)} %get-tuple-element.38), channel_id=1, source_target_pairs={{0,4},{1,5},{2,6},{3,7},{4,8},{5,9},{6,10},{7,11},{8,12},{9,13},{1... | collective-permute-start | bytes 1671176 | tf_op jit(solution)/shard_map/ppermute | solution.py:253
  246.8 18.5 %collective-permute-start.21 = (f32[64,1536]{1,0:T(8,128)S(1)}, f32[64,1536]{1,0:T(8,128)S(1)}, u32[]{:S(2)}, u32[]{:S(2)}) collective-permute-start(f32[64,1536]{1,0:T(8,128)S(1)} %copy-done.26), channel_id=1, source_target_pairs={{1,4},{2,5},{3,6},{5,8},{6,9},{7,10},{9,12},{10,13},{11,14},{13,16... | collective-permute-start | bytes 1179656 | tf_op jit(solution)/shard_map/ppermute | solution.py:229
  248.1 28.6 %collective-permute-start.10 = (f32[64,1536]{1,0:T(8,128)}, f32[64,1536]{1,0:T(8,128)S(1)}, u32[]{:S(2)}, u32[]{:S(2)}) collective-permute-start(f32[64,1536]{1,0:T(8,128)} %get-tuple-element.39), channel_id=1, source_target_pairs={{1,4},{2,5},{3,6},{5,8},{6,9},{7,10},{9,12},{10,13},{11,14},{13,16... | collective-permute-start | bytes 1179656 | tf_op jit(solution)/shard_map/ppermute | solution.py:229
  266.0 0.8 copy-start.7
  276.7 11.5 %copy-start.28 = (f32[1,128]{1,0:T(1,128)S(1)}, f32[1,128]{1,0:T(1,128)}, u32[]{:S(2)}) copy-start(f32[1,128]{1,0:T(1,128)} %param.8) | copy-start | bytes 1540
  277.4 0.8 copy-start.8
  288.2 2.0 collective-permute-start.22
  290.2 37.4 %copy-start.22 = (f32[1,128]{1,0:T(1,128)}, f32[1,128]{1,0:T(1,128)S(1)}, u32[]{:S(2)}) copy-start(f32[1,128]{1,0:T(1,128)S(1)} %collective-permute-done.22.refs_4_) | copy-start | bytes 1540
  (5 other events, 3.8 us)
Sparse Core Ops, SparseCore 0:
  288.3 39.1 all-reduce.2

commit v2 on v1

v2 whole, which is shorter than its diff:
```python
import functools
import jax
import jax.numpy as jnp
from jax import lax
from jax.experimental import pallas as pl
from jax.experimental.pallas import tpu as pltpu
from jax.sharding import PartitionSpec as P


EPSILON = 1e-06
SCALE = 256.0
LANES = 128
CHUNKS = 2
BF = jnp.bfloat16
F32 = jnp.float32
AXES = ("site", "sector")
VMEM_SPEC = pl.BlockSpec(memory_space=pltpu.VMEM)
VMEM_LIMIT = 8 << 20
UNROLL = 2


def in_vmem(value):
    return pltpu.with_memory_space_constraint(value, pltpu.VMEM)


def split_kernel(w_ref, hi_ref, lo_ref, buffer, sems):
    count, depth = w_ref.shape[0], buffer.shape[0]
    copies = [
        pltpu.make_async_copy(w_ref.at[i], buffer.at[i % depth], sems.at[i % depth])
        for i in range(count)
    ]
    for copy in copies[:depth]:
        copy.start()
    for i in range(count):
        copies[i].wait()
        w = buffer[i % depth]
        hi = w.astype(BF)
        hi_ref[i] = hi
        lo_ref[i] = (w - hi.astype(F32)).astype(BF)
        if i + depth < count:
            copies[i + depth].start()


def split_weights(w):
    count, width, _ = w.shape
    depth = min(4, count)
    return pl.pallas_call(
        split_kernel,
        in_specs=[pl.BlockSpec(memory_space=pl.ANY)],
        out_specs=[VMEM_SPEC] * 2,
        out_shape=[pltpu.VMEM(w.shape, BF)] * 2,
        scratch_shapes=[
            pltpu.VMEM((depth, width, width), F32),
            pltpu.SemaphoreType.DMA((depth,)),
        ],
        compiler_params=pltpu.CompilerParams(vmem_limit_bytes=(4 * depth + 2) * width * width),
        name="split_weights",
        cost_estimate=pl.CostEstimate(flops=w.size, bytes_accessed=8 * w.size, transcendentals=0),
    )(w)


def step_kernel(dims, tick, ticks, chunk, *refs):
    n_out, local, width, rows, halo = dims
    first, last = tick == 0, tick == ticks - 1
    span = local * width
    refs = list(refs)
    flag_ref = refs.pop(0)
    choice_ref = refs.pop(0)
    main_ref = refs.pop(0)
    halo_refs = [refs.pop(0) for _ in halo]
    entering_ref = refs.pop(0)
    hi_ref, lo_ref = refs.pop(0), refs.pop(0)
    out_ref = refs.pop(0)
    part_ref = refs.pop(0) if last else None
    edge_ref = None if last else refs.pop(0)
    stack = refs.pop(0)
    own = slice(chunk * rows, (chunk + 1) * rows)
    at_start = flag_ref[0] == 1
    at_end = flag_ref[1] == 1

    def put(index, value):
        hi = value.astype(BF)
        stack[index, :rows] = hi
        stack[index, rows:] = (value - hi.astype(F32)).astype(BF)

    for q in range(local):
        cols = slice(q * width, (q + 1) * width)
        if first:
            value = main_ref[0, own, cols] * SCALE
        else:
            value = jnp.where(at_start, entering_ref[tick - 1, own, cols] * SCALE, main_ref[:, cols])
        put(q, value)
    index = local
    for ref, blocks in zip(halo_refs, halo):
        for q in range(blocks):
            value = ref[:, q * width : (q + 1) * width]
            put(index, value * SCALE if first else value)
            index += 1

    choice = choice_ref[own, tick : tick + 1]

    def column(s, carry):
        picked, total = carry
        selected = None
        for n in range(n_out):
            both = stack[s + n]
            wide = jnp.dot(both, hi_ref[n, s], preferred_element_type=F32)
            value = wide[:rows] + wide[rows:]
            value = value + jnp.dot(both[:rows], lo_ref[n, s], preferred_element_type=F32)
            power = jnp.sum(value * value, axis=1, keepdims=True)
            mine = choice == n
            total = total + power
            picked = picked + jnp.where(mine, power, 0.0)
            selected = jnp.where(mine, value, 0.0 if n == 0 else selected)
        out_ref[:, pl.ds(pl.multiple_of(s * width, width), width)] = selected
        return picked, total

    zero = jnp.zeros((rows, 1), F32)
    picked, total = lax.fori_loop(0, local, column, (zero, zero), unroll=min(UNROLL, local))
    if not last:
        for q in range(halo[0]):
            cols = slice(q * width, (q + 1) * width)
            own_rows = entering_ref[tick, own, cols] * SCALE
            edge_ref[:, cols] = jnp.where(at_end, own_rows, out_ref[:, cols])

    lane = lax.broadcasted_iota(jnp.int32, (rows, LANES), 1)
    sums = jnp.where(lane == 2 * tick, picked, jnp.where(lane == 2 * tick + 1, total, 0.0))
    if not first:
        sums = sums + jnp.where(at_start, 0.0, main_ref[:, span : span + LANES])
    if last:
        part_ref[...] = sums
    else:
        out_ref[:, span : span + LANES] = sums


def step(dims, tick, ticks, chunk, flags, choice, main, halos, entering, weights):
    n_out, local, width, rows, halo = dims
    last = tick == ticks - 1
    span = local * width
    operands = [choice, main, *halos, entering, *weights]
    if last:
        shapes = [(rows, span), (rows, LANES)]
    else:
        shapes = [(rows, span + LANES), (rows, halo[0] * width)]
    blocks = local + sum(halo)
    return pl.pallas_call(
        functools.partial(step_kernel, dims, tick, ticks, chunk),
        in_specs=[pl.BlockSpec(memory_space=pltpu.SMEM)] + [VMEM_SPEC] * len(operands),
        out_specs=[VMEM_SPEC] * 2,
        out_shape=[pltpu.VMEM(shape, F32) for shape in shapes],
        scratch_shapes=[pltpu.VMEM((blocks, 2 * rows, width), BF)],
        compiler_params=pltpu.CompilerParams(vmem_limit_bytes=VMEM_LIMIT),
        cost_estimate=pl.CostEstimate(
            flops=6 * rows * n_out * local * width * width,
            bytes_accessed=4 * rows * span,
            transcendentals=0,
        ),
    )(flags, *[in_vmem(value) for value in operands])


def final_kernel(ticks, bond, chunks, copies, *refs):
    refs = list(refs)
    state_refs = [refs.pop(0) for _ in range(chunks)]
    part_refs = [[refs.pop(0) for _ in range(copies)] for _ in range(chunks)]
    prior_ref, env_ref, logp_ref = refs
    rows = state_refs[0].shape[0]
    scale = 1.0 / (bond * SCALE * SCALE)
    for c in range(chunks):
        sums = [ref[...] for ref in part_refs[c]]
        while len(sums) > 1:
            sums = [sums[i] + sums[i + 1] for i in range(0, len(sums), 2)]
        sums = sums[0].T * scale
        own = slice(c * rows, (c + 1) * rows)
        log_weight = prior_ref[:, own]
        factor = jnp.ones((1, rows), F32)
        for t in range(ticks):
            picked = sums[2 * t : 2 * t + 1] * factor * factor + EPSILON
            total = sums[2 * t + 1 : 2 * t + 2] * factor * factor + EPSILON
            log_weight = log_weight + jnp.log(picked) - jnp.log(total)
            factor = factor * lax.rsqrt(picked)
        logp_ref[:, own] = log_weight
        column = jnp.broadcast_to(factor, (LANES, rows)).T[:, :1]
        env_ref[0, own] = state_refs[c][...] * (column * (1.0 / SCALE))


def finish(states, parts, prior, ticks, bond):
    rows = sum(value.shape[0] for value in states)
    span = states[0].shape[1]
    operands = [*states, *[value for group in parts for value in group], prior]
    return pl.pallas_call(
        functools.partial(final_kernel, ticks, float(bond), len(states), len(parts[0])),
        in_specs=[VMEM_SPEC] * len(operands),
        out_shape=[
            jax.ShapeDtypeStruct((1, rows, span), F32),
            jax.ShapeDtypeStruct((1, rows), F32),
        ],
        compiler_params=pltpu.CompilerParams(vmem_limit_bytes=VMEM_LIMIT),
        name="finish",
    )(*operands)


def sector_terms(value, sectors):
    if sectors & (sectors - 1) or sectors == 1:
        return [lax.psum(value, "sector")]
    if sectors <= 4:
        return [value] + [
            lax.ppermute(value, "sector", [(d, d ^ mask) for d in range(sectors)])
            for mask in range(1, sectors)
        ]
    mask = 1
    while 2 * mask < sectors:
        value = value + lax.ppermute(value, "sector", [(d, d ^ mask) for d in range(sectors)])
        mask *= 2
    return [value, lax.ppermute(value, "sector", [(d, d ^ mask) for d in range(sectors)])]


def per_device(sites, sectors, site_tensor, outcomes, in_flight, prior_logp, entering):
    weights = site_tensor[0]
    n_out, local, width = weights.shape[:3]
    span = in_flight.shape[2]
    total_rows = in_flight.shape[1]
    ticks = outcomes.shape[0]
    rows = total_rows // CHUNKS
    need = n_out - 1
    halo = []
    while need > 0:
        halo.append(min(local, need))
        need -= halo[-1]
    dims = (n_out, local, width, rows, tuple(halo))
    place = lambda k, d: k * sectors + d
    main_pairs = [(place(k, d), place(k + 1, d)) for k in range(sites - 1) for d in range(sectors)]

    def halo_pairs(hop, shift):
        return [
            (place(k, d + hop), place((k + shift) % sites, d))
            for k in range(sites)
            for d in range(sectors - hop)
        ]

    def halo_moved(edge, shift):
        moved = []
        for hop, blocks in enumerate(halo):
            moved.append(lax.ppermute(edge[:, : blocks * width], AXES, halo_pairs(hop + 1, shift)))
        return moved

    site = lax.axis_index("site")
    flags = jnp.stack([site == 0, site == sites - 1]).astype(jnp.int32)
    choice = outcomes[:, 0].T
    prior = lax.ppermute(
        prior_logp, "site", [(k, k + ticks - 1) for k in range(sites - ticks + 1)]
    )
    halos = [
        halo_moved(in_flight[0, c * rows : (c + 1) * rows, : halo[0] * width], 0)
        for c in range(CHUNKS)
    ]
    split = split_weights(weights.reshape(n_out * local, width, width))
    split = [value.reshape(weights.shape) for value in split]
    mains = [in_flight] * CHUNKS
    parts = [None] * CHUNKS
    for tick in range(ticks):
        for c in range(CHUNKS):
            main, other = step(
                dims, tick, ticks, c, flags, choice, mains[c], halos[c], entering, split
            )
            if tick < ticks - 1:
                halos[c] = halo_moved(other, 1)
                mains[c] = lax.ppermute(main, AXES, main_pairs)
            else:
                mains[c] = main
                parts[c] = sector_terms(other, sectors)
    return tuple(finish(mains, parts, prior, ticks, span * sectors))


def solution(mesh):
    sizes = (mesh.shape["site"], mesh.shape["sector"])

    def whole(site_tensor, outcomes, *others):
        call = jax.shard_map(
            functools.partial(per_device, *sizes),
            mesh=mesh,
            in_specs=(
                P("site", None, "sector", None, None),
                P(None, "site", None),
                P("site", None, "sector"),
                P("site", None),
                P(None, None, "sector"),
            ),
            out_specs=(P("site", None, "sector"), P("site", None)),
            check_vma=False,
        )
        return call(site_tensor, outcomes, *others)

    return whole
```

time: 339 us -> 195 us (0.58)
  Pallas kernels: 141 us -> 52.7 us
  waiting for transfers between devices: 120 us -> 81.8 us
  between operations: 14.4 us -> 0.96 us
  local copies, waits for them, and re-layouts: 19.7 us -> 7.83 us
  starting transfers between devices: 40.9 us -> 49.3 us
    pallas_call x13, Pallas kernels: 139 us -> 51.3 us  [the longest x12 47.9 us: step(): pl.pallas_call(functools.partial(step_kernel, dims, tick, ticks, chunk),...]
    psum x1 -> x0, waiting for transfers between devices: 37.4 us -> none  [per_device(): parts[c] = lax.psum(other, 'sector')]
    unnamed x59 -> x11, local copies, waits for them, and re-layouts: 18.5 us -> 6.58 us
    ppermute x0 -> x6, starting transfers between devices: none -> 6.15 us  [sector_terms(): lax.ppermute(value, 'sector', [(d, d ^ mask) for d in range(sectors)])]
  transfers between devices with their start and end apart: 24 -> 29, of which waited for: 7 -> 9; matrix products, arithmetic and copies ran while one was open for 1% -> 0% of each run, Pallas kernels for 38% -> 27%
where the time goes in v2:
time: 195 us; the launch traced here: 193 us
  waiting for transfers between devices  81.8 us (42%)
  Pallas kernels  52.7 us (27%)
  starting transfers between devices  49.3 us (25%)
  local copies, waits for them, and re-layouts  7.83 us (4%)
    ppermute x12, waiting for transfers between devices, halo_moved(): lax.ppermute(edge[:, :blocks * width], AXES, halo_pairs(hop + 1, shift))  79.4 us
    pallas_call x12, Pallas kernels, step(): pl.pallas_call(functools.partial(step_kernel, dims, tick, ticks, chunk),...  47.9 us
    ppermute x10, starting transfers between devices, per_device(): mains[c] = lax.ppermute(main, AXES, main_pairs)  26.4 us
    ppermute x12, starting transfers between devices, halo_moved(): lax.ppermute(edge[:, :blocks * width], AXES, halo_pairs(hop + 1, shift))  15.5 us
    unnamed x11, local copies, waits for them, and re-layouts  6.58 us
    ppermute x6, starting transfers between devices, sector_terms(): lax.ppermute(value, 'sector', [(d, d ^ mask) for d in range(sectors)])  6.15 us
  transfers between devices with their start and end apart: 29, of which 9 were waited for; matrix products, arithmetic and copies ran while one was open for 0% of the time, Pallas kernels for 27%

profile of v2, /device:TPU:1, one launch (start us, length us, event | category | flops | bytes accessed | tf_op | source)
XLA Modules:
  0.0 192.7 jit_solution(14012268814576970673)
XLA Ops:
  1.9 1.3 collective-permute-start
  3.2 1.3 collective-permute-start.11
  5.3 5.8 %copy-done = f32[1,4,4,512,512]{4,3,2,1,0:T(8,128)S(1)} copy-done((f32[1,4,4,512,512]{4,3,2,1,0:T(8,128)S(1)}, f32[1,4,4,512,512]{4,3,2,1,0:T(8,128)}, u32[]{:S(2)}) %copy-start) | copy-done | bytes 16777240
  11.1 3.4 %split_weights.1 = (bf16[16,512,512]{2,1,0:T(8,128)(2,1)S(1)}, bf16[16,512,512]{2,1,0:T(8,128)(2,1)S(1)}) custom-call(f32[16,512,512]{2,1,0:T(8,128)S(1)} %bitcast.38), custom_call_target="tpu_custom_call" | custom-call | flops 4194304 | bytes 33554432 | tf_op jit(solution)/shard_map/split_weights/pallas_call | solution.py:47
  14.7 4.0 %shard_map.68 = (f32[64,2176]{1,0:T(8,128)S(1)}, f32[64,1536]{1,0:T(8,128)S(1)}) custom-call(s32[2]{0:T(128)S(1)} %add_convert_fusion.refs_0_, s32[128,6]{1,0:T(8,128)S(1)} %bitcast.39, f32[1,128,2048]{2,1,0:T(8,128)S(1)} %copy-done.1, f32[64,1536]{1,0:T(8,128)S(1)} %collective-permute-done.refs_3_, f32[5,128,2048]{2,1,0:T(8,128)S(1)} %bitcast.37, ...), custom_call_target="tpu_custom_call" | custom-call | flops 1610612736 | bytes 524288 | tf_op jit(solution)/shard_map/pallas_call | solution.py:146
  18.7 5.7 %collective-permute-start.1 = (f32[64,2176]{1,0:T(8,128)S(1)}, f32[64,2176]{1,0:T(8,128)S(1)}, u32[]{:S(2)}, u32[]{:S(2)}) collective-permute-start(f32[64,2176]{1,0:T(8,128)S(1)} %get-tuple-element.30), channel_id=1, source_target_pairs={{0,4},{1,5},{2,6},{3,7},{4,8},{5,9},{6,10},{7,11},{8,12},{9,13},{1... | collective-permute-start | bytes 1671176 | tf_op jit(solution)/shard_map/ppermute | solution.py:267
  24.4 4.0 %shard_map.74 = (f32[64,2176]{1,0:T(8,128)S(1)}, f32[64,1536]{1,0:T(8,128)S(1)}) custom-call(s32[2]{0:T(128)S(1)} %add_convert_fusion.refs_0_, s32[128,6]{1,0:T(8,128)S(1)} %bitcast.40, f32[1,128,2048]{2,1,0:T(8,128)S(1)} %copy-done.1, f32[64,1536]{1,0:T(8,128)S(1)} %collective-permute-done.11.refs_3_, f32[5,128,2048]{2,1,0:T(8,128)S(1)} %bitcast.37, ...), custom_call_target="tpu_custom_call" | custom-call | flops 1610612736 | bytes 524288 | tf_op jit(solution)/shard_map/pallas_call | solution.py:146
  28.4 3.2 %collective-permute-start.12 = (f32[64,2176]{1,0:T(8,128)S(1)}, f32[64,2176]{1,0:T(8,128)S(1)}, u32[]{:S(2)}, u32[]{:S(2)}) collective-permute-start(f32[64,2176]{1,0:T(8,128)S(1)} %get-tuple-element.41), channel_id=1, source_target_pairs={{0,4},{1,5},{2,6},{3,7},{4,8},{5,9},{6,10},{7,11},{8,12},{9,13},{1... | collective-permute-start | bytes 1671176 | tf_op jit(solution)/shard_map/ppermute | solution.py:267
  31.7 1.3 collective-permute-start.2
  33.0 1.3 collective-permute-start.13
  34.3 14.9 %collective-permute-done.2.refs_3_ = f32[64,1536]{1,0:T(8,128)S(1)} collective-permute-done((f32[64,1536]{1,0:T(8,128)S(1)}, f32[64,1536]{1,0:T(8,128)S(1)}, u32[]{:S(2)}, u32[]{:S(2)}) %collective-permute-start.2) | collective-permute-done | bytes 393248 | tf_op jit(solution)/shard_map/ppermute | solution.py:243
  49.2 4.0 %shard_map.69 = (f32[64,2176]{1,0:T(8,128)S(1)}, f32[64,1536]{1,0:T(8,128)S(1)}) custom-call(s32[2]{0:T(128)S(1)} %add_convert_fusion.refs_0_, s32[128,6]{1,0:T(8,128)S(1)} %bitcast.41, f32[64,2176]{1,0:T(8,128)S(1)} %collective-permute-done.1.refs_2_, f32[64,1536]{1,0:T(8,128)S(1)} %collective-permute-done.2.refs_3_, f32[5,128,2048]{2,1,0:T(8,128)S(1)} %bitcast.37, ...), custom_call_target="tpu_custom_call" | custom-call | flops 1610612736 | bytes 524288 | tf_op jit(solution)/shard_map/pallas_call | solution.py:146
  53.2 1.9 collective-permute-start.3
  55.1 4.0 %shard_map.75 = (f32[64,2176]{1,0:T(8,128)S(1)}, f32[64,1536]{1,0:T(8,128)S(1)}) custom-call(s32[2]{0:T(128)S(1)} %add_convert_fusion.refs_0_, s32[128,6]{1,0:T(8,128)S(1)} %bitcast.42, f32[64,2176]{1,0:T(8,128)S(1)} %collective-permute-done.12.refs_2_, f32[64,1536]{1,0:T(8,128)S(1)} %collective-permute-done.13.refs_3_, f32[5,128,2048]{2,1,0:T(8,128)S(1)} %bitcast.37, ...), custom_call_target="tpu_custom_call" | custom-call | flops 1610612736 | bytes 524288 | tf_op jit(solution)/shard_map/pallas_call | solution.py:146
  59.1 3.7 %collective-permute-start.14 = (f32[64,2176]{1,0:T(8,128)S(1)}, f32[64,2176]{1,0:T(8,128)S(1)}, u32[]{:S(2)}, u32[]{:S(2)}) collective-permute-start(f32[64,2176]{1,0:T(8,128)S(1)} %get-tuple-element.43), channel_id=1, source_target_pairs={{0,4},{1,5},{2,6},{3,7},{4,8},{5,9},{6,10},{7,11},{8,12},{9,13},{1... | collective-permute-start | bytes 1671176 | tf_op jit(solution)/shard_map/ppermute | solution.py:267
  62.9 1.3 collective-permute-start.4
  64.2 1.3 collective-permute-start.15
  65.5 14.9 %collective-permute-done.4.refs_3_ = f32[64,1536]{1,0:T(8,128)S(1)} collective-permute-done((f32[64,1536]{1,0:T(8,128)S(1)}, f32[64,1536]{1,0:T(8,128)S(1)}, u32[]{:S(2)}, u32[]{:S(2)}) %collective-permute-start.4) | collective-permute-done | bytes 393248 | tf_op jit(solution)/shard_map/ppermute | solution.py:243
  80.4 4.0 %shard_map.70 = (f32[64,2176]{1,0:T(8,128)S(1)}, f32[64,1536]{1,0:T(8,128)S(1)}) custom-call(s32[2]{0:T(128)S(1)} %add_convert_fusion.refs_0_, s32[128,6]{1,0:T(8,128)S(1)} %bitcast.43, f32[64,2176]{1,0:T(8,128)S(1)} %collective-permute-done.3.refs_2_, f32[64,1536]{1,0:T(8,128)S(1)} %collective-permute-done.4.refs_3_, f32[5,128,2048]{2,1,0:T(8,128)S(1)} %bitcast.37, ...), custom_call_target="tpu_custom_call" | custom-call | flops 1610612736 | bytes 524288 | tf_op jit(solution)/shard_map/pallas_call | solution.py:146
  84.4 2.1 %collective-permute-start.5 = (f32[64,2176]{1,0:T(8,128)S(1)}, f32[64,2176]{1,0:T(8,128)S(1)}, u32[]{:S(2)}, u32[]{:S(2)}) collective-permute-start(f32[64,2176]{1,0:T(8,128)S(1)} %get-tuple-element.34), channel_id=1, source_target_pairs={{0,4},{1,5},{2,6},{3,7},{4,8},{5,9},{6,10},{7,11},{8,12},{9,13},{1... | collective-permute-start | bytes 1671176 | tf_op jit(solution)/shard_map/ppermute | solution.py:267
  86.5 4.0 %shard_map.76 = (f32[64,2176]{1,0:T(8,128)S(1)}, f32[64,1536]{1,0:T(8,128)S(1)}) custom-call(s32[2]{0:T(128)S(1)} %add_convert_fusion.refs_0_, s32[128,6]{1,0:T(8,128)S(1)} %bitcast.44, f32[64,2176]{1,0:T(8,128)S(1)} %collective-permute-done.14.refs_2_, f32[64,1536]{1,0:T(8,128)S(1)} %collective-permute-done.15.refs_3_, f32[5,128,2048]{2,1,0:T(8,128)S(1)} %bitcast.37, ...), custom_call_target="tpu_custom_call" | custom-call | flops 1610612736 | bytes 524288 | tf_op jit(solution)/shard_map/pallas_call | solution.py:146
  90.5 1.9 collective-permute-start.16
  92.4 1.3 collective-permute-start.6
  93.7 1.3 collective-permute-start.17
  95.0 17.4 %collective-permute-done.6.refs_3_ = f32[64,1536]{1,0:T(8,128)S(1)} collective-permute-done((f32[64,1536]{1,0:T(8,128)S(1)}, f32[64,1536]{1,0:T(8,128)S(1)}, u32[]{:S(2)}, u32[]{:S(2)}) %collective-permute-start.6) | collective-permute-done | bytes 393248 | tf_op jit(solution)/shard_map/ppermute | solution.py:243
  112.4 4.0 %shard_map.71 = (f32[64,2176]{1,0:T(8,128)S(1)}, f32[64,1536]{1,0:T(8,128)S(1)}) custom-call(s32[2]{0:T(128)S(1)} %add_convert_fusion.refs_0_, s32[128,6]{1,0:T(8,128)S(1)} %bitcast.45, f32[64,2176]{1,0:T(8,128)S(1)} %collective-permute-done.5.refs_2_, f32[64,1536]{1,0:T(8,128)S(1)} %collective-permute-done.6.refs_3_, f32[5,128,2048]{2,1,0:T(8,128)S(1)} %bitcast.37, ...), custom_call_target="tpu_custom_call" | custom-call | flops 1610612736 | bytes 524288 | tf_op jit(solution)/shard_map/pallas_call | solution.py:146
  116.4 1.9 collective-permute-start.7
  118.3 4.0 %shard_map.77 = (f32[64,2176]{1,0:T(8,128)S(1)}, f32[64,1536]{1,0:T(8,128)S(1)}) custom-call(s32[2]{0:T(128)S(1)} %add_convert_fusion.refs_0_, s32[128,6]{1,0:T(8,128)S(1)} %bitcast.46, f32[64,2176]{1,0:T(8,128)S(1)} %collective-permute-done.16.refs_2_, f32[64,1536]{1,0:T(8,128)S(1)} %collective-permute-done.17.refs_3_, f32[5,128,2048]{2,1,0:T(8,128)S(1)} %bitcast.37, ...), custom_call_target="tpu_custom_call" | custom-call | flops 1610612736 | bytes 524288 | tf_op jit(solution)/shard_map/pallas_call | solution.py:146
  122.3 1.9 collective-permute-start.18
  124.2 1.3 collective-permute-start.8
  125.5 1.3 collective-permute-start.19
  126.8 17.5 %collective-permute-done.8.refs_3_ = f32[64,1536]{1,0:T(8,128)S(1)} collective-permute-done((f32[64,1536]{1,0:T(8,128)S(1)}, f32[64,1536]{1,0:T(8,128)S(1)}, u32[]{:S(2)}, u32[]{:S(2)}) %collective-permute-start.8) | collective-permute-done | bytes 393248 | tf_op jit(solution)/shard_map/ppermute | solution.py:243
  144.3 4.0 %shard_map.72 = (f32[64,2176]{1,0:T(8,128)S(1)}, f32[64,1536]{1,0:T(8,128)S(1)}) custom-call(s32[2]{0:T(128)S(1)} %add_convert_fusion.refs_0_, s32[128,6]{1,0:T(8,128)S(1)} %bitcast.47, f32[64,2176]{1,0:T(8,128)S(1)} %collective-permute-done.7.refs_2_, f32[64,1536]{1,0:T(8,128)S(1)} %collective-permute-done.8.refs_3_, f32[5,128,2048]{2,1,0:T(8,128)S(1)} %bitcast.37, ...), custom_call_target="tpu_custom_call" | custom-call | flops 1610612736 | bytes 524288 | tf_op jit(solution)/shard_map/pallas_call | solution.py:146
  148.3 2.0 %collective-permute-start.9 = (f32[64,2176]{1,0:T(8,128)S(1)}, f32[64,2176]{1,0:T(8,128)S(1)}, u32[]{:S(2)}, u32[]{:S(2)}) collective-permute-start(f32[64,2176]{1,0:T(8,128)S(1)} %get-tuple-element.38), channel_id=1, source_target_pairs={{0,4},{1,5},{2,6},{3,7},{4,8},{5,9},{6,10},{7,11},{8,12},{9,13},{1... | collective-permute-start | bytes 1671176 | tf_op jit(solution)/shard_map/ppermute | solution.py:267
  150.4 4.0 %shard_map.78 = (f32[64,2176]{1,0:T(8,128)S(1)}, f32[64,1536]{1,0:T(8,128)S(1)}) custom-call(s32[2]{0:T(128)S(1)} %add_convert_fusion.refs_0_, s32[128,6]{1,0:T(8,128)S(1)} %bitcast.48, f32[64,2176]{1,0:T(8,128)S(1)} %collective-permute-done.18.refs_2_, f32[64,1536]{1,0:T(8,128)S(1)} %collective-permute-done.19.refs_3_, f32[5,128,2048]{2,1,0:T(8,128)S(1)} %bitcast.37, ...), custom_call_target="tpu_custom_call" | custom-call | flops 1610612736 | bytes 524288 | tf_op jit(solution)/shard_map/pallas_call | solution.py:146
  154.3 1.9 collective-permute-start.20
  156.3 1.3 collective-permute-start.10
  157.6 1.3 collective-permute-start.21
  158.9 1.3 collective-permute-start.28
  160.2 14.6 %collective-permute-done.10.refs_3_ = f32[64,1536]{1,0:T(8,128)S(1)} collective-permute-done((f32[64,1536]{1,0:T(8,128)S(1)}, f32[64,1536]{1,0:T(8,128)S(1)}, u32[]{:S(2)}, u32[]{:S(2)}) %collective-permute-start.10) | collective-permute-done | bytes 393248 | tf_op jit(solution)/shard_map/ppermute | solution.py:243
  174.7 4.0 %shard_map.73 = (f32[64,2048]{1,0:T(8,128)S(1)}, f32[64,128]{1,0:T(8,128)S(1)}) custom-call(s32[2]{0:T(128)S(1)} %add_convert_fusion.refs_0_, s32[128,6]{1,0:T(8,128)S(1)} %bitcast.49, f32[64,2176]{1,0:T(8,128)S(1)} %collective-permute-done.9.refs_2_, f32[64,1536]{1,0:T(8,128)S(1)} %collective-permute-done.10.refs_3_, f32[5,128,2048]{2,1,0:T(8,128)S(1)} %bitcast.37, ...), custom_call_target="tpu_custom_call" | custom-call | flops 1610612736 | bytes 524288 | tf_op jit(solution)/shard_map/pallas_call | solution.py:146
  178.7 2.2 %collective-permute-start.22 = (f32[64,128]{1,0:T(8,128)S(1)}, f32[64,128]{1,0:T(8,128)S(1)}, u32[]{:S(2)}, u32[]{:S(2)}) collective-permute-start(f32[64,128]{1,0:T(8,128)S(1)} %get-tuple-element.52.refs_2_), channel_id=1, source_target_pairs={{0,1},{1,0},{2,3},{3,2},{4,5},{5,4},{6,7},{7,6},{8,9},{9,8},{10,11... | collective-permute-start | bytes 98312 | tf_op jit(solution)/shard_map/ppermute | solution.py:207
  181.0 1.3 collective-permute-start.24
  182.2 4.0 %shard_map.79 = (f32[64,2048]{1,0:T(8,128)S(1)}, f32[64,128]{1,0:T(8,128)S(1)}) custom-call(s32[2]{0:T(128)S(1)} %add_convert_fusion.refs_0_, s32[128,6]{1,0:T(8,128)S(1)} %bitcast.50, f32[64,2176]{1,0:T(8,128)S(1)} %collective-permute-done.20.refs_2_, f32[64,1536]{1,0:T(8,128)S(1)} %collective-permute-done.21.refs_3_, f32[5,128,2048]{2,1,0:T(8,128)S(1)} %bitcast.37, ...), custom_call_target="tpu_custom_call" | custom-call | flops 1610612736 | bytes 524288 | tf_op jit(solution)/shard_map/pallas_call | solution.py:146
  186.2 1.4 collective-permute-start.25
  187.6 1.3 collective-permute-start.27
  189.1 1.3 collective-permute-done.26.refs_8_
  191.4 1.4 finish.1
  (38 shorter events, 3.4 us)
Async XLA Ops:
  0.6 14.0 %slice-start = ((s8[5242880]{0:T(1024)(128)(4,1)}), s8[1048576]{0:T(1024)(128)(4,1)S(1)}, s32[]{:S(2)}) async-start(s8[5242880]{0:T(1024)(128)(4,1)} %bitcast.36), calls=%async_computation | async-start | bytes 2097152
  1.9 12.7 %collective-permute-start = (f32[64,1536]{1,0:T(8,128)S(1)}, f32[64,1536]{1,0:T(8,128)S(1)}, u32[]{:S(2)}, u32[]{:S(2)}) collective-permute-start(f32[64,1536]{1,0:T(8,128)S(1)} %get-tuple-element.55), channel_id=1, source_target_pairs={{1,0},{2,1},{3,2},{5,4},{6,5},{7,6},{9,8},{10,9},{11,10},{13,12},{... | collective-permute-start | bytes 1179656 | tf_op jit(solution)/shard_map/ppermute | solution.py:243
  3.2 21.2 %collective-permute-start.11 = (f32[64,1536]{1,0:T(8,128)S(1)}, f32[64,1536]{1,0:T(8,128)S(1)}, u32[]{:S(2)}, u32[]{:S(2)}) collective-permute-start(f32[64,1536]{1,0:T(8,128)S(1)} %get-tuple-element.54), channel_id=1, source_target_pairs={{1,0},{2,1},{3,2},{5,4},{6,5},{7,6},{9,8},{10,9},{11,10},{13,12},{... | collective-permute-start | bytes 1179656 | tf_op jit(solution)/shard_map/ppermute | solution.py:243
  5.3 5.8 %copy-start = (f32[1,4,4,512,512]{4,3,2,1,0:T(8,128)S(1)}, f32[1,4,4,512,512]{4,3,2,1,0:T(8,128)}, u32[]{:S(2)}) copy-start(f32[1,4,4,512,512]{4,3,2,1,0:T(8,128)} %param.5) | copy-start | bytes 50331652
  11.1 3.6 %slice-start.1 = ((s8[5242880]{0:T(1024)(128)(4,1)}), s8[4194304]{0:T(1024)(128)(4,1)S(1)}, s32[]{:S(2)}) async-start(s8[5242880]{0:T(1024)(128)(4,1)} %bitcast.36), calls=%async_computation.1 | async-start | bytes 8388608
  11.1 3.6 %copy-start.1 = (f32[1,128,2048]{2,1,0:T(8,128)S(1)}, f32[1,128,2048]{2,1,0:T(8,128)}, u32[]{:S(2)}) copy-start(f32[1,128,2048]{2,1,0:T(8,128)} %refs_2_.3) | copy-start | bytes 3145732
  18.7 30.5 %collective-permute-start.1 = (f32[64,2176]{1,0:T(8,128)S(1)}, f32[64,2176]{1,0:T(8,128)S(1)}, u32[]{:S(2)}, u32[]{:S(2)}) collective-permute-start(f32[64,2176]{1,0:T(8,128)S(1)} %get-tuple-element.30), channel_id=1, source_target_pairs={{0,4},{1,5},{2,6},{3,7},{4,8},{5,9},{6,10},{7,11},{8,12},{9,13},{1... | collective-permute-start | bytes 1671176 | tf_op jit(solution)/shard_map/ppermute | solution.py:267
  28.4 26.7 %collective-permute-start.12 = (f32[64,2176]{1,0:T(8,128)S(1)}, f32[64,2176]{1,0:T(8,128)S(1)}, u32[]{:S(2)}, u32[]{:S(2)}) collective-permute-start(f32[64,2176]{1,0:T(8,128)S(1)} %get-tuple-element.41), channel_id=1, source_target_pairs={{0,4},{1,5},{2,6},{3,7},{4,8},{5,9},{6,10},{7,11},{8,12},{9,13},{1... | collective-permute-start | bytes 1671176 | tf_op jit(solution)/shard_map/ppermute | solution.py:267
  31.7 17.5 %collective-permute-start.2 = (f32[64,1536]{1,0:T(8,128)S(1)}, f32[64,1536]{1,0:T(8,128)S(1)}, u32[]{:S(2)}, u32[]{:S(2)}) collective-permute-start(f32[64,1536]{1,0:T(8,128)S(1)} %get-tuple-element.31), channel_id=1, source_target_pairs={{1,4},{2,5},{3,6},{5,8},{6,9},{7,10},{9,12},{10,13},{11,14},{13,16... | collective-permute-start | bytes 1179656 | tf_op jit(solution)/shard_map/ppermute | solution.py:243
  33.0 22.1 %collective-permute-start.13 = (f32[64,1536]{1,0:T(8,128)S(1)}, f32[64,1536]{1,0:T(8,128)S(1)}, u32[]{:S(2)}, u32[]{:S(2)}) collective-permute-start(f32[64,1536]{1,0:T(8,128)S(1)} %get-tuple-element.42), channel_id=1, source_target_pairs={{1,4},{2,5},{3,6},{5,8},{6,9},{7,10},{9,12},{10,13},{11,14},{13,16... | collective-permute-start | bytes 1179656 | tf_op jit(solution)/shard_map/ppermute | solution.py:243
  53.2 27.2 %collective-permute-start.3 = (f32[64,2176]{1,0:T(8,128)S(1)}, f32[64,2176]{1,0:T(8,128)S(1)}, u32[]{:S(2)}, u32[]{:S(2)}) collective-permute-start(f32[64,2176]{1,0:T(8,128)S(1)} %get-tuple-element.32), channel_id=1, source_target_pairs={{0,4},{1,5},{2,6},{3,7},{4,8},{5,9},{6,10},{7,11},{8,12},{9,13},{1... | collective-permute-start | bytes 1671176 | tf_op jit(solution)/shard_map/ppermute | solution.py:267
  59.1 27.4 %collective-permute-start.14 = (f32[64,2176]{1,0:T(8,128)S(1)}, f32[64,2176]{1,0:T(8,128)S(1)}, u32[]{:S(2)}, u32[]{:S(2)}) collective-permute-start(f32[64,2176]{1,0:T(8,128)S(1)} %get-tuple-element.43), channel_id=1, source_target_pairs={{0,4},{1,5},{2,6},{3,7},{4,8},{5,9},{6,10},{7,11},{8,12},{9,13},{1... | collective-permute-start | bytes 1671176 | tf_op jit(solution)/shard_map/ppermute | solution.py:267
  62.9 17.5 %collective-permute-start.4 = (f32[64,1536]{1,0:T(8,128)S(1)}, f32[64,1536]{1,0:T(8,128)S(1)}, u32[]{:S(2)}, u32[]{:S(2)}) collective-permute-start(f32[64,1536]{1,0:T(8,128)S(1)} %get-tuple-element.33), channel_id=1, source_target_pairs={{1,4},{2,5},{3,6},{5,8},{6,9},{7,10},{9,12},{10,13},{11,14},{13,16... | collective-permute-start | bytes 1179656 | tf_op jit(solution)/shard_map/ppermute | solution.py:243
  64.2 22.3 %collective-permute-start.15 = (f32[64,1536]{1,0:T(8,128)S(1)}, f32[64,1536]{1,0:T(8,128)S(1)}, u32[]{:S(2)}, u32[]{:S(2)}) collective-permute-start(f32[64,1536]{1,0:T(8,128)S(1)} %get-tuple-element.44), channel_id=1, source_target_pairs={{1,4},{2,5},{3,6},{5,8},{6,9},{7,10},{9,12},{10,13},{11,14},{13,16... | collective-permute-start | bytes 1179656 | tf_op jit(solution)/shard_map/ppermute | solution.py:243
  84.4 28.0 %collective-permute-start.5 = (f32[64,2176]{1,0:T(8,128)S(1)}, f32[64,2176]{1,0:T(8,128)S(1)}, u32[]{:S(2)}, u32[]{:S(2)}) collective-permute-start(f32[64,2176]{1,0:T(8,128)S(1)} %get-tuple-element.34), channel_id=1, source_target_pairs={{0,4},{1,5},{2,6},{3,7},{4,8},{5,9},{6,10},{7,11},{8,12},{9,13},{1... | collective-permute-start | bytes 1671176 | tf_op jit(solution)/shard_map/ppermute | solution.py:267
  90.5 27.8 %collective-permute-start.16 = (f32[64,2176]{1,0:T(8,128)S(1)}, f32[64,2176]{1,0:T(8,128)S(1)}, u32[]{:S(2)}, u32[]{:S(2)}) collective-permute-start(f32[64,2176]{1,0:T(8,128)S(1)} %get-tuple-element.45), channel_id=1, source_target_pairs={{0,4},{1,5},{2,6},{3,7},{4,8},{5,9},{6,10},{7,11},{8,12},{9,13},{1... | collective-permute-start | bytes 1671176 | tf_op jit(solution)/shard_map/ppermute | solution.py:267
  92.4 20.0 %collective-permute-start.6 = (f32[64,1536]{1,0:T(8,128)S(1)}, f32[64,1536]{1,0:T(8,128)S(1)}, u32[]{:S(2)}, u32[]{:S(2)}) collective-permute-start(f32[64,1536]{1,0:T(8,128)S(1)} %get-tuple-element.35), channel_id=1, source_target_pairs={{1,4},{2,5},{3,6},{5,8},{6,9},{7,10},{9,12},{10,13},{11,14},{13,16... | collective-permute-start | bytes 1179656 | tf_op jit(solution)/shard_map/ppermute | solution.py:243
  93.7 24.6 %collective-permute-start.17 = (f32[64,1536]{1,0:T(8,128)S(1)}, f32[64,1536]{1,0:T(8,128)S(1)}, u32[]{:S(2)}, u32[]{:S(2)}) collective-permute-start(f32[64,1536]{1,0:T(8,128)S(1)} %get-tuple-element.46), channel_id=1, source_target_pairs={{1,4},{2,5},{3,6},{5,8},{6,9},{7,10},{9,12},{10,13},{11,14},{13,16... | collective-permute-start | bytes 1179656 | tf_op jit(solution)/shard_map/ppermute | solution.py:243
  116.4 27.9 %collective-permute-start.7 = (f32[64,2176]{1,0:T(8,128)S(1)}, f32[64,2176]{1,0:T(8,128)S(1)}, u32[]{:S(2)}, u32[]{:S(2)}) collective-permute-start(f32[64,2176]{1,0:T(8,128)S(1)} %get-tuple-element.36), channel_id=1, source_target_pairs={{0,4},{1,5},{2,6},{3,7},{4,8},{5,9},{6,10},{7,11},{8,12},{9,13},{1... | collective-permute-start | bytes 1671176 | tf_op jit(solution)/shard_map/ppermute | solution.py:267
  122.3 28.0 %collective-permute-start.18 = (f32[64,2176]{1,0:T(8,128)S(1)}, f32[64,2176]{1,0:T(8,128)S(1)}, u32[]{:S(2)}, u32[]{:S(2)}) collective-permute-start(f32[64,2176]{1,0:T(8,128)S(1)} %get-tuple-element.47), channel_id=1, source_target_pairs={{0,4},{1,5},{2,6},{3,7},{4,8},{5,9},{6,10},{7,11},{8,12},{9,13},{1... | collective-permute-start | bytes 1671176 | tf_op jit(solution)/shard_map/ppermute | solution.py:267
  124.2 20.1 %collective-permute-start.8 = (f32[64,1536]{1,0:T(8,128)S(1)}, f32[64,1536]{1,0:T(8,128)S(1)}, u32[]{:S(2)}, u32[]{:S(2)}) collective-permute-start(f32[64,1536]{1,0:T(8,128)S(1)} %get-tuple-element.37), channel_id=1, source_target_pairs={{1,4},{2,5},{3,6},{5,8},{6,9},{7,10},{9,12},{10,13},{11,14},{13,16... | collective-permute-start | bytes 1179656 | tf_op jit(solution)/shard_map/ppermute | solution.py:243
  125.5 24.8 %collective-permute-start.19 = (f32[64,1536]{1,0:T(8,128)S(1)}, f32[64,1536]{1,0:T(8,128)S(1)}, u32[]{:S(2)}, u32[]{:S(2)}) collective-permute-start(f32[64,1536]{1,0:T(8,128)S(1)} %get-tuple-element.48), channel_id=1, source_target_pairs={{1,4},{2,5},{3,6},{5,8},{6,9},{7,10},{9,12},{10,13},{11,14},{13,16... | collective-permute-start | bytes 1179656 | tf_op jit(solution)/shard_map/ppermute | solution.py:243
  148.3 10.6 %copy-start.2 = (f32[1,128]{1,0:T(1,128)S(1)}, f32[1,128]{1,0:T(1,128)}, u32[]{:S(2)}) copy-start(f32[1,128]{1,0:T(1,128)} %param.8) | copy-start | bytes 1540
  148.3 26.5 %collective-permute-start.9 = (f32[64,2176]{1,0:T(8,128)S(1)}, f32[64,2176]{1,0:T(8,128)S(1)}, u32[]{:S(2)}, u32[]{:S(2)}) collective-permute-start(f32[64,2176]{1,0:T(8,128)S(1)} %get-tuple-element.38), channel_id=1, source_target_pairs={{0,4},{1,5},{2,6},{3,7},{4,8},{5,9},{6,10},{7,11},{8,12},{9,13},{1... | collective-permute-start | bytes 1671176 | tf_op jit(solution)/shard_map/ppermute | solution.py:267
  154.3 27.9 %collective-permute-start.20 = (f32[64,2176]{1,0:T(8,128)S(1)}, f32[64,2176]{1,0:T(8,128)S(1)}, u32[]{:S(2)}, u32[]{:S(2)}) collective-permute-start(f32[64,2176]{1,0:T(8,128)S(1)} %get-tuple-element.49), channel_id=1, source_target_pairs={{0,4},{1,5},{2,6},{3,7},{4,8},{5,9},{6,10},{7,11},{8,12},{9,13},{1... | collective-permute-start | bytes 1671176 | tf_op jit(solution)/shard_map/ppermute | solution.py:267
  156.3 18.5 %collective-permute-start.10 = (f32[64,1536]{1,0:T(8,128)S(1)}, f32[64,1536]{1,0:T(8,128)S(1)}, u32[]{:S(2)}, u32[]{:S(2)}) collective-permute-start(f32[64,1536]{1,0:T(8,128)S(1)} %get-tuple-element.39), channel_id=1, source_target_pairs={{1,4},{2,5},{3,6},{5,8},{6,9},{7,10},{9,12},{10,13},{11,14},{13,16... | collective-permute-start | bytes 1179656 | tf_op jit(solution)/shard_map/ppermute | solution.py:243
  157.6 23.4 %collective-permute-start.21 = (f32[64,1536]{1,0:T(8,128)S(1)}, f32[64,1536]{1,0:T(8,128)S(1)}, u32[]{:S(2)}, u32[]{:S(2)}) collective-permute-start(f32[64,1536]{1,0:T(8,128)S(1)} %get-tuple-element.50), channel_id=1, source_target_pairs={{1,4},{2,5},{3,6},{5,8},{6,9},{7,10},{9,12},{10,13},{11,14},{13,16... | collective-permute-start | bytes 1179656 | tf_op jit(solution)/shard_map/ppermute | solution.py:243
  158.9 28.7 %collective-permute-start.28 = (f32[1,128]{1,0:T(1,128)S(1)}, f32[1,128]{1,0:T(1,128)S(1)}, u32[]{:S(2)}, u32[]{:S(2)}) collective-permute-start(f32[1,128]{1,0:T(1,128)S(1)} %copy-done.2), channel_id=1, source_target_pairs={{0,20},{4,24},{8,28},{1,21},{5,25},{9,29},{2,22},{6,26},{10,30},{3... | collective-permute-start | bytes 1544 | tf_op jit(solution)/shard_map/ppermute | solution.py:249
  178.7 8.9 %collective-permute-start.22 = (f32[64,128]{1,0:T(8,128)S(1)}, f32[64,128]{1,0:T(8,128)S(1)}, u32[]{:S(2)}, u32[]{:S(2)}) collective-permute-start(f32[64,128]{1,0:T(8,128)S(1)} %get-tuple-element.52.refs_2_), channel_id=1, source_target_pairs={{0,1},{1,0},{2,3},{3,2},{4,5},{5,4},{6,7},{7,6},{8,9},{9,8},{10,11... | collective-permute-start | bytes 98312 | tf_op jit(solution)/shard_map/ppermute | solution.py:207
  181.0 7.9 %collective-permute-start.23 = (f32[64,128]{1,0:T(8,128)S(1)}, f32[64,128]{1,0:T(8,128)S(1)}, u32[]{:S(2)}, u32[]{:S(2)}) collective-permute-start(f32[64,128]{1,0:T(8,128)S(1)} %get-tuple-element.52.refs_2_), channel_id=1, source_target_pairs={{0,2},{1,3},{2,0},{3,1},{4,6},{5,7},{6,4},{7,5},{8,10},{9,11},{10,... | collective-permute-start | bytes 98312 | tf_op jit(solution)/shard_map/ppermute | solution.py:207
  181.0 7.9 %collective-permute-start.24 = (f32[64,128]{1,0:T(8,128)S(1)}, f32[64,128]{1,0:T(8,128)S(1)}, u32[]{:S(2)}, u32[]{:S(2)}) collective-permute-start(f32[64,128]{1,0:T(8,128)S(1)} %get-tuple-element.52.refs_2_), channel_id=1, source_target_pairs={{0,3},{1,2},{2,1},{3,0},{4,7},{5,6},{6,5},{7,4},{8,11},{9,10},{10,... | collective-permute-start | bytes 98312 | tf_op jit(solution)/shard_map/ppermute | solution.py:207
  186.2 2.8 %collective-permute-start.25 = (f32[64,128]{1,0:T(8,128)S(1)}, f32[64,128]{1,0:T(8,128)S(1)}, u32[]{:S(2)}, u32[]{:S(2)}) collective-permute-start(f32[64,128]{1,0:T(8,128)S(1)} %get-tuple-element.53.refs_6_), channel_id=1, source_target_pairs={{0,1},{1,0},{2,3},{3,2},{4,5},{5,4},{6,7},{7,6},{8,9},{9,8},{10,11... | collective-permute-start | bytes 98312 | tf_op jit(solution)/shard_map/ppermute | solution.py:207
  187.6 2.8 %collective-permute-start.26 = (f32[64,128]{1,0:T(8,128)S(1)}, f32[64,128]{1,0:T(8,128)S(1)}, u32[]{:S(2)}, u32[]{:S(2)}) collective-permute-start(f32[64,128]{1,0:T(8,128)S(1)} %get-tuple-element.53.refs_6_), channel_id=1, source_target_pairs={{0,2},{1,3},{2,0},{3,1},{4,6},{5,7},{6,4},{7,5},{8,10},{9,11},{10,... | collective-permute-start | bytes 98312 | tf_op jit(solution)/shard_map/ppermute | solution.py:207
  187.6 3.7 %collective-permute-start.27 = (f32[64,128]{1,0:T(8,128)S(1)}, f32[64,128]{1,0:T(8,128)S(1)}, u32[]{:S(2)}, u32[]{:S(2)}) collective-permute-start(f32[64,128]{1,0:T(8,128)S(1)} %get-tuple-element.53.refs_6_), channel_id=1, source_target_pairs={{0,3},{1,2},{2,1},{3,0},{4,7},{5,6},{6,5},{7,4},{8,11},{9,10},{10,... | collective-permute-start | bytes 98312 | tf_op jit(solution)/shard_map/ppermute | solution.py:207

commit v3 on v2

v3 whole, which is shorter than its diff:
```python
import functools

import jax
import jax.numpy as jnp
from jax import lax
from jax.experimental import pallas as pl
from jax.experimental.pallas import tpu as pltpu
from jax.sharding import PartitionSpec as P


EPSILON = 1e-06
SCALE = 256.0
LANES = 128
CHUNKS = 2
BUFFERS = 8
VMEM_LIMIT = 12 << 20
BF = jnp.bfloat16
F32 = jnp.float32
VMEM_SPEC = pl.BlockSpec(memory_space=pltpu.VMEM)


def sums_depth(ticks):
    return -(-(2 * ticks + 1) // 8) * 8


def in_vmem(value):
    return pltpu.with_memory_space_constraint(value, pltpu.VMEM)


def put(stack, index, start, value):
    rows, cols = value.shape
    hi = value.astype(BF)
    stack[index, :rows, start : start + cols] = hi
    stack[index, rows:, start : start + cols] = (value - hi.astype(F32)).astype(BF)


def product(both, hi, lo):
    rows = both.shape[0] // 2
    wide = jnp.dot(both, hi, preferred_element_type=F32)
    value = wide[:rows] + wide[rows:]
    return value + jnp.dot(both[:rows], lo, preferred_element_type=F32)


def folded_squares(value):
    square = value * value
    total = square[:, :LANES]
    for start in range(LANES, square.shape[1], LANES):
        total = total + square[:, start : start + LANES]
    return total


def as_row(index, squares, depth):
    rows = squares.shape[0]
    lane = lax.broadcasted_iota(jnp.int32, (rows, LANES), 1)
    column = jnp.sum(squares, axis=1, keepdims=True)
    return jnp.where(lane == index, column, 0.0).T[:depth]


def open_kernel(dims, ticks, flag_ref, w_ref, rows_ref, outcome_ref, prior_ref, *rest):
    hi_ref, lo_ref, out_ref, sums_ref, choice_ref, *rest = rest
    stack, buffer, row_buffer, outcome_buffer, prior_buffer, sems = rest
    n_out, local, width, _, _ = dims
    rows = rows_ref.shape[1]
    depth, count = buffer.shape[0], n_out * local
    order = [(n, s) for s in range(local) for n in range(n_out)]
    copies = [
        pltpu.make_async_copy(w_ref.at[n, s], buffer.at[i % depth], sems.at[i % depth])
        for i, (n, s) in enumerate(order)
    ]
    inputs = [
        pltpu.make_async_copy(outcome_ref, outcome_buffer, sems.at[depth]),
        pltpu.make_async_copy(rows_ref, row_buffer, sems.at[depth + 1]),
        pltpu.make_async_copy(prior_ref, prior_buffer, sems.at[depth + 2]),
    ]
    for copy in inputs:
        copy.start()
    for copy in copies[:depth]:
        copy.start()
    for copy in inputs:
        copy.wait()
    outcomes = outcome_buffer[:, 0].astype(F32)
    padding = jnp.zeros((LANES - outcomes.shape[0], rows), F32)
    choice_ref[...] = jnp.concatenate([outcomes, padding], axis=0).T
    choice = choice_ref[:, :1]
    for q in range(local):
        put(stack, q, 0, row_buffer[0, :, q * width : (q + 1) * width] * SCALE)
    total = jnp.zeros((rows, LANES), F32)
    selected = None
    for i, (n, s) in enumerate(order):
        copies[i].wait()
        w = buffer[i % depth]
        hi = w.astype(BF)
        lo = (w - hi.astype(F32)).astype(BF)
        hi_ref[n, s] = hi
        lo_ref[n, s] = lo
        if s + n < local:
            value = product(stack[s + n], hi, lo)
            total = total + folded_squares(value)
            selected = jnp.where(choice == n, value, 0.0 if n == 0 else selected)
        if i + depth < count:
            copies[i + depth].start()
        if n == n_out - 1:
            out_ref[:, s * width : (s + 1) * width] = selected
    depth = sums_ref.shape[0]
    row = lax.broadcasted_iota(jnp.int32, (depth, rows), 0)
    prior = jnp.where(flag_ref[2] == 1, jnp.broadcast_to(prior_buffer[...], (depth, rows)), 0.0)
    sums_ref[...] = as_row(1, total, depth) + jnp.where(row == 2 * ticks, prior, 0.0)


def opened(dims, ticks, flags, weights, in_flight, outcomes, prior):
    n_out, local, width, _, _ = dims
    rows = in_flight.shape[1]
    depth = min(BUFFERS, n_out * local)
    operands = [weights, in_flight, outcomes, prior]
    return pl.pallas_call(
        functools.partial(open_kernel, dims, ticks),
        in_specs=[pl.BlockSpec(memory_space=pltpu.SMEM)]
        + [pl.BlockSpec(memory_space=pltpu.HBM)] * len(operands),
        out_specs=[VMEM_SPEC] * 5,
        out_shape=[
            pltpu.VMEM(weights.shape, BF),
            pltpu.VMEM(weights.shape, BF),
            pltpu.VMEM((rows, local * width), F32),
            pltpu.VMEM((sums_depth(ticks), rows), F32),
            pltpu.VMEM((rows, LANES), F32),
        ],
        scratch_shapes=[
            pltpu.VMEM((local, 2 * rows, width), BF),
            pltpu.VMEM((depth, width, width), F32),
            pltpu.VMEM(in_flight.shape, F32),
            pltpu.VMEM(outcomes.shape, jnp.int32),
            pltpu.VMEM(prior.shape, F32),
            pltpu.SemaphoreType.DMA((depth + 3,)),
        ],
        compiler_params=pltpu.CompilerParams(vmem_limit_bytes=2 * VMEM_LIMIT),
        name="opened",
        cost_estimate=pl.CostEstimate(
            flops=3 * rows * n_out * local * width * width,
            bytes_accessed=4 * weights.size,
            transcendentals=0,
        ),
    )(flags, *[pltpu.with_memory_space_constraint(value, pltpu.HBM) for value in operands])


def near_kernel(dims, tick, chunk, *refs):
    flag_ref, choice_ref, hi_ref, lo_ref, main_ref, entering_ref, out_ref, sums_ref, stack = refs
    n_out, local, width, rows, _ = dims
    own = slice(chunk * rows, (chunk + 1) * rows)
    at_start = flag_ref[0] == 1
    group = 0
    for q in range(local):
        for start in range(0, width, LANES):
            cols = slice(q * width + start, q * width + start + LANES)
            fresh = entering_ref[tick - 1, own, cols] * SCALE
            value = main_ref[group * rows : (group + 1) * rows]
            put(stack, q, start, jnp.where(at_start, fresh, value))
            group += 1
    choice = choice_ref[own, tick : tick + 1]
    total = jnp.zeros((rows, LANES), F32)
    for s in range(local):
        selected = None
        for n in range(min(n_out, local - s)):
            value = product(stack[s + n], hi_ref[n, s], lo_ref[n, s])
            total = total + folded_squares(value)
            selected = jnp.where(choice == n, value, 0.0 if n == 0 else selected)
        out_ref[:, s * width : (s + 1) * width] = selected
    depth = sums_ref.shape[0]
    old = main_ref[group * rows :, :rows]
    sums_ref[...] = jnp.where(at_start, 0.0, old) + as_row(2 * tick + 1, total, depth)


def far_kernel(dims, tick, ticks, chunk, *refs):
    n_out, local, width, rows, halo = dims
    last = tick == ticks - 1
    refs = list(refs)
    flag_ref, choice_ref, hi_ref, lo_ref, base_ref, base_sums_ref = refs[:6]
    halo_refs = refs[6 : 6 + len(halo)]
    other_refs, stack = refs[6 + len(halo) : -1], refs[-1]
    own = slice(chunk * rows, (chunk + 1) * rows)
    base = slice(None) if base_ref.shape[0] == rows else own
    index = local
    for ref, blocks in zip(halo_refs, halo):
        for q in range(blocks):
            value = ref[:, q * width : (q + 1) * width]
            put(stack, index, 0, value * SCALE if tick == 0 else value)
            index += 1
    if last:
        *done_refs, out_ref, part_ref = other_refs
    else:
        entering_ref, out_ref, edge_ref = other_refs
    at_end = flag_ref[1] == 1
    choice = choice_ref[own, tick : tick + 1]
    total = jnp.zeros((rows, LANES), F32)
    picked = jnp.zeros((rows, LANES), F32)
    for s in range(local):
        cols = slice(s * width, (s + 1) * width)
        selected = base_ref[base, cols]
        for n in range(max(0, local - s), n_out):
            value = product(stack[s + n], hi_ref[n, s], lo_ref[n, s])
            total = total + folded_squares(value)
            selected = jnp.where(choice == n, value, selected)
        picked = picked + folded_squares(selected)
        if last:
            out_ref[:, cols] = selected
            continue
        for start in range(0, width, LANES):
            at = (s * width + start) // LANES * rows
            out_ref[at : at + rows] = selected[:, start : start + LANES]
        if s < halo[0]:
            fresh = entering_ref[tick, own, cols] * SCALE
            edge_ref[:, cols] = jnp.where(at_end, fresh, selected)
    depth = base_sums_ref.shape[0]
    sums = base_sums_ref[:, base] + as_row(2 * tick + 1, total, depth)
    sums = sums + as_row(2 * tick, picked, depth)
    if last:
        for ref in done_refs:
            part_ref[:, : chunk * rows] = ref[:, : chunk * rows]
        part_ref[:, own] = sums
    else:
        out_ref[local * width // LANES * rows :, :rows] = sums


def step(kernel, dims, blocks, count, outs, operands):
    _, local, width, rows, _ = dims
    flags, *values = operands
    return pl.pallas_call(
        kernel,
        in_specs=[pl.BlockSpec(memory_space=pltpu.SMEM)] + [VMEM_SPEC] * len(values),
        out_specs=[VMEM_SPEC] * len(outs),
        out_shape=[pltpu.VMEM(shape, F32) for shape in outs],
        scratch_shapes=[pltpu.VMEM((blocks, 2 * rows, width), BF)],
        compiler_params=pltpu.CompilerParams(vmem_limit_bytes=VMEM_LIMIT),
        cost_estimate=pl.CostEstimate(
            flops=6 * rows * count * width * width,
            bytes_accessed=4 * rows * local * width,
            transcendentals=0,
        ),
    )(flags, *[in_vmem(value) for value in values])


def near(dims, tick, ticks, chunk, shared, main, entering):
    n_out, local, width, rows, _ = dims
    count = sum(s + n < local for s in range(local) for n in range(n_out))
    outs = [(rows, local * width), (sums_depth(ticks), rows)]
    kernel = functools.partial(near_kernel, dims, tick, chunk)
    operands = [*shared, main, entering]
    return step(kernel, dims, local, count, outs, operands)


def far(dims, tick, ticks, chunk, shared, state, halos, entering, done):
    n_out, local, width, rows, halo = dims
    count = sum(s + n >= local for s in range(local) for n in range(n_out))
    depth = sums_depth(ticks)
    if tick == ticks - 1:
        outs = [(rows, local * width), (depth, CHUNKS * rows)]
        others = done
    else:
        outs = [(local * width // LANES * rows + depth, LANES), (rows, halo[0] * width)]
        others = [entering]
    kernel = functools.partial(far_kernel, dims, tick, ticks, chunk)
    operands = [*shared, *state, *halos, *others]
    blocks = local + sum(halo)
    return step(kernel, dims, blocks, count, outs, operands)


def final_kernel(ticks, bond, chunks, copies, *refs):
    state_refs = refs[:chunks]
    part_refs = refs[chunks : chunks + copies]
    env_ref, logp_ref = refs[chunks + copies :]
    rows = state_refs[0].shape[0]
    sums = [ref[...] for ref in part_refs]
    while len(sums) > 1:
        sums = [sums[i] + sums[i + 1] for i in range(0, len(sums), 2)]
    log_weight = sums[0][2 * ticks : 2 * ticks + 1]
    sums = sums[0] * (1.0 / (bond * SCALE * SCALE))
    factor = jnp.ones_like(log_weight)
    for t in range(ticks):
        picked = sums[2 * t : 2 * t + 1] * factor * factor + EPSILON
        total = sums[2 * t + 1 : 2 * t + 2] * factor * factor + EPSILON
        log_weight = log_weight + jnp.log(picked) - jnp.log(total)
        factor = factor * lax.rsqrt(picked)
    logp_ref[...] = log_weight
    column = jnp.broadcast_to(factor * (1.0 / SCALE), (LANES, factor.shape[1])).T[:, :1]
    for c in range(chunks):
        own = slice(c * rows, (c + 1) * rows)
        env_ref[0, own] = state_refs[c][...] * column[own]


def finish(states, parts, ticks, bond):
    rows = sum(value.shape[0] for value in states)
    span = states[0].shape[1]
    operands = [*states, *parts]
    return pl.pallas_call(
        functools.partial(final_kernel, ticks, float(bond), len(states), len(parts)),
        in_specs=[VMEM_SPEC] * len(operands),
        out_shape=[
            jax.ShapeDtypeStruct((1, rows, span), F32),
            jax.ShapeDtypeStruct((1, rows), F32),
        ],
        compiler_params=pltpu.CompilerParams(vmem_limit_bytes=VMEM_LIMIT),
        name="finish",
    )(*[in_vmem(value) for value in operands])


def sector_terms(value, sectors):
    if sectors & (sectors - 1) or sectors == 1:
        return [lax.psum(value, "sector")]

    def partner(term, mask):
        return lax.ppermute(term, "sector", [(d, d ^ mask) for d in range(sectors)])

    if sectors <= 4:
        return [value] + [partner(value, mask) for mask in range(1, sectors)]
    mask = 1
    while 2 * mask < sectors:
        value = value + partner(value, mask)
        mask *= 2
    return [value, partner(value, mask)]


def per_device(sites, sectors, site_tensor, outcomes, in_flight, prior_logp, entering):
    weights = site_tensor[0]
    n_out, local, width = weights.shape[:3]
    span = in_flight.shape[2]
    ticks = outcomes.shape[0]
    rows = in_flight.shape[1] // CHUNKS
    need = n_out - 1
    halo = []
    while need > 0:
        halo.append(min(local, need))
        need -= halo[-1]
    dims = (n_out, local, width, rows, tuple(halo))
    up = [(k, k + 1) for k in range(sites - 1)]

    def moved(edge, shift):
        pieces = []
        for hop, blocks in enumerate(halo):
            pairs = [
                (k * sectors + d + hop + 1, (k + shift) % sites * sectors + d)
                for k in range(sites)
                for d in range(sectors - hop - 1)
            ]
            pieces.append(lax.ppermute(edge[:, : blocks * width], ("site", "sector"), pairs))
        return pieces

    site = lax.axis_index("site")
    flags = [site == 0, site == sites - 1, lax.axis_index("sector") == 0]
    flags = jnp.stack(flags).astype(jnp.int32)
    halos = [
        moved(in_flight[0, c * rows : (c + 1) * rows, : halo[0] * width], 0)
        for c in range(CHUNKS)
    ]
    hi, lo, base, base_sums, choice = opened(
        dims, ticks, flags, weights, in_flight, outcomes, prior_logp
    )
    shared = [flags, choice, hi, lo]
    states = [(base, base_sums)] * CHUNKS
    mains = [None] * CHUNKS
    done = []
    for tick in range(ticks):
        for c in range(CHUNKS):
            if tick > 0:
                states[c] = near(dims, tick, ticks, c, shared, mains[c], entering)
            mains[c], other = far(dims, tick, ticks, c, shared, states[c], halos[c], entering, done)
            if tick == ticks - 1:
                done = [other]
                continue
            mains[c] = lax.ppermute(mains[c], "site", up)
            halos[c] = moved(other, 1)
    parts = sector_terms(done[0], sectors)
    return tuple(finish(mains, parts, ticks, span * sectors))


def solution(mesh):
    sizes = (mesh.shape["site"], mesh.shape["sector"])

    def whole(site_tensor, outcomes, *others):
        call = jax.shard_map(
            functools.partial(per_device, *sizes),
            mesh=mesh,
            in_specs=(
                P("site", None, "sector", None, None),
                P(None, "site", None),
                P("site", None, "sector"),
                P("site", None),
                P(None, None, "sector"),
            ),
            out_specs=(P("site", None, "sector"), P("site", None)),
            check_vma=False,
        )
        return call(site_tensor, outcomes, *others)

    return whole
```

time: 195 us -> 181 us (0.928)
  waiting for transfers between devices: 81.8 us -> 72.6 us
  local copies, waits for them, and re-layouts: 7.83 us -> 1.27 us
  Pallas kernels: 52.7 us -> 58.5 us
  starting transfers between devices: 49.3 us -> 46.6 us
    ppermute x29 -> x25, waiting for transfers between devices: 81.8 us -> 72.6 us  [the longest x12 70.1 us: moved(): lax.ppermute(edge[:, :blocks * width], ('site', 'sector'), pairs)]
    unnamed x11 -> x4, local copies, waits for them, and re-layouts: 6.58 us -> 0.01 us
    pallas_call x13 -> x23, Pallas kernels: 51.3 us -> 57.2 us  [the longest x22 49.4 us: step(): pl.pallas_call(kernel, in_specs=[pl.BlockSpec(memory_space=pltpu.SMEM)] +...]
    ppermute x29 -> x25, starting transfers between devices: 49.3 us -> 46.6 us  [the longest x10 27.3 us: per_device(): mains[c] = lax.ppermute(mains[c], 'site', up)]
  transfers between devices with their start and end apart: 29 -> 25, of which waited for: 9 -> 9; matrix products, arithmetic and copies ran while one was open for 0% -> 0% of each run, Pallas kernels for 27% -> 31%
where the time goes in v3:
time: 181 us; the launch traced here: 180 us
  waiting for transfers between devices  72.6 us (40%)
  Pallas kernels  58.5 us (32%)
  starting transfers between devices  46.6 us (26%)
    ppermute x12, waiting for transfers between devices, moved(): lax.ppermute(edge[:, :blocks * width], ('site', 'sector'), pairs)  70.1 us
    pallas_call x22, Pallas kernels, step(): pl.pallas_call(kernel, in_specs=[pl.BlockSpec(memory_space=pltpu.SMEM)] +...  49.4 us
    ppermute x10, starting transfers between devices, per_device(): mains[c] = lax.ppermute(mains[c], 'site', up)  27.3 us
    ppermute x12, starting transfers between devices, moved(): lax.ppermute(edge[:, :blocks * width], ('site', 'sector'), pairs)  15.9 us
    pallas_call x1, Pallas kernels, opened(): pl.pallas_call(functools.partial(open_kernel, dims, ticks), in_specs=[pl....  7.82 us
  transfers between devices with their start and end apart: 25, of which 9 were waited for; matrix products, arithmetic and copies ran while one was open for 0% of the time, Pallas kernels for 31%

profile of v3, /device:TPU:1, one launch (start us, length us, event | category | flops | bytes accessed | tf_op | source)
XLA Modules:
  0.0 180.0 jit_solution(10809941680536694666)
XLA Ops:
  4.6 7.8 %opened.1 = (bf16[4,4,512,512]{3,2,1,0:T(8,128)(2,1)S(1)}, bf16[4,4,512,512]{3,2,1,0:T(8,128)(2,1)S(1)}, f32[128,2048]{1,0:T(8,128)S(1)}, f32[16,128]{1,0:T(8,128)S(1)}, f32[128,128]{1,0:T(8,128)S(1)}) custom-call(s32[3]{0:T(128)S(1)} %add_convert_fusion.flag_ref.refs_0_, f32[4,4,512,512]{3,2,1,0:T(8,128)} %bitcast.10, f32[1,128,2048]{2,1,0:T(8,128)} %rows_ref.1, ...), custom_call_target="tpu_custom_call" | custom-call | flops 1610612736 | bytes 16777216 | tf_op jit(solution)/shard_map/opened/pallas_call | solution.py:115
  12.4 2.2 %collective-permute-done.refs_6_ = f32[64,1536]{1,0:T(8,128)S(1)} collective-permute-done((f32[64,1536]{1,0:T(8,128)S(1)}, f32[64,1536]{1,0:T(8,128)S(1)}, u32[]{:S(2)}, u32[]{:S(2)}) %collective-permute-start) | collective-permute-done | bytes 393248 | tf_op jit(solution)/shard_map/ppermute | solution.py:343
  14.7 1.9 %shard_map.68 = (f32[1040,128]{1,0:T(8,128)S(1)}, f32[64,1536]{1,0:T(8,128)S(1)}) custom-call(s32[3]{0:T(128)S(1)} %add_convert_fusion.flag_ref.refs_0_, f32[128,128]{1,0:T(8,128)S(1)} %get-tuple-element.51.refs_1_, bf16[4,4,512,512]{3,2,1,0:T(8,128)(2,1)S(1)} %get-tuple-element.52.refs_2_, bf16[4,4,512,512]{3,2,1,0:T(8,128)(2,1)S(1)} %get-tuple-element.53.refs_3_, ...), custom_call_target="tpu_custom_call" | custom-call | flops 603979776 | bytes 524288 | tf_op jit(solution)/shard_map/pallas_call | solution.py:226
  16.6 5.7 %collective-permute-start.1 = (f32[1040,128]{1,0:T(8,128)S(1)}, f32[1040,128]{1,0:T(8,128)S(1)}, u32[]{:S(2)}, u32[]{:S(2)}) collective-permute-start(f32[1040,128]{1,0:T(8,128)S(1)} %get-tuple-element.56), channel_id=1, source_target_pairs={{0,4},{4,8},{8,12},{12,16},{16,20},{20,24},{24,28},{1,5},{5,9},{9,... | collective-permute-start | bytes 1597448 | tf_op jit(solution)/shard_map/ppermute | solution.py:368
  23.1 2.0 %shard_map.79 = (f32[1040,128]{1,0:T(8,128)S(1)}, f32[64,1536]{1,0:T(8,128)S(1)}) custom-call(s32[3]{0:T(128)S(1)} %add_convert_fusion.flag_ref.refs_0_, f32[128,128]{1,0:T(8,128)S(1)} %get-tuple-element.51.refs_1_, bf16[4,4,512,512]{3,2,1,0:T(8,128)(2,1)S(1)} %get-tuple-element.52.refs_2_, bf16[4,4,512,512]{3,2,1,0:T(8,128)(2,1)S(1)} %get-tuple-element.53.refs_3_, ...), custom_call_target="tpu_custom_call" | custom-call | flops 603979776 | bytes 524288 | tf_op jit(solution)/shard_map/pallas_call | solution.py:226
  25.1 4.6 %collective-permute-start.12 = (f32[1040,128]{1,0:T(8,128)S(1)}, f32[1040,128]{1,0:T(8,128)S(1)}, u32[]{:S(2)}, u32[]{:S(2)}) collective-permute-start(f32[1040,128]{1,0:T(8,128)S(1)} %get-tuple-element.77), channel_id=1, source_target_pairs={{0,4},{4,8},{8,12},{12,16},{16,20},{20,24},{24,28},{1,5},{5,9},{9,... | collective-permute-start | bytes 1597448 | tf_op jit(solution)/shard_map/ppermute | solution.py:368
  32.3 2.6 %shard_map.69 = (f32[64,2048]{1,0:T(8,128)S(1)}, f32[16,64]{1,0:T(8,128)S(1)}) custom-call(s32[3]{0:T(128)S(1)} %add_convert_fusion.flag_ref.refs_0_, f32[128,128]{1,0:T(8,128)S(1)} %get-tuple-element.51.refs_1_, bf16[4,4,512,512]{3,2,1,0:T(8,128)(2,1)S(1)} %get-tuple-element.52.refs_2_, bf16[4,4,512,512]{3,2,1,0:T(8,128)(2,1)S(1)} %get-tuple-element.53.refs_3_, ...), custom_call_target="tpu_custom_call" | custom-call | flops 1006632960 | bytes 524288 | tf_op jit(solution)/shard_map/pallas_call | solution.py:226
  34.9 12.3 %collective-permute-done.2.refs_6_ = f32[64,1536]{1,0:T(8,128)S(1)} collective-permute-done((f32[64,1536]{1,0:T(8,128)S(1)}, f32[64,1536]{1,0:T(8,128)S(1)}, u32[]{:S(2)}, u32[]{:S(2)}) %collective-permute-start.2) | collective-permute-done | bytes 393248 | tf_op jit(solution)/shard_map/ppermute | solution.py:343
  47.2 1.9 %shard_map.70 = (f32[1040,128]{1,0:T(8,128)S(1)}, f32[64,1536]{1,0:T(8,128)S(1)}) custom-call(s32[3]{0:T(128)S(1)} %add_convert_fusion.flag_ref.refs_0_, f32[128,128]{1,0:T(8,128)S(1)} %get-tuple-element.51.refs_1_, bf16[4,4,512,512]{3,2,1,0:T(8,128)(2,1)S(1)} %get-tuple-element.52.refs_2_, bf16[4,4,512,512]{3,2,1,0:T(8,128)(2,1)S(1)} %get-tuple-element.53.refs_3_, ...), custom_call_target="tpu_custom_call" | custom-call | flops 603979776 | bytes 524288 | tf_op jit(solution)/shard_map/pallas_call | solution.py:226
  49.1 1.9 %collective-permute-start.3 = (f32[1040,128]{1,0:T(8,128)S(1)}, f32[1040,128]{1,0:T(8,128)S(1)}, u32[]{:S(2)}, u32[]{:S(2)}) collective-permute-start(f32[1040,128]{1,0:T(8,128)S(1)} %get-tuple-element.60), channel_id=1, source_target_pairs={{0,4},{4,8},{8,12},{12,16},{16,20},{20,24},{24,28},{1,5},{5,9},{9,... | collective-permute-start | bytes 1597448 | tf_op jit(solution)/shard_map/ppermute | solution.py:368
  51.0 2.6 %shard_map.80 = (f32[64,2048]{1,0:T(8,128)S(1)}, f32[16,64]{1,0:T(8,128)S(1)}) custom-call(s32[3]{0:T(128)S(1)} %add_convert_fusion.flag_ref.refs_0_, f32[128,128]{1,0:T(8,128)S(1)} %get-tuple-element.51.refs_1_, bf16[4,4,512,512]{3,2,1,0:T(8,128)(2,1)S(1)} %get-tuple-element.52.refs_2_, bf16[4,4,512,512]{3,2,1,0:T(8,128)(2,1)S(1)} %get-tuple-element.53.refs_3_, ...), custom_call_target="tpu_custom_call" | custom-call | flops 1006632960 | bytes 524288 | tf_op jit(solution)/shard_map/pallas_call | solution.py:226
  53.7 1.9 %shard_map.81 = (f32[1040,128]{1,0:T(8,128)S(1)}, f32[64,1536]{1,0:T(8,128)S(1)}) custom-call(s32[3]{0:T(128)S(1)} %add_convert_fusion.flag_ref.refs_0_, f32[128,128]{1,0:T(8,128)S(1)} %get-tuple-element.51.refs_1_, bf16[4,4,512,512]{3,2,1,0:T(8,128)(2,1)S(1)} %get-tuple-element.52.refs_2_, bf16[4,4,512,512]{3,2,1,0:T(8,128)(2,1)S(1)} %get-tuple-element.53.refs_3_, ...), custom_call_target="tpu_custom_call" | custom-call | flops 603979776 | bytes 524288 | tf_op jit(solution)/shard_map/pallas_call | solution.py:226
  55.6 3.6 %collective-permute-start.14 = (f32[1040,128]{1,0:T(8,128)S(1)}, f32[1040,128]{1,0:T(8,128)S(1)}, u32[]{:S(2)}, u32[]{:S(2)}) collective-permute-start(f32[1040,128]{1,0:T(8,128)S(1)} %get-tuple-element.81), channel_id=1, source_target_pairs={{0,4},{4,8},{8,12},{12,16},{16,20},{20,24},{24,28},{1,5},{5,9},{9,... | collective-permute-start | bytes 1597448 | tf_op jit(solution)/shard_map/ppermute | solution.py:368
  59.2 1.3 collective-permute-start.4
  60.5 1.5 collective-permute-start.15
  62.0 2.6 %shard_map.71 = (f32[64,2048]{1,0:T(8,128)S(1)}, f32[16,64]{1,0:T(8,128)S(1)}) custom-call(s32[3]{0:T(128)S(1)} %add_convert_fusion.flag_ref.refs_0_, f32[128,128]{1,0:T(8,128)S(1)} %get-tuple-element.51.refs_1_, bf16[4,4,512,512]{3,2,1,0:T(8,128)(2,1)S(1)} %get-tuple-element.52.refs_2_, bf16[4,4,512,512]{3,2,1,0:T(8,128)(2,1)S(1)} %get-tuple-element.53.refs_3_, ...), custom_call_target="tpu_custom_call" | custom-call | flops 1006632960 | bytes 524288 | tf_op jit(solution)/shard_map/pallas_call | solution.py:226
  64.6 12.1 %collective-permute-done.4.refs_6_ = f32[64,1536]{1,0:T(8,128)S(1)} collective-permute-done((f32[64,1536]{1,0:T(8,128)S(1)}, f32[64,1536]{1,0:T(8,128)S(1)}, u32[]{:S(2)}, u32[]{:S(2)}) %collective-permute-start.4) | collective-permute-done | bytes 393248 | tf_op jit(solution)/shard_map/ppermute | solution.py:343
  76.8 1.9 %shard_map.72 = (f32[1040,128]{1,0:T(8,128)S(1)}, f32[64,1536]{1,0:T(8,128)S(1)}) custom-call(s32[3]{0:T(128)S(1)} %add_convert_fusion.flag_ref.refs_0_, f32[128,128]{1,0:T(8,128)S(1)} %get-tuple-element.51.refs_1_, bf16[4,4,512,512]{3,2,1,0:T(8,128)(2,1)S(1)} %get-tuple-element.52.refs_2_, bf16[4,4,512,512]{3,2,1,0:T(8,128)(2,1)S(1)} %get-tuple-element.53.refs_3_, ...), custom_call_target="tpu_custom_call" | custom-call | flops 603979776 | bytes 524288 | tf_op jit(solution)/shard_map/pallas_call | solution.py:226
  78.7 1.9 %collective-permute-start.5 = (f32[1040,128]{1,0:T(8,128)S(1)}, f32[1040,128]{1,0:T(8,128)S(1)}, u32[]{:S(2)}, u32[]{:S(2)}) collective-permute-start(f32[1040,128]{1,0:T(8,128)S(1)} %get-tuple-element.64), channel_id=1, source_target_pairs={{0,4},{4,8},{8,12},{12,16},{16,20},{20,24},{24,28},{1,5},{5,9},{9,... | collective-permute-start | bytes 1597448 | tf_op jit(solution)/shard_map/ppermute | solution.py:368
  80.6 2.6 %shard_map.82 = (f32[64,2048]{1,0:T(8,128)S(1)}, f32[16,64]{1,0:T(8,128)S(1)}) custom-call(s32[3]{0:T(128)S(1)} %add_convert_fusion.flag_ref.refs_0_, f32[128,128]{1,0:T(8,128)S(1)} %get-tuple-element.51.refs_1_, bf16[4,4,512,512]{3,2,1,0:T(8,128)(2,1)S(1)} %get-tuple-element.52.refs_2_, bf16[4,4,512,512]{3,2,1,0:T(8,128)(2,1)S(1)} %get-tuple-element.53.refs_3_, ...), custom_call_target="tpu_custom_call" | custom-call | flops 1006632960 | bytes 524288 | tf_op jit(solution)/shard_map/pallas_call | solution.py:226
  83.2 1.9 %shard_map.83 = (f32[1040,128]{1,0:T(8,128)S(1)}, f32[64,1536]{1,0:T(8,128)S(1)}) custom-call(s32[3]{0:T(128)S(1)} %add_convert_fusion.flag_ref.refs_0_, f32[128,128]{1,0:T(8,128)S(1)} %get-tuple-element.51.refs_1_, bf16[4,4,512,512]{3,2,1,0:T(8,128)(2,1)S(1)} %get-tuple-element.52.refs_2_, bf16[4,4,512,512]{3,2,1,0:T(8,128)(2,1)S(1)} %get-tuple-element.53.refs_3_, ...), custom_call_target="tpu_custom_call" | custom-call | flops 603979776 | bytes 524288 | tf_op jit(solution)/shard_map/pallas_call | solution.py:226
  85.2 1.9 %collective-permute-start.16 = (f32[1040,128]{1,0:T(8,128)S(1)}, f32[1040,128]{1,0:T(8,128)S(1)}, u32[]{:S(2)}, u32[]{:S(2)}) collective-permute-start(f32[1040,128]{1,0:T(8,128)S(1)} %get-tuple-element.85), channel_id=1, source_target_pairs={{0,4},{4,8},{8,12},{12,16},{16,20},{20,24},{24,28},{1,5},{5,9},{9,... | collective-permute-start | bytes 1597448 | tf_op jit(solution)/shard_map/ppermute | solution.py:368
  87.1 1.3 collective-permute-start.6
  88.4 1.3 collective-permute-start.17
  89.7 2.6 %shard_map.73 = (f32[64,2048]{1,0:T(8,128)S(1)}, f32[16,64]{1,0:T(8,128)S(1)}) custom-call(s32[3]{0:T(128)S(1)} %add_convert_fusion.flag_ref.refs_0_, f32[128,128]{1,0:T(8,128)S(1)} %get-tuple-element.51.refs_1_, bf16[4,4,512,512]{3,2,1,0:T(8,128)(2,1)S(1)} %get-tuple-element.52.refs_2_, bf16[4,4,512,512]{3,2,1,0:T(8,128)(2,1)S(1)} %get-tuple-element.53.refs_3_, ...), custom_call_target="tpu_custom_call" | custom-call | flops 1006632960 | bytes 524288 | tf_op jit(solution)/shard_map/pallas_call | solution.py:226
  92.3 14.8 %collective-permute-done.6.refs_6_ = f32[64,1536]{1,0:T(8,128)S(1)} collective-permute-done((f32[64,1536]{1,0:T(8,128)S(1)}, f32[64,1536]{1,0:T(8,128)S(1)}, u32[]{:S(2)}, u32[]{:S(2)}) %collective-permute-start.6) | collective-permute-done | bytes 393248 | tf_op jit(solution)/shard_map/ppermute | solution.py:343
  107.1 1.9 %shard_map.74 = (f32[1040,128]{1,0:T(8,128)S(1)}, f32[64,1536]{1,0:T(8,128)S(1)}) custom-call(s32[3]{0:T(128)S(1)} %add_convert_fusion.flag_ref.refs_0_, f32[128,128]{1,0:T(8,128)S(1)} %get-tuple-element.51.refs_1_, bf16[4,4,512,512]{3,2,1,0:T(8,128)(2,1)S(1)} %get-tuple-element.52.refs_2_, bf16[4,4,512,512]{3,2,1,0:T(8,128)(2,1)S(1)} %get-tuple-element.53.refs_3_, ...), custom_call_target="tpu_custom_call" | custom-call | flops 603979776 | bytes 524288 | tf_op jit(solution)/shard_map/pallas_call | solution.py:226
  109.0 1.9 %collective-permute-start.7 = (f32[1040,128]{1,0:T(8,128)S(1)}, f32[1040,128]{1,0:T(8,128)S(1)}, u32[]{:S(2)}, u32[]{:S(2)}) collective-permute-start(f32[1040,128]{1,0:T(8,128)S(1)} %get-tuple-element.68), channel_id=1, source_target_pairs={{0,4},{4,8},{8,12},{12,16},{16,20},{20,24},{24,28},{1,5},{5,9},{9,... | collective-permute-start | bytes 1597448 | tf_op jit(solution)/shard_map/ppermute | solution.py:368
  111.0 2.6 %shard_map.84 = (f32[64,2048]{1,0:T(8,128)S(1)}, f32[16,64]{1,0:T(8,128)S(1)}) custom-call(s32[3]{0:T(128)S(1)} %add_convert_fusion.flag_ref.refs_0_, f32[128,128]{1,0:T(8,128)S(1)} %get-tuple-element.51.refs_1_, bf16[4,4,512,512]{3,2,1,0:T(8,128)(2,1)S(1)} %get-tuple-element.52.refs_2_, bf16[4,4,512,512]{3,2,1,0:T(8,128)(2,1)S(1)} %get-tuple-element.53.refs_3_, ...), custom_call_target="tpu_custom_call" | custom-call | flops 1006632960 | bytes 524288 | tf_op jit(solution)/shard_map/pallas_call | solution.py:226
  113.6 1.9 %shard_map.85 = (f32[1040,128]{1,0:T(8,128)S(1)}, f32[64,1536]{1,0:T(8,128)S(1)}) custom-call(s32[3]{0:T(128)S(1)} %add_convert_fusion.flag_ref.refs_0_, f32[128,128]{1,0:T(8,128)S(1)} %get-tuple-element.51.refs_1_, bf16[4,4,512,512]{3,2,1,0:T(8,128)(2,1)S(1)} %get-tuple-element.52.refs_2_, bf16[4,4,512,512]{3,2,1,0:T(8,128)(2,1)S(1)} %get-tuple-element.53.refs_3_, ...), custom_call_target="tpu_custom_call" | custom-call | flops 603979776 | bytes 524288 | tf_op jit(solution)/shard_map/pallas_call | solution.py:226
  115.5 1.9 %collective-permute-start.18 = (f32[1040,128]{1,0:T(8,128)S(1)}, f32[1040,128]{1,0:T(8,128)S(1)}, u32[]{:S(2)}, u32[]{:S(2)}) collective-permute-start(f32[1040,128]{1,0:T(8,128)S(1)} %get-tuple-element.89), channel_id=1, source_target_pairs={{0,4},{4,8},{8,12},{12,16},{16,20},{20,24},{24,28},{1,5},{5,9},{9,... | collective-permute-start | bytes 1597448 | tf_op jit(solution)/shard_map/ppermute | solution.py:368
  117.5 1.3 collective-permute-start.8
  118.8 1.5 collective-permute-start.19
  120.3 2.6 %shard_map.75 = (f32[64,2048]{1,0:T(8,128)S(1)}, f32[16,64]{1,0:T(8,128)S(1)}) custom-call(s32[3]{0:T(128)S(1)} %add_convert_fusion.flag_ref.refs_0_, f32[128,128]{1,0:T(8,128)S(1)} %get-tuple-element.51.refs_1_, bf16[4,4,512,512]{3,2,1,0:T(8,128)(2,1)S(1)} %get-tuple-element.52.refs_2_, bf16[4,4,512,512]{3,2,1,0:T(8,128)(2,1)S(1)} %get-tuple-element.53.refs_3_, ...), custom_call_target="tpu_custom_call" | custom-call | flops 1006632960 | bytes 524288 | tf_op jit(solution)/shard_map/pallas_call | solution.py:226
  122.9 14.6 %collective-permute-done.8.refs_6_ = f32[64,1536]{1,0:T(8,128)S(1)} collective-permute-done((f32[64,1536]{1,0:T(8,128)S(1)}, f32[64,1536]{1,0:T(8,128)S(1)}, u32[]{:S(2)}, u32[]{:S(2)}) %collective-permute-start.8) | collective-permute-done | bytes 393248 | tf_op jit(solution)/shard_map/ppermute | solution.py:343
  137.5 1.9 %shard_map.76 = (f32[1040,128]{1,0:T(8,128)S(1)}, f32[64,1536]{1,0:T(8,128)S(1)}) custom-call(s32[3]{0:T(128)S(1)} %add_convert_fusion.flag_ref.refs_0_, f32[128,128]{1,0:T(8,128)S(1)} %get-tuple-element.51.refs_1_, bf16[4,4,512,512]{3,2,1,0:T(8,128)(2,1)S(1)} %get-tuple-element.52.refs_2_, bf16[4,4,512,512]{3,2,1,0:T(8,128)(2,1)S(1)} %get-tuple-element.53.refs_3_, ...), custom_call_target="tpu_custom_call" | custom-call | flops 603979776 | bytes 524288 | tf_op jit(solution)/shard_map/pallas_call | solution.py:226
  139.4 1.9 %collective-permute-start.9 = (f32[1040,128]{1,0:T(8,128)S(1)}, f32[1040,128]{1,0:T(8,128)S(1)}, u32[]{:S(2)}, u32[]{:S(2)}) collective-permute-start(f32[1040,128]{1,0:T(8,128)S(1)} %get-tuple-element.72), channel_id=1, source_target_pairs={{0,4},{4,8},{8,12},{12,16},{16,20},{20,24},{24,28},{1,5},{5,9},{9,... | collective-permute-start | bytes 1597448 | tf_op jit(solution)/shard_map/ppermute | solution.py:368
  141.3 2.6 %shard_map.86 = (f32[64,2048]{1,0:T(8,128)S(1)}, f32[16,64]{1,0:T(8,128)S(1)}) custom-call(s32[3]{0:T(128)S(1)} %add_convert_fusion.flag_ref.refs_0_, f32[128,128]{1,0:T(8,128)S(1)} %get-tuple-element.51.refs_1_, bf16[4,4,512,512]{3,2,1,0:T(8,128)(2,1)S(1)} %get-tuple-element.52.refs_2_, bf16[4,4,512,512]{3,2,1,0:T(8,128)(2,1)S(1)} %get-tuple-element.53.refs_3_, ...), custom_call_target="tpu_custom_call" | custom-call | flops 1006632960 | bytes 524288 | tf_op jit(solution)/shard_map/pallas_call | solution.py:226
  144.0 1.9 %shard_map.87 = (f32[1040,128]{1,0:T(8,128)S(1)}, f32[64,1536]{1,0:T(8,128)S(1)}) custom-call(s32[3]{0:T(128)S(1)} %add_convert_fusion.flag_ref.refs_0_, f32[128,128]{1,0:T(8,128)S(1)} %get-tuple-element.51.refs_1_, bf16[4,4,512,512]{3,2,1,0:T(8,128)(2,1)S(1)} %get-tuple-element.52.refs_2_, bf16[4,4,512,512]{3,2,1,0:T(8,128)(2,1)S(1)} %get-tuple-element.53.refs_3_, ...), custom_call_target="tpu_custom_call" | custom-call | flops 603979776 | bytes 524288 | tf_op jit(solution)/shard_map/pallas_call | solution.py:226
  145.9 1.9 %collective-permute-start.20 = (f32[1040,128]{1,0:T(8,128)S(1)}, f32[1040,128]{1,0:T(8,128)S(1)}, u32[]{:S(2)}, u32[]{:S(2)}) collective-permute-start(f32[1040,128]{1,0:T(8,128)S(1)} %get-tuple-element.93), channel_id=1, source_target_pairs={{0,4},{4,8},{8,12},{12,16},{16,20},{20,24},{24,28},{1,5},{5,9},{9,... | collective-permute-start | bytes 1597448 | tf_op jit(solution)/shard_map/ppermute | solution.py:368
  147.8 1.3 collective-permute-start.10
  150.4 2.6 %shard_map.77 = (f32[64,2048]{1,0:T(8,128)S(1)}, f32[16,64]{1,0:T(8,128)S(1)}) custom-call(s32[3]{0:T(128)S(1)} %add_convert_fusion.flag_ref.refs_0_, f32[128,128]{1,0:T(8,128)S(1)} %get-tuple-element.51.refs_1_, bf16[4,4,512,512]{3,2,1,0:T(8,128)(2,1)S(1)} %get-tuple-element.52.refs_2_, bf16[4,4,512,512]{3,2,1,0:T(8,128)(2,1)S(1)} %get-tuple-element.53.refs_3_, ...), custom_call_target="tpu_custom_call" | custom-call | flops 1006632960 | bytes 524288 | tf_op jit(solution)/shard_map/pallas_call | solution.py:226
  153.0 13.3 %collective-permute-done.10.refs_6_ = f32[64,1536]{1,0:T(8,128)S(1)} collective-permute-done((f32[64,1536]{1,0:T(8,128)S(1)}, f32[64,1536]{1,0:T(8,128)S(1)}, u32[]{:S(2)}, u32[]{:S(2)}) %collective-permute-start.10) | collective-permute-done | bytes 393248 | tf_op jit(solution)/shard_map/ppermute | solution.py:343
  166.3 1.9 %shard_map.78 = (f32[64,2048]{1,0:T(8,128)S(1)}, f32[16,128]{1,0:T(8,128)S(1)}) custom-call(s32[3]{0:T(128)S(1)} %add_convert_fusion.flag_ref.refs_0_, f32[128,128]{1,0:T(8,128)S(1)} %get-tuple-element.51.refs_1_, bf16[4,4,512,512]{3,2,1,0:T(8,128)(2,1)S(1)} %get-tuple-element.52.refs_2_, bf16[4,4,512,512]{3,2,1,0:T(8,128)(2,1)S(1)} %get-tuple-element.53.refs_3_, ...), custom_call_target="tpu_custom_call" | custom-call | flops 603979776 | bytes 524288 | tf_op jit(solution)/shard_map/pallas_call | solution.py:226
  168.2 2.6 %shard_map.88 = (f32[64,2048]{1,0:T(8,128)S(1)}, f32[16,64]{1,0:T(8,128)S(1)}) custom-call(s32[3]{0:T(128)S(1)} %add_convert_fusion.flag_ref.refs_0_, f32[128,128]{1,0:T(8,128)S(1)} %get-tuple-element.51.refs_1_, bf16[4,4,512,512]{3,2,1,0:T(8,128)(2,1)S(1)} %get-tuple-element.52.refs_2_, bf16[4,4,512,512]{3,2,1,0:T(8,128)(2,1)S(1)} %get-tuple-element.53.refs_3_, ...), custom_call_target="tpu_custom_call" | custom-call | flops 1006632960 | bytes 524288 | tf_op jit(solution)/shard_map/pallas_call | solution.py:226
  170.8 1.9 %shard_map.89 = (f32[64,2048]{1,0:T(8,128)S(1)}, f32[16,128]{1,0:T(8,128)S(1)}) custom-call(s32[3]{0:T(128)S(1)} %add_convert_fusion.flag_ref.refs_0_, f32[128,128]{1,0:T(8,128)S(1)} %get-tuple-element.51.refs_1_, bf16[4,4,512,512]{3,2,1,0:T(8,128)(2,1)S(1)} %get-tuple-element.52.refs_2_, bf16[4,4,512,512]{3,2,1,0:T(8,128)(2,1)S(1)} %get-tuple-element.53.refs_3_, ...), custom_call_target="tpu_custom_call" | custom-call | flops 603979776 | bytes 524288 | tf_op jit(solution)/shard_map/pallas_call | solution.py:226
  172.8 3.4 %collective-permute-start.23 = (f32[16,128]{1,0:T(8,128)S(1)}, f32[16,128]{1,0:T(8,128)S(1)}, u32[]{:S(2)}, u32[]{:S(2)}) collective-permute-start(f32[16,128]{1,0:T(8,128)S(1)} %get-tuple-element.99.refs_2_), channel_id=1, source_target_pairs={{0,2},{1,3},{2,0},{3,1},{4,6},{5,7},{6,4},{7,5},{8,10},{9,11},{10,... | collective-permute-start | bytes 24584 | tf_op jit(solution)/shard_map/ppermute | solution.py:310
  177.2 1.5 collective-permute-done.22.refs_3_
  (33 shorter events, 11.0 us)
Async XLA Ops:
  0.6 14.0 %slice-start = ((s8[5242880]{0:T(1024)(128)(4,1)}), s8[1048576]{0:T(1024)(128)(4,1)S(1)}, s32[]{:S(2)}) async-start(s8[5242880]{0:T(1024)(128)(4,1)} %bitcast.8), calls=%async_computation | async-start | bytes 2097152
  1.9 12.7 %collective-permute-start = (f32[64,1536]{1,0:T(8,128)S(1)}, f32[64,1536]{1,0:T(8,128)S(1)}, u32[]{:S(2)}, u32[]{:S(2)}) collective-permute-start(f32[64,1536]{1,0:T(8,128)S(1)} %get-tuple-element.101), channel_id=1, source_target_pairs={{1,0},{2,1},{3,2},{5,4},{6,5},{7,6},{9,8},{10,9},{11,10},{13,12},{... | collective-permute-start | bytes 1179656 | tf_op jit(solution)/shard_map/ppermute | solution.py:343
  3.2 19.9 %collective-permute-start.11 = (f32[64,1536]{1,0:T(8,128)S(1)}, f32[64,1536]{1,0:T(8,128)S(1)}, u32[]{:S(2)}, u32[]{:S(2)}) collective-permute-start(f32[64,1536]{1,0:T(8,128)S(1)} %get-tuple-element.100), channel_id=1, source_target_pairs={{1,0},{2,1},{3,2},{5,4},{6,5},{7,6},{9,8},{10,9},{11,10},{13,12},{... | collective-permute-start | bytes 1179656 | tf_op jit(solution)/shard_map/ppermute | solution.py:343
  4.6 10.1 %slice-start.1 = ((s8[5242880]{0:T(1024)(128)(4,1)}), s8[4194304]{0:T(1024)(128)(4,1)S(1)}, s32[]{:S(2)}) async-start(s8[5242880]{0:T(1024)(128)(4,1)} %bitcast.8), calls=%async_computation.1 | async-start | bytes 8388608
  16.6 15.7 %collective-permute-start.1 = (f32[1040,128]{1,0:T(8,128)S(1)}, f32[1040,128]{1,0:T(8,128)S(1)}, u32[]{:S(2)}, u32[]{:S(2)}) collective-permute-start(f32[1040,128]{1,0:T(8,128)S(1)} %get-tuple-element.56), channel_id=1, source_target_pairs={{0,4},{4,8},{8,12},{12,16},{16,20},{20,24},{24,28},{1,5},{5,9},{9,... | collective-permute-start | bytes 1597448 | tf_op jit(solution)/shard_map/ppermute | solution.py:368
  25.1 25.9 %collective-permute-start.12 = (f32[1040,128]{1,0:T(8,128)S(1)}, f32[1040,128]{1,0:T(8,128)S(1)}, u32[]{:S(2)}, u32[]{:S(2)}) collective-permute-start(f32[1040,128]{1,0:T(8,128)S(1)} %get-tuple-element.77), channel_id=1, source_target_pairs={{0,4},{4,8},{8,12},{12,16},{16,20},{20,24},{24,28},{1,5},{5,9},{9,... | collective-permute-start | bytes 1597448 | tf_op jit(solution)/shard_map/ppermute | solution.py:368
  29.7 17.5 %collective-permute-start.2 = (f32[64,1536]{1,0:T(8,128)S(1)}, f32[64,1536]{1,0:T(8,128)S(1)}, u32[]{:S(2)}, u32[]{:S(2)}) collective-permute-start(f32[64,1536]{1,0:T(8,128)S(1)} %get-tuple-element.59), channel_id=1, source_target_pairs={{1,4},{2,5},{3,6},{5,8},{6,9},{7,10},{9,12},{10,13},{11,14},{13,16... | collective-permute-start | bytes 1179656 | tf_op jit(solution)/shard_map/ppermute | solution.py:343
  31.0 22.7 %collective-permute-start.13 = (f32[64,1536]{1,0:T(8,128)S(1)}, f32[64,1536]{1,0:T(8,128)S(1)}, u32[]{:S(2)}, u32[]{:S(2)}) collective-permute-start(f32[64,1536]{1,0:T(8,128)S(1)} %get-tuple-element.80), channel_id=1, source_target_pairs={{1,4},{2,5},{3,6},{5,8},{6,9},{7,10},{9,12},{10,13},{11,14},{13,16... | collective-permute-start | bytes 1179656 | tf_op jit(solution)/shard_map/ppermute | solution.py:343
  49.1 12.9 %collective-permute-start.3 = (f32[1040,128]{1,0:T(8,128)S(1)}, f32[1040,128]{1,0:T(8,128)S(1)}, u32[]{:S(2)}, u32[]{:S(2)}) collective-permute-start(f32[1040,128]{1,0:T(8,128)S(1)} %get-tuple-element.60), channel_id=1, source_target_pairs={{0,4},{4,8},{8,12},{12,16},{16,20},{20,24},{24,28},{1,5},{5,9},{9,... | collective-permute-start | bytes 1597448 | tf_op jit(solution)/shard_map/ppermute | solution.py:368
  55.6 25.0 %collective-permute-start.14 = (f32[1040,128]{1,0:T(8,128)S(1)}, f32[1040,128]{1,0:T(8,128)S(1)}, u32[]{:S(2)}, u32[]{:S(2)}) collective-permute-start(f32[1040,128]{1,0:T(8,128)S(1)} %get-tuple-element.81), channel_id=1, source_target_pairs={{0,4},{4,8},{8,12},{12,16},{16,20},{20,24},{24,28},{1,5},{5,9},{9,... | collective-permute-start | bytes 1597448 | tf_op jit(solution)/shard_map/ppermute | solution.py:368
  59.2 17.6 %collective-permute-start.4 = (f32[64,1536]{1,0:T(8,128)S(1)}, f32[64,1536]{1,0:T(8,128)S(1)}, u32[]{:S(2)}, u32[]{:S(2)}) collective-permute-start(f32[64,1536]{1,0:T(8,128)S(1)} %get-tuple-element.63), channel_id=1, source_target_pairs={{1,4},{2,5},{3,6},{5,8},{6,9},{7,10},{9,12},{10,13},{11,14},{13,16... | collective-permute-start | bytes 1179656 | tf_op jit(solution)/shard_map/ppermute | solution.py:343
  60.5 22.8 %collective-permute-start.15 = (f32[64,1536]{1,0:T(8,128)S(1)}, f32[64,1536]{1,0:T(8,128)S(1)}, u32[]{:S(2)}, u32[]{:S(2)}) collective-permute-start(f32[64,1536]{1,0:T(8,128)S(1)} %get-tuple-element.84), channel_id=1, source_target_pairs={{1,4},{2,5},{3,6},{5,8},{6,9},{7,10},{9,12},{10,13},{11,14},{13,16... | collective-permute-start | bytes 1179656 | tf_op jit(solution)/shard_map/ppermute | solution.py:343
  78.7 11.0 %collective-permute-start.5 = (f32[1040,128]{1,0:T(8,128)S(1)}, f32[1040,128]{1,0:T(8,128)S(1)}, u32[]{:S(2)}, u32[]{:S(2)}) collective-permute-start(f32[1040,128]{1,0:T(8,128)S(1)} %get-tuple-element.64), channel_id=1, source_target_pairs={{0,4},{4,8},{8,12},{12,16},{16,20},{20,24},{24,28},{1,5},{5,9},{9,... | collective-permute-start | bytes 1597448 | tf_op jit(solution)/shard_map/ppermute | solution.py:368
  85.2 25.8 %collective-permute-start.16 = (f32[1040,128]{1,0:T(8,128)S(1)}, f32[1040,128]{1,0:T(8,128)S(1)}, u32[]{:S(2)}, u32[]{:S(2)}) collective-permute-start(f32[1040,128]{1,0:T(8,128)S(1)} %get-tuple-element.85), channel_id=1, source_target_pairs={{0,4},{4,8},{8,12},{12,16},{16,20},{20,24},{24,28},{1,5},{5,9},{9,... | collective-permute-start | bytes 1597448 | tf_op jit(solution)/shard_map/ppermute | solution.py:368
  87.1 20.0 %collective-permute-start.6 = (f32[64,1536]{1,0:T(8,128)S(1)}, f32[64,1536]{1,0:T(8,128)S(1)}, u32[]{:S(2)}, u32[]{:S(2)}) collective-permute-start(f32[64,1536]{1,0:T(8,128)S(1)} %get-tuple-element.67), channel_id=1, source_target_pairs={{1,4},{2,5},{3,6},{5,8},{6,9},{7,10},{9,12},{10,13},{11,14},{13,16... | collective-permute-start | bytes 1179656 | tf_op jit(solution)/shard_map/ppermute | solution.py:343
  88.4 25.2 %collective-permute-start.17 = (f32[64,1536]{1,0:T(8,128)S(1)}, f32[64,1536]{1,0:T(8,128)S(1)}, u32[]{:S(2)}, u32[]{:S(2)}) collective-permute-start(f32[64,1536]{1,0:T(8,128)S(1)} %get-tuple-element.88), channel_id=1, source_target_pairs={{1,4},{2,5},{3,6},{5,8},{6,9},{7,10},{9,12},{10,13},{11,14},{13,16... | collective-permute-start | bytes 1179656 | tf_op jit(solution)/shard_map/ppermute | solution.py:343
  109.0 11.2 %collective-permute-start.7 = (f32[1040,128]{1,0:T(8,128)S(1)}, f32[1040,128]{1,0:T(8,128)S(1)}, u32[]{:S(2)}, u32[]{:S(2)}) collective-permute-start(f32[1040,128]{1,0:T(8,128)S(1)} %get-tuple-element.68), channel_id=1, source_target_pairs={{0,4},{4,8},{8,12},{12,16},{16,20},{20,24},{24,28},{1,5},{5,9},{9,... | collective-permute-start | bytes 1597448 | tf_op jit(solution)/shard_map/ppermute | solution.py:368
  115.5 25.8 %collective-permute-start.18 = (f32[1040,128]{1,0:T(8,128)S(1)}, f32[1040,128]{1,0:T(8,128)S(1)}, u32[]{:S(2)}, u32[]{:S(2)}) collective-permute-start(f32[1040,128]{1,0:T(8,128)S(1)} %get-tuple-element.89), channel_id=1, source_target_pairs={{0,4},{4,8},{8,12},{12,16},{16,20},{20,24},{24,28},{1,5},{5,9},{9,... | collective-permute-start | bytes 1597448 | tf_op jit(solution)/shard_map/ppermute | solution.py:368
  117.5 20.1 %collective-permute-start.8 = (f32[64,1536]{1,0:T(8,128)S(1)}, f32[64,1536]{1,0:T(8,128)S(1)}, u32[]{:S(2)}, u32[]{:S(2)}) collective-permute-start(f32[64,1536]{1,0:T(8,128)S(1)} %get-tuple-element.71), channel_id=1, source_target_pairs={{1,4},{2,5},{3,6},{5,8},{6,9},{7,10},{9,12},{10,13},{11,14},{13,16... | collective-permute-start | bytes 1179656 | tf_op jit(solution)/shard_map/ppermute | solution.py:343
  118.8 25.2 %collective-permute-start.19 = (f32[64,1536]{1,0:T(8,128)S(1)}, f32[64,1536]{1,0:T(8,128)S(1)}, u32[]{:S(2)}, u32[]{:S(2)}) collective-permute-start(f32[64,1536]{1,0:T(8,128)S(1)} %get-tuple-element.92), channel_id=1, source_target_pairs={{1,4},{2,5},{3,6},{5,8},{6,9},{7,10},{9,12},{10,13},{11,14},{13,16... | collective-permute-start | bytes 1179656 | tf_op jit(solution)/shard_map/ppermute | solution.py:343
  139.4 11.0 %collective-permute-start.9 = (f32[1040,128]{1,0:T(8,128)S(1)}, f32[1040,128]{1,0:T(8,128)S(1)}, u32[]{:S(2)}, u32[]{:S(2)}) collective-permute-start(f32[1040,128]{1,0:T(8,128)S(1)} %get-tuple-element.72), channel_id=1, source_target_pairs={{0,4},{4,8},{8,12},{12,16},{16,20},{20,24},{24,28},{1,5},{5,9},{9,... | collective-permute-start | bytes 1597448 | tf_op jit(solution)/shard_map/ppermute | solution.py:368
  145.9 22.3 %collective-permute-start.20 = (f32[1040,128]{1,0:T(8,128)S(1)}, f32[1040,128]{1,0:T(8,128)S(1)}, u32[]{:S(2)}, u32[]{:S(2)}) collective-permute-start(f32[1040,128]{1,0:T(8,128)S(1)} %get-tuple-element.93), channel_id=1, source_target_pairs={{0,4},{4,8},{8,12},{12,16},{16,20},{20,24},{24,28},{1,5},{5,9},{9,... | collective-permute-start | bytes 1597448 | tf_op jit(solution)/shard_map/ppermute | solution.py:368
  147.8 18.5 %collective-permute-start.10 = (f32[64,1536]{1,0:T(8,128)S(1)}, f32[64,1536]{1,0:T(8,128)S(1)}, u32[]{:S(2)}, u32[]{:S(2)}) collective-permute-start(f32[64,1536]{1,0:T(8,128)S(1)} %get-tuple-element.75), channel_id=1, source_target_pairs={{1,4},{2,5},{3,6},{5,8},{6,9},{7,10},{9,12},{10,13},{11,14},{13,16... | collective-permute-start | bytes 1179656 | tf_op jit(solution)/shard_map/ppermute | solution.py:343
  149.1 21.7 %collective-permute-start.21 = (f32[64,1536]{1,0:T(8,128)S(1)}, f32[64,1536]{1,0:T(8,128)S(1)}, u32[]{:S(2)}, u32[]{:S(2)}) collective-permute-start(f32[64,1536]{1,0:T(8,128)S(1)} %get-tuple-element.96), channel_id=1, source_target_pairs={{1,4},{2,5},{3,6},{5,8},{6,9},{7,10},{9,12},{10,13},{11,14},{13,16... | collective-permute-start | bytes 1179656 | tf_op jit(solution)/shard_map/ppermute | solution.py:343
  172.8 3.4 %collective-permute-start.24 = (f32[16,128]{1,0:T(8,128)S(1)}, f32[16,128]{1,0:T(8,128)S(1)}, u32[]{:S(2)}, u32[]{:S(2)}) collective-permute-start(f32[16,128]{1,0:T(8,128)S(1)} %get-tuple-element.99.refs_2_), channel_id=1, source_target_pairs={{0,3},{1,2},{2,1},{3,0},{4,7},{5,6},{6,5},{7,4},{8,11},{9,10},{10,... | collective-permute-start | bytes 24584 | tf_op jit(solution)/shard_map/ppermute | solution.py:310
  172.8 4.5 %collective-permute-start.23 = (f32[16,128]{1,0:T(8,128)S(1)}, f32[16,128]{1,0:T(8,128)S(1)}, u32[]{:S(2)}, u32[]{:S(2)}) collective-permute-start(f32[16,128]{1,0:T(8,128)S(1)} %get-tuple-element.99.refs_2_), channel_id=1, source_target_pairs={{0,2},{1,3},{2,0},{3,1},{4,6},{5,7},{6,4},{7,5},{8,10},{9,11},{10,... | collective-permute-start | bytes 24584 | tf_op jit(solution)/shard_map/ppermute | solution.py:310
  176.2 2.5 %collective-permute-start.22 = (f32[16,128]{1,0:T(8,128)S(1)}, f32[16,128]{1,0:T(8,128)S(1)}, u32[]{:S(2)}, u32[]{:S(2)}) collective-permute-start(f32[16,128]{1,0:T(8,128)S(1)} %get-tuple-element.99.refs_2_), channel_id=1, source_target_pairs={{0,1},{1,0},{2,3},{3,2},{4,5},{5,4},{6,7},{7,6},{8,9},{9,8},{10,11... | collective-permute-start | bytes 24584 | tf_op jit(solution)/shard_map/ppermute | solution.py:310

commit v4 on v3

--- a/solution.py
+++ b/solution.py
@@ -56,7 +56,38 @@
     return jnp.where(lane == index, column, 0.0).T[:depth]
 
 
-def open_kernel(dims, ticks, flag_ref, w_ref, rows_ref, outcome_ref, prior_ref, *rest):
+def edge_kernel(rows_ref, *rest):
+    *edge_refs, sems = rest
+    rows, cols = edge_refs[0].shape
+    copies = [
+        pltpu.make_async_copy(
+            rows_ref.at[0, pl.ds(c * rows, rows), pl.ds(0, cols)], ref, sems.at[c]
+        )
+        for c, ref in enumerate(edge_refs)
+    ]
+    for copy in copies:
+        copy.start()
+    for copy in copies:
+        copy.wait()
+
+
+def first_edges(in_flight, rows, cols):
+    count = in_flight.shape[1] // rows
+    return pl.pallas_call(
+        edge_kernel,
+        in_specs=[pl.BlockSpec(memory_space=pltpu.HBM)],
+        out_specs=[VMEM_SPEC] * count,
+        out_shape=[pltpu.VMEM((rows, cols), F32)] * count,
+        scratch_shapes=[pltpu.SemaphoreType.DMA((count,))],
+        compiler_params=pltpu.CompilerParams(vmem_limit_bytes=1 << 20),
+        name="first_edges",
+        cost_estimate=pl.CostEstimate(
+            flops=0, bytes_accessed=8 * count * rows * cols, transcendentals=0
+        ),
+    )(pltpu.with_memory_space_constraint(in_flight, pltpu.HBM))
+
+
+def open_kernel(dims, ticks, w_ref, rows_ref, outcome_ref, prior_ref, *rest):
     hi_ref, lo_ref, out_ref, sums_ref, choice_ref, *rest = rest
     stack, buffer, row_buffer, outcome_buffer, prior_buffer, sems = rest
     n_out, local, width, _, _ = dims
@@ -72,9 +103,7 @@
         pltpu.make_async_copy(rows_ref, row_buffer, sems.at[depth + 1]),
         pltpu.make_async_copy(prior_ref, prior_buffer, sems.at[depth + 2]),
     ]
-    for copy in inputs:
-        copy.start()
-    for copy in copies[:depth]:
+    for copy in inputs + copies[:depth]:
         copy.start()
     for copy in inputs:
         copy.wait()
@@ -103,19 +132,18 @@
             out_ref[:, s * width : (s + 1) * width] = selected
     depth = sums_ref.shape[0]
     row = lax.broadcasted_iota(jnp.int32, (depth, rows), 0)
-    prior = jnp.where(flag_ref[2] == 1, jnp.broadcast_to(prior_buffer[...], (depth, rows)), 0.0)
+    prior = jnp.where(lax.axis_index("sector") == 0, jnp.broadcast_to(prior_buffer[...], (depth, rows)), 0.0)
     sums_ref[...] = as_row(1, total, depth) + jnp.where(row == 2 * ticks, prior, 0.0)
 
 
-def opened(dims, ticks, flags, weights, in_flight, outcomes, prior):
+def opened(dims, ticks, weights, in_flight, outcomes, prior):
     n_out, local, width, _, _ = dims
     rows = in_flight.shape[1]
     depth = min(BUFFERS, n_out * local)
     operands = [weights, in_flight, outcomes, prior]
     return pl.pallas_call(
         functools.partial(open_kernel, dims, ticks),
-        in_specs=[pl.BlockSpec(memory_space=pltpu.SMEM)]
-        + [pl.BlockSpec(memory_space=pltpu.HBM)] * len(operands),
+        in_specs=[pl.BlockSpec(memory_space=pltpu.HBM)] * len(operands),
         out_specs=[VMEM_SPEC] * 5,
         out_shape=[
             pltpu.VMEM(weights.shape, BF),
@@ -139,14 +167,14 @@
             bytes_accessed=4 * weights.size,
             transcendentals=0,
         ),
-    )(flags, *[pltpu.with_memory_space_constraint(value, pltpu.HBM) for value in operands])
+    )(*[pltpu.with_memory_space_constraint(value, pltpu.HBM) for value in operands])
 
 
 def near_kernel(dims, tick, chunk, *refs):
-    flag_ref, choice_ref, hi_ref, lo_ref, main_ref, entering_ref, out_ref, sums_ref, stack = refs
+    choice_ref, hi_ref, lo_ref, main_ref, entering_ref, out_ref, sums_ref, stack = refs
     n_out, local, width, rows, _ = dims
     own = slice(chunk * rows, (chunk + 1) * rows)
-    at_start = flag_ref[0] == 1
+    at_start = lax.axis_index("site") == 0
     group = 0
     for q in range(local):
         for start in range(0, width, LANES):
@@ -173,9 +201,9 @@
     n_out, local, width, rows, halo = dims
     last = tick == ticks - 1
     refs = list(refs)
-    flag_ref, choice_ref, hi_ref, lo_ref, base_ref, base_sums_ref = refs[:6]
-    halo_refs = refs[6 : 6 + len(halo)]
-    other_refs, stack = refs[6 + len(halo) : -1], refs[-1]
+    choice_ref, hi_ref, lo_ref, base_ref, base_sums_ref = refs[:5]
+    halo_refs = refs[5 : 5 + len(halo)]
+    other_refs, stack = refs[5 + len(halo) : -1], refs[-1]
     own = slice(chunk * rows, (chunk + 1) * rows)
     base = slice(None) if base_ref.shape[0] == rows else own
     index = local
@@ -188,7 +216,7 @@
         *done_refs, out_ref, part_ref = other_refs
     else:
         entering_ref, out_ref, edge_ref = other_refs
-    at_end = flag_ref[1] == 1
+    at_end = lax.axis_index("site") == lax.axis_size("site") - 1
     choice = choice_ref[own, tick : tick + 1]
     total = jnp.zeros((rows, LANES), F32)
     picked = jnp.zeros((rows, LANES), F32)
@@ -222,10 +250,9 @@
 
 def step(kernel, dims, blocks, count, outs, operands):
     _, local, width, rows, _ = dims
-    flags, *values = operands
     return pl.pallas_call(
         kernel,
-        in_specs=[pl.BlockSpec(memory_space=pltpu.SMEM)] + [VMEM_SPEC] * len(values),
+        in_specs=[VMEM_SPEC] * len(operands),
         out_specs=[VMEM_SPEC] * len(outs),
         out_shape=[pltpu.VMEM(shape, F32) for shape in outs],
         scratch_shapes=[pltpu.VMEM((blocks, 2 * rows, width), BF)],
@@ -235,7 +262,7 @@
             bytes_accessed=4 * rows * local * width,
             transcendentals=0,
         ),
-    )(flags, *[in_vmem(value) for value in values])
+    )(*[in_vmem(value) for value in operands])
 
 
 def near(dims, tick, ticks, chunk, shared, main, entering):
@@ -343,17 +370,12 @@
             pieces.append(lax.ppermute(edge[:, : blocks * width], ("site", "sector"), pairs))
         return pieces
 
-    site = lax.axis_index("site")
-    flags = [site == 0, site == sites - 1, lax.axis_index("sector") == 0]
-    flags = jnp.stack(flags).astype(jnp.int32)
-    halos = [
-        moved(in_flight[0, c * rows : (c + 1) * rows, : halo[0] * width], 0)
-        for c in range(CHUNKS)
-    ]
+    edges = first_edges(in_flight, rows, halo[0] * width)
+    halos = [moved(edges[c], 0) for c in range(CHUNKS)]
     hi, lo, base, base_sums, choice = opened(
-        dims, ticks, flags, weights, in_flight, outcomes, prior_logp
+        dims, ticks, weights, in_flight, outcomes, prior_logp
     )
-    shared = [flags, choice, hi, lo]
+    shared = [choice, hi, lo]
     states = [(base, base_sums)] * CHUNKS
     mains = [None] * CHUNKS
     done = []
@@ -361,7 +383,9 @@
         for c in range(CHUNKS):
             if tick > 0:
                 states[c] = near(dims, tick, ticks, c, shared, mains[c], entering)
-            mains[c], other = far(dims, tick, ticks, c, shared, states[c], halos[c], entering, done)
+            mains[c], other = far(
+                dims, tick, ticks, c, shared, states[c], halos[c], entering, done
+            )
             if tick == ticks - 1:
                 done = [other]
                 continue

time: 181 us -> 173 us (0.956)
  Pallas kernels: 58.5 us -> 46.6 us
  waiting for transfers between devices: 72.6 us -> 77.6 us
    pallas_call x22 -> x23, Pallas kernels: 49.4 us -> 38.2 us  [the longest x22 37 us: step(): pl.pallas_call(kernel, in_specs=[VMEM_SPEC] * len(operands), out_specs=[V...]
    ppermute x12, waiting for transfers between devices: 70.1 us -> 75 us  [moved(): lax.ppermute(edge[:, :blocks * width], ('site', 'sector'), pairs)]
  transfers between devices with their start and end apart: 25 -> 25, of which waited for: 9 -> 10; matrix products, arithmetic and copies ran while one was open for 0% -> 0% of each run, Pallas kernels for 31% -> 25%
where the time goes in v4:
time: 173 us; the launch traced here: 172 us
  waiting for transfers between devices  77.6 us (45%)
  starting transfers between devices  46.7 us (27%)
  Pallas kernels  46.6 us (27%)
    ppermute x12, waiting for transfers between devices, moved(): lax.ppermute(edge[:, :blocks * width], ('site', 'sector'), pairs)  75 us
    pallas_call x22, Pallas kernels, step(): pl.pallas_call(kernel, in_specs=[VMEM_SPEC] * len(operands), out_specs=[V...  37 us
    ppermute x10, starting transfers between devices, per_device(): mains[c] = lax.ppermute(mains[c], 'site', up)  27.3 us
    ppermute x12, starting transfers between devices, moved(): lax.ppermute(edge[:, :blocks * width], ('site', 'sector'), pairs)  16 us
    pallas_call x1, Pallas kernels, opened(): pl.pallas_call(functools.partial(open_kernel, dims, ticks), in_specs=[pl....  7.13 us
  transfers between devices with their start and end apart: 25, of which 10 were waited for; matrix products, arithmetic and copies ran while one was open for 0% of the time, Pallas kernels for 25%

profile of v4, /device:TPU:1, one launch (start us, length us, event | category | flops | bytes accessed | tf_op | source)
XLA Modules:
  0.0 171.8 jit_solution(2065522392419423430)
XLA Ops:
  1.9 1.4 collective-permute-start
  3.4 1.3 collective-permute-start.11
  4.7 7.1 %opened.1 = (bf16[4,4,512,512]{3,2,1,0:T(8,128)(2,1)S(1)}, bf16[4,4,512,512]{3,2,1,0:T(8,128)(2,1)S(1)}, f32[128,2048]{1,0:T(8,128)S(1)}, f32[16,128]{1,0:T(8,128)S(1)}, f32[128,128]{1,0:T(8,128)S(1)}) custom-call(f32[4,4,512,512]{3,2,1,0:T(8,128)} %bitcast.3, f32[1,128,2048]{2,1,0:T(8,128)} %rows_ref.3, s32[6,1,128]{2,1,0:T(1,128)} %outcome_ref.1, ...), custom_call_target="tpu_custom_call" | custom-call | flops 1610612736 | bytes 16777216 | tf_op jit(solution)/shard_map/opened/pallas_call | solution.py:144
  11.8 3.0 %collective-permute-done.refs_5_ = f32[64,1536]{1,0:T(8,128)S(1)} collective-permute-done((f32[64,1536]{1,0:T(8,128)S(1)}, f32[64,1536]{1,0:T(8,128)S(1)}, u32[]{:S(2)}, u32[]{:S(2)}) %collective-permute-start) | collective-permute-done | bytes 393248 | tf_op jit(solution)/shard_map/ppermute | solution.py:370
  14.8 1.3 shard_map.68
  16.1 5.7 %collective-permute-start.1 = (f32[1040,128]{1,0:T(8,128)S(1)}, f32[1040,128]{1,0:T(8,128)S(1)}, u32[]{:S(2)}, u32[]{:S(2)}) collective-permute-start(f32[1040,128]{1,0:T(8,128)S(1)} %get-tuple-element.59), channel_id=1, source_target_pairs={{0,4},{4,8},{8,12},{12,16},{16,20},{20,24},{24,28},{1,5},{5,9},{9,... | collective-permute-start | bytes 1597448 | tf_op jit(solution)/shard_map/ppermute | solution.py:392
  21.9 1.4 collective-permute-done.11.refs_5_
  23.2 1.5 shard_map.79
  24.7 4.6 %collective-permute-start.12 = (f32[1040,128]{1,0:T(8,128)S(1)}, f32[1040,128]{1,0:T(8,128)S(1)}, u32[]{:S(2)}, u32[]{:S(2)}) collective-permute-start(f32[1040,128]{1,0:T(8,128)S(1)} %get-tuple-element.81), channel_id=1, source_target_pairs={{0,4},{4,8},{8,12},{12,16},{16,20},{20,24},{24,28},{1,5},{5,9},{9,... | collective-permute-start | bytes 1597448 | tf_op jit(solution)/shard_map/ppermute | solution.py:392
  29.3 1.3 collective-permute-start.2
  31.9 2.1 %shard_map.69 = (f32[64,2048]{1,0:T(8,128)S(1)}, f32[16,64]{1,0:T(8,128)S(1)}) custom-call(f32[128,128]{1,0:T(8,128)S(1)} %get-tuple-element.53.refs_0_, bf16[4,4,512,512]{3,2,1,0:T(8,128)(2,1)S(1)} %get-tuple-element.54.refs_1_, bf16[4,4,512,512]{3,2,1,0:T(8,128)(2,1)S(1)} %get-tuple-element.55.refs_2_, f32[1040,128]{1,0:T(8,128)S(1)} %collective-permute-done.1.refs_3_, ...), custom_call_target="tpu_custom_call" | custom-call | flops 1006632960 | bytes 524288 | tf_op jit(solution)/shard_map/pallas_call | solution.py:253
  34.0 12.8 %collective-permute-done.2.refs_5_ = f32[64,1536]{1,0:T(8,128)S(1)} collective-permute-done((f32[64,1536]{1,0:T(8,128)S(1)}, f32[64,1536]{1,0:T(8,128)S(1)}, u32[]{:S(2)}, u32[]{:S(2)}) %collective-permute-start.2) | collective-permute-done | bytes 393248 | tf_op jit(solution)/shard_map/ppermute | solution.py:370
  46.8 1.3 shard_map.70
  48.1 1.9 %collective-permute-start.3 = (f32[1040,128]{1,0:T(8,128)S(1)}, f32[1040,128]{1,0:T(8,128)S(1)}, u32[]{:S(2)}, u32[]{:S(2)}) collective-permute-start(f32[1040,128]{1,0:T(8,128)S(1)} %get-tuple-element.63), channel_id=1, source_target_pairs={{0,4},{4,8},{8,12},{12,16},{16,20},{20,24},{24,28},{1,5},{5,9},{9,... | collective-permute-start | bytes 1597448 | tf_op jit(solution)/shard_map/ppermute | solution.py:392
  50.1 2.1 %shard_map.80 = (f32[64,2048]{1,0:T(8,128)S(1)}, f32[16,64]{1,0:T(8,128)S(1)}) custom-call(f32[128,128]{1,0:T(8,128)S(1)} %get-tuple-element.53.refs_0_, bf16[4,4,512,512]{3,2,1,0:T(8,128)(2,1)S(1)} %get-tuple-element.54.refs_1_, bf16[4,4,512,512]{3,2,1,0:T(8,128)(2,1)S(1)} %get-tuple-element.55.refs_2_, f32[1040,128]{1,0:T(8,128)S(1)} %collective-permute-done.12.refs_3_, ...), custom_call_target="tpu_custom_call" | custom-call | flops 1006632960 | bytes 524288 | tf_op jit(solution)/shard_map/pallas_call | solution.py:253
  52.2 1.3 shard_map.81
  53.5 3.6 %collective-permute-start.14 = (f32[1040,128]{1,0:T(8,128)S(1)}, f32[1040,128]{1,0:T(8,128)S(1)}, u32[]{:S(2)}, u32[]{:S(2)}) collective-permute-start(f32[1040,128]{1,0:T(8,128)S(1)} %get-tuple-element.85), channel_id=1, source_target_pairs={{0,4},{4,8},{8,12},{12,16},{16,20},{20,24},{24,28},{1,5},{5,9},{9,... | collective-permute-start | bytes 1597448 | tf_op jit(solution)/shard_map/ppermute | solution.py:392
  58.4 1.5 collective-permute-start.15
  59.9 2.1 %shard_map.71 = (f32[64,2048]{1,0:T(8,128)S(1)}, f32[16,64]{1,0:T(8,128)S(1)}) custom-call(f32[128,128]{1,0:T(8,128)S(1)} %get-tuple-element.53.refs_0_, bf16[4,4,512,512]{3,2,1,0:T(8,128)(2,1)S(1)} %get-tuple-element.54.refs_1_, bf16[4,4,512,512]{3,2,1,0:T(8,128)(2,1)S(1)} %get-tuple-element.55.refs_2_, f32[1040,128]{1,0:T(8,128)S(1)} %collective-permute-done.3.refs_3_, ...), custom_call_target="tpu_custom_call" | custom-call | flops 1006632960 | bytes 524288 | tf_op jit(solution)/shard_map/pallas_call | solution.py:253
  62.0 12.7 %collective-permute-done.4.refs_5_ = f32[64,1536]{1,0:T(8,128)S(1)} collective-permute-done((f32[64,1536]{1,0:T(8,128)S(1)}, f32[64,1536]{1,0:T(8,128)S(1)}, u32[]{:S(2)}, u32[]{:S(2)}) %collective-permute-start.4) | collective-permute-done | bytes 393248 | tf_op jit(solution)/shard_map/ppermute | solution.py:370
  74.6 1.3 shard_map.72
  76.0 1.9 %collective-permute-start.5 = (f32[1040,128]{1,0:T(8,128)S(1)}, f32[1040,128]{1,0:T(8,128)S(1)}, u32[]{:S(2)}, u32[]{:S(2)}) collective-permute-start(f32[1040,128]{1,0:T(8,128)S(1)} %get-tuple-element.67), channel_id=1, source_target_pairs={{0,4},{4,8},{8,12},{12,16},{16,20},{20,24},{24,28},{1,5},{5,9},{9,... | collective-permute-start | bytes 1597448 | tf_op jit(solution)/shard_map/ppermute | solution.py:392
  77.9 2.1 %shard_map.82 = (f32[64,2048]{1,0:T(8,128)S(1)}, f32[16,64]{1,0:T(8,128)S(1)}) custom-call(f32[128,128]{1,0:T(8,128)S(1)} %get-tuple-element.53.refs_0_, bf16[4,4,512,512]{3,2,1,0:T(8,128)(2,1)S(1)} %get-tuple-element.54.refs_1_, bf16[4,4,512,512]{3,2,1,0:T(8,128)(2,1)S(1)} %get-tuple-element.55.refs_2_, f32[1040,128]{1,0:T(8,128)S(1)} %collective-permute-done.14.refs_3_, ...), custom_call_target="tpu_custom_call" | custom-call | flops 1006632960 | bytes 524288 | tf_op jit(solution)/shard_map/pallas_call | solution.py:253
  80.0 1.3 shard_map.83
  81.3 1.9 %collective-permute-start.16 = (f32[1040,128]{1,0:T(8,128)S(1)}, f32[1040,128]{1,0:T(8,128)S(1)}, u32[]{:S(2)}, u32[]{:S(2)}) collective-permute-start(f32[1040,128]{1,0:T(8,128)S(1)} %get-tuple-element.89), channel_id=1, source_target_pairs={{0,4},{4,8},{8,12},{12,16},{16,20},{20,24},{24,28},{1,5},{5,9},{9,... | collective-permute-start | bytes 1597448 | tf_op jit(solution)/shard_map/ppermute | solution.py:392
  85.8 2.1 %shard_map.73 = (f32[64,2048]{1,0:T(8,128)S(1)}, f32[16,64]{1,0:T(8,128)S(1)}) custom-call(f32[128,128]{1,0:T(8,128)S(1)} %get-tuple-element.53.refs_0_, bf16[4,4,512,512]{3,2,1,0:T(8,128)(2,1)S(1)} %get-tuple-element.54.refs_1_, bf16[4,4,512,512]{3,2,1,0:T(8,128)(2,1)S(1)} %get-tuple-element.55.refs_2_, f32[1040,128]{1,0:T(8,128)S(1)} %collective-permute-done.5.refs_3_, ...), custom_call_target="tpu_custom_call" | custom-call | flops 1006632960 | bytes 524288 | tf_op jit(solution)/shard_map/pallas_call | solution.py:253
  87.9 15.4 %collective-permute-done.6.refs_5_ = f32[64,1536]{1,0:T(8,128)S(1)} collective-permute-done((f32[64,1536]{1,0:T(8,128)S(1)}, f32[64,1536]{1,0:T(8,128)S(1)}, u32[]{:S(2)}, u32[]{:S(2)}) %collective-permute-start.6) | collective-permute-done | bytes 393248 | tf_op jit(solution)/shard_map/ppermute | solution.py:370
  103.3 1.3 shard_map.74
  104.6 1.9 %collective-permute-start.7 = (f32[1040,128]{1,0:T(8,128)S(1)}, f32[1040,128]{1,0:T(8,128)S(1)}, u32[]{:S(2)}, u32[]{:S(2)}) collective-permute-start(f32[1040,128]{1,0:T(8,128)S(1)} %get-tuple-element.71), channel_id=1, source_target_pairs={{0,4},{4,8},{8,12},{12,16},{16,20},{20,24},{24,28},{1,5},{5,9},{9,... | collective-permute-start | bytes 1597448 | tf_op jit(solution)/shard_map/ppermute | solution.py:392
  106.5 2.1 %shard_map.84 = (f32[64,2048]{1,0:T(8,128)S(1)}, f32[16,64]{1,0:T(8,128)S(1)}) custom-call(f32[128,128]{1,0:T(8,128)S(1)} %get-tuple-element.53.refs_0_, bf16[4,4,512,512]{3,2,1,0:T(8,128)(2,1)S(1)} %get-tuple-element.54.refs_1_, bf16[4,4,512,512]{3,2,1,0:T(8,128)(2,1)S(1)} %get-tuple-element.55.refs_2_, f32[1040,128]{1,0:T(8,128)S(1)} %collective-permute-done.16.refs_3_, ...), custom_call_target="tpu_custom_call" | custom-call | flops 1006632960 | bytes 524288 | tf_op jit(solution)/shard_map/pallas_call | solution.py:253
  108.6 1.3 shard_map.85
  110.0 1.9 %collective-permute-start.18 = (f32[1040,128]{1,0:T(8,128)S(1)}, f32[1040,128]{1,0:T(8,128)S(1)}, u32[]{:S(2)}, u32[]{:S(2)}) collective-permute-start(f32[1040,128]{1,0:T(8,128)S(1)} %get-tuple-element.93), channel_id=1, source_target_pairs={{0,4},{4,8},{8,12},{12,16},{16,20},{20,24},{24,28},{1,5},{5,9},{9,... | collective-permute-start | bytes 1597448 | tf_op jit(solution)/shard_map/ppermute | solution.py:392
  111.9 1.3 collective-permute-start.8
  113.2 1.5 collective-permute-start.19
  114.7 2.1 %shard_map.75 = (f32[64,2048]{1,0:T(8,128)S(1)}, f32[16,64]{1,0:T(8,128)S(1)}) custom-call(f32[128,128]{1,0:T(8,128)S(1)} %get-tuple-element.53.refs_0_, bf16[4,4,512,512]{3,2,1,0:T(8,128)(2,1)S(1)} %get-tuple-element.54.refs_1_, bf16[4,4,512,512]{3,2,1,0:T(8,128)(2,1)S(1)} %get-tuple-element.55.refs_2_, f32[1040,128]{1,0:T(8,128)S(1)} %collective-permute-done.7.refs_3_, ...), custom_call_target="tpu_custom_call" | custom-call | flops 1006632960 | bytes 524288 | tf_op jit(solution)/shard_map/pallas_call | solution.py:253
  116.8 15.2 %collective-permute-done.8.refs_5_ = f32[64,1536]{1,0:T(8,128)S(1)} collective-permute-done((f32[64,1536]{1,0:T(8,128)S(1)}, f32[64,1536]{1,0:T(8,128)S(1)}, u32[]{:S(2)}, u32[]{:S(2)}) %collective-permute-start.8) | collective-permute-done | bytes 393248 | tf_op jit(solution)/shard_map/ppermute | solution.py:370
  131.9 1.3 shard_map.76
  133.3 1.9 %collective-permute-start.9 = (f32[1040,128]{1,0:T(8,128)S(1)}, f32[1040,128]{1,0:T(8,128)S(1)}, u32[]{:S(2)}, u32[]{:S(2)}) collective-permute-start(f32[1040,128]{1,0:T(8,128)S(1)} %get-tuple-element.75), channel_id=1, source_target_pairs={{0,4},{4,8},{8,12},{12,16},{16,20},{20,24},{24,28},{1,5},{5,9},{9,... | collective-permute-start | bytes 1597448 | tf_op jit(solution)/shard_map/ppermute | solution.py:392
  135.2 2.1 %shard_map.86 = (f32[64,2048]{1,0:T(8,128)S(1)}, f32[16,64]{1,0:T(8,128)S(1)}) custom-call(f32[128,128]{1,0:T(8,128)S(1)} %get-tuple-element.53.refs_0_, bf16[4,4,512,512]{3,2,1,0:T(8,128)(2,1)S(1)} %get-tuple-element.54.refs_1_, bf16[4,4,512,512]{3,2,1,0:T(8,128)(2,1)S(1)} %get-tuple-element.55.refs_2_, f32[1040,128]{1,0:T(8,128)S(1)} %collective-permute-done.18.refs_3_, ...), custom_call_target="tpu_custom_call" | custom-call | flops 1006632960 | bytes 524288 | tf_op jit(solution)/shard_map/pallas_call | solution.py:253
  137.3 1.3 shard_map.87
  138.6 1.9 %collective-permute-start.20 = (f32[1040,128]{1,0:T(8,128)S(1)}, f32[1040,128]{1,0:T(8,128)S(1)}, u32[]{:S(2)}, u32[]{:S(2)}) collective-permute-start(f32[1040,128]{1,0:T(8,128)S(1)} %get-tuple-element.97), channel_id=1, source_target_pairs={{0,4},{4,8},{8,12},{12,16},{16,20},{20,24},{24,28},{1,5},{5,9},{9,... | collective-permute-start | bytes 1597448 | tf_op jit(solution)/shard_map/ppermute | solution.py:392
  143.2 2.1 %shard_map.77 = (f32[64,2048]{1,0:T(8,128)S(1)}, f32[16,64]{1,0:T(8,128)S(1)}) custom-call(f32[128,128]{1,0:T(8,128)S(1)} %get-tuple-element.53.refs_0_, bf16[4,4,512,512]{3,2,1,0:T(8,128)(2,1)S(1)} %get-tuple-element.54.refs_1_, bf16[4,4,512,512]{3,2,1,0:T(8,128)(2,1)S(1)} %get-tuple-element.55.refs_2_, f32[1040,128]{1,0:T(8,128)S(1)} %collective-permute-done.9.refs_3_, ...), custom_call_target="tpu_custom_call" | custom-call | flops 1006632960 | bytes 524288 | tf_op jit(solution)/shard_map/pallas_call | solution.py:253
  145.2 13.8 %collective-permute-done.10.refs_5_ = f32[64,1536]{1,0:T(8,128)S(1)} collective-permute-done((f32[64,1536]{1,0:T(8,128)S(1)}, f32[64,1536]{1,0:T(8,128)S(1)}, u32[]{:S(2)}, u32[]{:S(2)}) %collective-permute-start.10) | collective-permute-done | bytes 393248 | tf_op jit(solution)/shard_map/ppermute | solution.py:370
  159.1 1.3 shard_map.78
  160.4 2.1 %shard_map.88 = (f32[64,2048]{1,0:T(8,128)S(1)}, f32[16,64]{1,0:T(8,128)S(1)}) custom-call(f32[128,128]{1,0:T(8,128)S(1)} %get-tuple-element.53.refs_0_, bf16[4,4,512,512]{3,2,1,0:T(8,128)(2,1)S(1)} %get-tuple-element.54.refs_1_, bf16[4,4,512,512]{3,2,1,0:T(8,128)(2,1)S(1)} %get-tuple-element.55.refs_2_, f32[1040,128]{1,0:T(8,128)S(1)} %collective-permute-done.20.refs_3_, ...), custom_call_target="tpu_custom_call" | custom-call | flops 1006632960 | bytes 524288 | tf_op jit(solution)/shard_map/pallas_call | solution.py:253
  163.3 1.4 shard_map.89
  164.7 3.4 %collective-permute-start.23 = (f32[16,128]{1,0:T(8,128)S(1)}, f32[16,128]{1,0:T(8,128)S(1)}, u32[]{:S(2)}, u32[]{:S(2)}) collective-permute-start(f32[16,128]{1,0:T(8,128)S(1)} %get-tuple-element.103.refs_2_), channel_id=1, source_target_pairs={{0,2},{1,3},{2,0},{3,1},{4,6},{5,7},{6,4},{7,5},{8,10},{9,11},{10,... | collective-permute-start | bytes 24584 | tf_op jit(solution)/shard_map/ppermute | solution.py:337
  169.1 1.5 collective-permute-done.22.refs_3_
  (32 shorter events, 12.2 us)
Async XLA Ops:
  0.6 14.2 %slice-start = ((s8[5242880]{0:T(1024)(128)(4,1)}), s8[4194304]{0:T(1024)(128)(4,1)S(1)}, s32[]{:S(2)}) async-start(s8[5242880]{0:T(1024)(128)(4,1)} %bitcast.1), calls=%async_computation | async-start | bytes 8388608
  1.9 12.9 %collective-permute-start = (f32[64,1536]{1,0:T(8,128)S(1)}, f32[64,1536]{1,0:T(8,128)S(1)}, u32[]{:S(2)}, u32[]{:S(2)}) collective-permute-start(f32[64,1536]{1,0:T(8,128)S(1)} %get-tuple-element.58), channel_id=1, source_target_pairs={{1,0},{2,1},{3,2},{5,4},{6,5},{7,6},{9,8},{10,9},{11,10},{13,12},{... | collective-permute-start | bytes 1179656 | tf_op jit(solution)/shard_map/ppermute | solution.py:370
  3.4 19.9 %collective-permute-start.11 = (f32[64,1536]{1,0:T(8,128)S(1)}, f32[64,1536]{1,0:T(8,128)S(1)}, u32[]{:S(2)}, u32[]{:S(2)}) collective-permute-start(f32[64,1536]{1,0:T(8,128)S(1)} %get-tuple-element.80), channel_id=1, source_target_pairs={{1,0},{2,1},{3,2},{5,4},{6,5},{7,6},{9,8},{10,9},{11,10},{13,12},{... | collective-permute-start | bytes 1179656 | tf_op jit(solution)/shard_map/ppermute | solution.py:370
  4.7 10.2 %slice-start.1 = ((s8[5242880]{0:T(1024)(128)(4,1)}), s8[1048576]{0:T(1024)(128)(4,1)S(1)}, s32[]{:S(2)}) async-start(s8[5242880]{0:T(1024)(128)(4,1)} %bitcast.1), calls=%async_computation.1 | async-start | bytes 2097152
  16.1 15.7 %collective-permute-start.1 = (f32[1040,128]{1,0:T(8,128)S(1)}, f32[1040,128]{1,0:T(8,128)S(1)}, u32[]{:S(2)}, u32[]{:S(2)}) collective-permute-start(f32[1040,128]{1,0:T(8,128)S(1)} %get-tuple-element.59), channel_id=1, source_target_pairs={{0,4},{4,8},{8,12},{12,16},{16,20},{20,24},{24,28},{1,5},{5,9},{9,... | collective-permute-start | bytes 1597448 | tf_op jit(solution)/shard_map/ppermute | solution.py:392
  24.7 25.4 %collective-permute-start.12 = (f32[1040,128]{1,0:T(8,128)S(1)}, f32[1040,128]{1,0:T(8,128)S(1)}, u32[]{:S(2)}, u32[]{:S(2)}) collective-permute-start(f32[1040,128]{1,0:T(8,128)S(1)} %get-tuple-element.81), channel_id=1, source_target_pairs={{0,4},{4,8},{8,12},{12,16},{16,20},{20,24},{24,28},{1,5},{5,9},{9,... | collective-permute-start | bytes 1597448 | tf_op jit(solution)/shard_map/ppermute | solution.py:392
  29.3 17.5 %collective-permute-start.2 = (f32[64,1536]{1,0:T(8,128)S(1)}, f32[64,1536]{1,0:T(8,128)S(1)}, u32[]{:S(2)}, u32[]{:S(2)}) collective-permute-start(f32[64,1536]{1,0:T(8,128)S(1)} %get-tuple-element.62), channel_id=1, source_target_pairs={{1,4},{2,5},{3,6},{5,8},{6,9},{7,10},{9,12},{10,13},{11,14},{13,16... | collective-permute-start | bytes 1179656 | tf_op jit(solution)/shard_map/ppermute | solution.py:370
  30.6 21.6 %collective-permute-start.13 = (f32[64,1536]{1,0:T(8,128)S(1)}, f32[64,1536]{1,0:T(8,128)S(1)}, u32[]{:S(2)}, u32[]{:S(2)}) collective-permute-start(f32[64,1536]{1,0:T(8,128)S(1)} %get-tuple-element.84), channel_id=1, source_target_pairs={{1,4},{2,5},{3,6},{5,8},{6,9},{7,10},{9,12},{10,13},{11,14},{13,16... | collective-permute-start | bytes 1179656 | tf_op jit(solution)/shard_map/ppermute | solution.py:370
  48.1 11.7 %collective-permute-start.3 = (f32[1040,128]{1,0:T(8,128)S(1)}, f32[1040,128]{1,0:T(8,128)S(1)}, u32[]{:S(2)}, u32[]{:S(2)}) collective-permute-start(f32[1040,128]{1,0:T(8,128)S(1)} %get-tuple-element.63), channel_id=1, source_target_pairs={{0,4},{4,8},{8,12},{12,16},{16,20},{20,24},{24,28},{1,5},{5,9},{9,... | collective-permute-start | bytes 1597448 | tf_op jit(solution)/shard_map/ppermute | solution.py:392
  53.5 24.4 %collective-permute-start.14 = (f32[1040,128]{1,0:T(8,128)S(1)}, f32[1040,128]{1,0:T(8,128)S(1)}, u32[]{:S(2)}, u32[]{:S(2)}) collective-permute-start(f32[1040,128]{1,0:T(8,128)S(1)} %get-tuple-element.85), channel_id=1, source_target_pairs={{0,4},{4,8},{8,12},{12,16},{16,20},{20,24},{24,28},{1,5},{5,9},{9,... | collective-permute-start | bytes 1597448 | tf_op jit(solution)/shard_map/ppermute | solution.py:392
  57.1 17.5 %collective-permute-start.4 = (f32[64,1536]{1,0:T(8,128)S(1)}, f32[64,1536]{1,0:T(8,128)S(1)}, u32[]{:S(2)}, u32[]{:S(2)}) collective-permute-start(f32[64,1536]{1,0:T(8,128)S(1)} %get-tuple-element.66), channel_id=1, source_target_pairs={{1,4},{2,5},{3,6},{5,8},{6,9},{7,10},{9,12},{10,13},{11,14},{13,16... | collective-permute-start | bytes 1179656 | tf_op jit(solution)/shard_map/ppermute | solution.py:370
  58.4 21.6 %collective-permute-start.15 = (f32[64,1536]{1,0:T(8,128)S(1)}, f32[64,1536]{1,0:T(8,128)S(1)}, u32[]{:S(2)}, u32[]{:S(2)}) collective-permute-start(f32[64,1536]{1,0:T(8,128)S(1)} %get-tuple-element.88), channel_id=1, source_target_pairs={{1,4},{2,5},{3,6},{5,8},{6,9},{7,10},{9,12},{10,13},{11,14},{13,16... | collective-permute-start | bytes 1179656 | tf_op jit(solution)/shard_map/ppermute | solution.py:370
  76.0 9.9 %collective-permute-start.5 = (f32[1040,128]{1,0:T(8,128)S(1)}, f32[1040,128]{1,0:T(8,128)S(1)}, u32[]{:S(2)}, u32[]{:S(2)}) collective-permute-start(f32[1040,128]{1,0:T(8,128)S(1)} %get-tuple-element.67), channel_id=1, source_target_pairs={{0,4},{4,8},{8,12},{12,16},{16,20},{20,24},{24,28},{1,5},{5,9},{9,... | collective-permute-start | bytes 1597448 | tf_op jit(solution)/shard_map/ppermute | solution.py:392
  81.3 25.2 %collective-permute-start.16 = (f32[1040,128]{1,0:T(8,128)S(1)}, f32[1040,128]{1,0:T(8,128)S(1)}, u32[]{:S(2)}, u32[]{:S(2)}) collective-permute-start(f32[1040,128]{1,0:T(8,128)S(1)} %get-tuple-element.89), channel_id=1, source_target_pairs={{0,4},{4,8},{8,12},{12,16},{16,20},{20,24},{24,28},{1,5},{5,9},{9,... | collective-permute-start | bytes 1597448 | tf_op jit(solution)/shard_map/ppermute | solution.py:392
  83.2 20.1 %collective-permute-start.6 = (f32[64,1536]{1,0:T(8,128)S(1)}, f32[64,1536]{1,0:T(8,128)S(1)}, u32[]{:S(2)}, u32[]{:S(2)}) collective-permute-start(f32[64,1536]{1,0:T(8,128)S(1)} %get-tuple-element.70), channel_id=1, source_target_pairs={{1,4},{2,5},{3,6},{5,8},{6,9},{7,10},{9,12},{10,13},{11,14},{13,16... | collective-permute-start | bytes 1179656 | tf_op jit(solution)/shard_map/ppermute | solution.py:370
  84.5 24.1 %collective-permute-start.17 = (f32[64,1536]{1,0:T(8,128)S(1)}, f32[64,1536]{1,0:T(8,128)S(1)}, u32[]{:S(2)}, u32[]{:S(2)}) collective-permute-start(f32[64,1536]{1,0:T(8,128)S(1)} %get-tuple-element.92), channel_id=1, source_target_pairs={{1,4},{2,5},{3,6},{5,8},{6,9},{7,10},{9,12},{10,13},{11,14},{13,16... | collective-permute-start | bytes 1179656 | tf_op jit(solution)/shard_map/ppermute | solution.py:370
  104.6 10.1 %collective-permute-start.7 = (f32[1040,128]{1,0:T(8,128)S(1)}, f32[1040,128]{1,0:T(8,128)S(1)}, u32[]{:S(2)}, u32[]{:S(2)}) collective-permute-start(f32[1040,128]{1,0:T(8,128)S(1)} %get-tuple-element.71), channel_id=1, source_target_pairs={{0,4},{4,8},{8,12},{12,16},{16,20},{20,24},{24,28},{1,5},{5,9},{9,... | collective-permute-start | bytes 1597448 | tf_op jit(solution)/shard_map/ppermute | solution.py:392
  110.0 25.2 %collective-permute-start.18 = (f32[1040,128]{1,0:T(8,128)S(1)}, f32[1040,128]{1,0:T(8,128)S(1)}, u32[]{:S(2)}, u32[]{:S(2)}) collective-permute-start(f32[1040,128]{1,0:T(8,128)S(1)} %get-tuple-element.93), channel_id=1, source_target_pairs={{0,4},{4,8},{8,12},{12,16},{16,20},{20,24},{24,28},{1,5},{5,9},{9,... | collective-permute-start | bytes 1597448 | tf_op jit(solution)/shard_map/ppermute | solution.py:392
  111.9 20.1 %collective-permute-start.8 = (f32[64,1536]{1,0:T(8,128)S(1)}, f32[64,1536]{1,0:T(8,128)S(1)}, u32[]{:S(2)}, u32[]{:S(2)}) collective-permute-start(f32[64,1536]{1,0:T(8,128)S(1)} %get-tuple-element.74), channel_id=1, source_target_pairs={{1,4},{2,5},{3,6},{5,8},{6,9},{7,10},{9,12},{10,13},{11,14},{13,16... | collective-permute-start | bytes 1179656 | tf_op jit(solution)/shard_map/ppermute | solution.py:370
  113.2 24.1 %collective-permute-start.19 = (f32[64,1536]{1,0:T(8,128)S(1)}, f32[64,1536]{1,0:T(8,128)S(1)}, u32[]{:S(2)}, u32[]{:S(2)}) collective-permute-start(f32[64,1536]{1,0:T(8,128)S(1)} %get-tuple-element.96), channel_id=1, source_target_pairs={{1,4},{2,5},{3,6},{5,8},{6,9},{7,10},{9,12},{10,13},{11,14},{13,16... | collective-permute-start | bytes 1179656 | tf_op jit(solution)/shard_map/ppermute | solution.py:370
  133.3 9.9 %collective-permute-start.9 = (f32[1040,128]{1,0:T(8,128)S(1)}, f32[1040,128]{1,0:T(8,128)S(1)}, u32[]{:S(2)}, u32[]{:S(2)}) collective-permute-start(f32[1040,128]{1,0:T(8,128)S(1)} %get-tuple-element.75), channel_id=1, source_target_pairs={{0,4},{4,8},{8,12},{12,16},{16,20},{20,24},{24,28},{1,5},{5,9},{9,... | collective-permute-start | bytes 1597448 | tf_op jit(solution)/shard_map/ppermute | solution.py:392
  138.6 21.8 %collective-permute-start.20 = (f32[1040,128]{1,0:T(8,128)S(1)}, f32[1040,128]{1,0:T(8,128)S(1)}, u32[]{:S(2)}, u32[]{:S(2)}) collective-permute-start(f32[1040,128]{1,0:T(8,128)S(1)} %get-tuple-element.97), channel_id=1, source_target_pairs={{0,4},{4,8},{8,12},{12,16},{16,20},{20,24},{24,28},{1,5},{5,9},{9,... | collective-permute-start | bytes 1597448 | tf_op jit(solution)/shard_map/ppermute | solution.py:392
  140.6 18.5 %collective-permute-start.10 = (f32[64,1536]{1,0:T(8,128)S(1)}, f32[64,1536]{1,0:T(8,128)S(1)}, u32[]{:S(2)}, u32[]{:S(2)}) collective-permute-start(f32[64,1536]{1,0:T(8,128)S(1)} %get-tuple-element.78), channel_id=1, source_target_pairs={{1,4},{2,5},{3,6},{5,8},{6,9},{7,10},{9,12},{10,13},{11,14},{13,16... | collective-permute-start | bytes 1179656 | tf_op jit(solution)/shard_map/ppermute | solution.py:370
  141.9 21.4 %collective-permute-start.21 = (f32[64,1536]{1,0:T(8,128)S(1)}, f32[64,1536]{1,0:T(8,128)S(1)}, u32[]{:S(2)}, u32[]{:S(2)}) collective-permute-start(f32[64,1536]{1,0:T(8,128)S(1)} %get-tuple-element.100), channel_id=1, source_target_pairs={{1,4},{2,5},{3,6},{5,8},{6,9},{7,10},{9,12},{10,13},{11,14},{13,16... | collective-permute-start | bytes 1179656 | tf_op jit(solution)/shard_map/ppermute | solution.py:370
  164.7 3.4 %collective-permute-start.24 = (f32[16,128]{1,0:T(8,128)S(1)}, f32[16,128]{1,0:T(8,128)S(1)}, u32[]{:S(2)}, u32[]{:S(2)}) collective-permute-start(f32[16,128]{1,0:T(8,128)S(1)} %get-tuple-element.103.refs_2_), channel_id=1, source_target_pairs={{0,3},{1,2},{2,1},{3,0},{4,7},{5,6},{6,5},{7,4},{8,11},{9,10},{10,... | collective-permute-start | bytes 24584 | tf_op jit(solution)/shard_map/ppermute | solution.py:337
  164.7 4.4 %collective-permute-start.23 = (f32[16,128]{1,0:T(8,128)S(1)}, f32[16,128]{1,0:T(8,128)S(1)}, u32[]{:S(2)}, u32[]{:S(2)}) collective-permute-start(f32[16,128]{1,0:T(8,128)S(1)} %get-tuple-element.103.refs_2_), channel_id=1, source_target_pairs={{0,2},{1,3},{2,0},{3,1},{4,6},{5,7},{6,4},{7,5},{8,10},{9,11},{10,... | collective-permute-start | bytes 24584 | tf_op jit(solution)/shard_map/ppermute | solution.py:337
  168.1 2.5 %collective-permute-start.22 = (f32[16,128]{1,0:T(8,128)S(1)}, f32[16,128]{1,0:T(8,128)S(1)}, u32[]{:S(2)}, u32[]{:S(2)}) collective-permute-start(f32[16,128]{1,0:T(8,128)S(1)} %get-tuple-element.103.refs_2_), channel_id=1, source_target_pairs={{0,1},{1,0},{2,3},{3,2},{4,5},{5,4},{6,7},{7,6},{8,9},{9,8},{10,11... | collective-permute-start | bytes 24584 | tf_op jit(solution)/shard_map/ppermute | solution.py:337

commit v5 on v4

--- a/solution.py
+++ b/solution.py
@@ -93,7 +93,9 @@
     n_out, local, width, _, _ = dims
     rows = rows_ref.shape[1]
     depth, count = buffer.shape[0], n_out * local
-    order = [(n, s) for s in range(local) for n in range(n_out)]
+    order = [(n, s) for s in range(local) for n in range(n_out) if s + n >= local]
+    alone = len(order)
+    order += [(n, s) for s in range(local) for n in range(n_out) if s + n < local]
     copies = [
         pltpu.make_async_copy(w_ref.at[n, s], buffer.at[i % depth], sems.at[i % depth])
         for i, (n, s) in enumerate(order)
@@ -105,6 +107,21 @@
     ]
     for copy in inputs + copies[:depth]:
         copy.start()
+
+    def split(i):
+        n, s = order[i]
+        copies[i].wait()
+        w = buffer[i % depth]
+        hi = w.astype(BF)
+        lo = (w - hi.astype(F32)).astype(BF)
+        hi_ref[n, s] = hi
+        lo_ref[n, s] = lo
+        if i + depth < count:
+            copies[i + depth].start()
+        return hi, lo
+
+    for i in range(alone):
+        split(i)
     for copy in inputs:
         copy.wait()
     outcomes = outcome_buffer[:, 0].astype(F32)
@@ -115,20 +132,12 @@
         put(stack, q, 0, row_buffer[0, :, q * width : (q + 1) * width] * SCALE)
     total = jnp.zeros((rows, LANES), F32)
     selected = None
-    for i, (n, s) in enumerate(order):
-        copies[i].wait()
-        w = buffer[i % depth]
-        hi = w.astype(BF)
-        lo = (w - hi.astype(F32)).astype(BF)
-        hi_ref[n, s] = hi
-        lo_ref[n, s] = lo
-        if s + n < local:
-            value = product(stack[s + n], hi, lo)
-            total = total + folded_squares(value)
-            selected = jnp.where(choice == n, value, 0.0 if n == 0 else selected)
-        if i + depth < count:
-            copies[i + depth].start()
-        if n == n_out - 1:
+    for i in range(alone, count):
+        n, s = order[i]
+        value = product(stack[s + n], *split(i))
+        total = total + folded_squares(value)
+        selected = jnp.where(choice == n, value, 0.0 if n == 0 else selected)
+        if n == min(n_out, local - s) - 1:
             out_ref[:, s * width : (s + 1) * width] = selected
     depth = sums_ref.shape[0]
     row = lax.broadcasted_iota(jnp.int32, (depth, rows), 0)
@@ -171,18 +180,28 @@
 
 
 def near_kernel(dims, tick, chunk, *refs):
-    choice_ref, hi_ref, lo_ref, main_ref, entering_ref, out_ref, sums_ref, stack = refs
+    choice_ref, hi_ref, lo_ref, main_ref, entering_ref, *refs = refs
+    out_ref, sums_ref, stack, fresh, sem = refs
     n_out, local, width, rows, _ = dims
     own = slice(chunk * rows, (chunk + 1) * rows)
     at_start = lax.axis_index("site") == 0
-    group = 0
-    for q in range(local):
-        for start in range(0, width, LANES):
-            cols = slice(q * width + start, q * width + start + LANES)
-            fresh = entering_ref[tick - 1, own, cols] * SCALE
-            value = main_ref[group * rows : (group + 1) * rows]
-            put(stack, q, start, jnp.where(at_start, fresh, value))
-            group += 1
+    groups = local * width // LANES
+
+    @pl.when(at_start)
+    def _():
+        source = entering_ref.at[tick - 1, pl.ds(own.start, rows), :]
+        copy = pltpu.make_async_copy(source, fresh, sem)
+        copy.start()
+        copy.wait()
+        for q in range(local):
+            put(stack, q, 0, fresh[:, q * width : (q + 1) * width] * SCALE)
+
+    @pl.when(jnp.logical_not(at_start))
+    def _():
+        for group in range(groups):
+            q, start = divmod(group * LANES, width)
+            put(stack, q, start, main_ref[group * rows : (group + 1) * rows])
+
     choice = choice_ref[own, tick : tick + 1]
     total = jnp.zeros((rows, LANES), F32)
     for s in range(local):
@@ -193,7 +212,7 @@
             selected = jnp.where(choice == n, value, 0.0 if n == 0 else selected)
         out_ref[:, s * width : (s + 1) * width] = selected
     depth = sums_ref.shape[0]
-    old = main_ref[group * rows :, :rows]
+    old = main_ref[groups * rows :, :rows]
     sums_ref[...] = jnp.where(at_start, 0.0, old) + as_row(2 * tick + 1, total, depth)
 
 
@@ -202,8 +221,11 @@
     last = tick == ticks - 1
     refs = list(refs)
     choice_ref, hi_ref, lo_ref, base_ref, base_sums_ref = refs[:5]
-    halo_refs = refs[5 : 5 + len(halo)]
-    other_refs, stack = refs[5 + len(halo) : -1], refs[-1]
+    halo_refs, other_refs = refs[5 : 5 + len(halo)], refs[5 + len(halo) :]
+    if last:
+        *done_refs, out_ref, part_ref, stack = other_refs
+    else:
+        entering_ref, out_ref, edge_ref, stack, fresh, sem = other_refs
     own = slice(chunk * rows, (chunk + 1) * rows)
     base = slice(None) if base_ref.shape[0] == rows else own
     index = local
@@ -212,11 +234,12 @@
             value = ref[:, q * width : (q + 1) * width]
             put(stack, index, 0, value * SCALE if tick == 0 else value)
             index += 1
-    if last:
-        *done_refs, out_ref, part_ref = other_refs
-    else:
-        entering_ref, out_ref, edge_ref = other_refs
     at_end = lax.axis_index("site") == lax.axis_size("site") - 1
+    if not last:
+        cols = edge_ref.shape[1]
+        source = entering_ref.at[tick, pl.ds(own.start, rows), pl.ds(0, cols)]
+        copy = pltpu.make_async_copy(source, fresh, sem)
+        pl.when(at_end)(copy.start)
     choice = choice_ref[own, tick : tick + 1]
     total = jnp.zeros((rows, LANES), F32)
     picked = jnp.zeros((rows, LANES), F32)
@@ -235,8 +258,14 @@
             at = (s * width + start) // LANES * rows
             out_ref[at : at + rows] = selected[:, start : start + LANES]
         if s < halo[0]:
-            fresh = entering_ref[tick, own, cols] * SCALE
-            edge_ref[:, cols] = jnp.where(at_end, fresh, selected)
+            edge_ref[:, cols] = selected
+    if not last:
+
+        @pl.when(at_end)
+        def _():
+            copy.wait()
+            edge_ref[...] = fresh[...] * SCALE
+
     depth = base_sums_ref.shape[0]
     sums = base_sums_ref[:, base] + as_row(2 * tick + 1, total, depth)
     sums = sums + as_row(2 * tick, picked, depth)
@@ -248,21 +277,28 @@
         out_ref[local * width // LANES * rows :, :rows] = sums
 
 
-def step(kernel, dims, blocks, count, outs, operands):
+def step(kernel, dims, blocks, count, outs, operands, entering=None, cols=0):
     _, local, width, rows, _ = dims
+    specs = [VMEM_SPEC] * len(operands)
+    operands = [in_vmem(value) for value in operands]
+    scratch = [pltpu.VMEM((blocks, 2 * rows, width), BF)]
+    if entering is not None:
+        specs.append(pl.BlockSpec(memory_space=pltpu.HBM))
+        operands.append(pltpu.with_memory_space_constraint(entering, pltpu.HBM))
+        scratch += [pltpu.VMEM((rows, cols), F32), pltpu.SemaphoreType.DMA]
     return pl.pallas_call(
         kernel,
-        in_specs=[VMEM_SPEC] * len(operands),
+        in_specs=specs,
         out_specs=[VMEM_SPEC] * len(outs),
         out_shape=[pltpu.VMEM(shape, F32) for shape in outs],
-        scratch_shapes=[pltpu.VMEM((blocks, 2 * rows, width), BF)],
+        scratch_shapes=scratch,
         compiler_params=pltpu.CompilerParams(vmem_limit_bytes=VMEM_LIMIT),
         cost_estimate=pl.CostEstimate(
             flops=6 * rows * count * width * width,
             bytes_accessed=4 * rows * local * width,
             transcendentals=0,
         ),
-    )(*[in_vmem(value) for value in operands])
+    )(*operands)
 
 
 def near(dims, tick, ticks, chunk, shared, main, entering):
@@ -270,8 +306,8 @@
     count = sum(s + n < local for s in range(local) for n in range(n_out))
     outs = [(rows, local * width), (sums_depth(ticks), rows)]
     kernel = functools.partial(near_kernel, dims, tick, chunk)
-    operands = [*shared, main, entering]
-    return step(kernel, dims, local, count, outs, operands)
+    operands = [*shared, main]
+    return step(kernel, dims, local, count, outs, operands, entering, local * width)
 
 
 def far(dims, tick, ticks, chunk, shared, state, halos, entering, done):
@@ -280,14 +316,13 @@
     depth = sums_depth(ticks)
     if tick == ticks - 1:
         outs = [(rows, local * width), (depth, CHUNKS * rows)]
-        others = done
+        operands, fresh = [*shared, *state, *halos, *done], None
     else:
         outs = [(local * width // LANES * rows + depth, LANES), (rows, halo[0] * width)]
-        others = [entering]
+        operands, fresh = [*shared, *state, *halos], entering
     kernel = functools.partial(far_kernel, dims, tick, ticks, chunk)
-    operands = [*shared, *state, *halos, *others]
     blocks = local + sum(halo)
-    return step(kernel, dims, blocks, count, outs, operands)
+    return step(kernel, dims, blocks, count, outs, operands, fresh, halo[0] * width)
 
 
 def final_kernel(ticks, bond, chunks, copies, *refs):
@@ -372,9 +407,7 @@
 
     edges = first_edges(in_flight, rows, halo[0] * width)
     halos = [moved(edges[c], 0) for c in range(CHUNKS)]
-    hi, lo, base, base_sums, choice = opened(
-        dims, ticks, weights, in_flight, outcomes, prior_logp
-    )
+    hi, lo, base, base_sums, choice = opened(dims, ticks, weights, in_flight, outcomes, prior_logp)
     shared = [choice, hi, lo]
     states = [(base, base_sums)] * CHUNKS
     mains = [None] * CHUNKS
@@ -383,9 +416,7 @@
         for c in range(CHUNKS):
             if tick > 0:
                 states[c] = near(dims, tick, ticks, c, shared, mains[c], entering)
-            mains[c], other = far(
-                dims, tick, ticks, c, shared, states[c], halos[c], entering, done
-            )
+            mains[c], other = far(dims, tick, ticks, c, shared, states[c], halos[c], entering, done)
             if tick == ticks - 1:
                 done = [other]
                 continue

time: 173 us -> 174 us (level)
  Pallas kernels: 46.6 us -> 48.7 us
  transfers between devices with their start and end apart: 25 -> 25, of which waited for: 10 -> 10; matrix products, arithmetic and copies ran while one was open for 0% -> 0% of each run, Pallas kernels for 25% -> 26%
where the time goes in v5:
time: 174 us; the launch traced here: 173 us
  waiting for transfers between devices  76.6 us (44%)
  Pallas kernels  48.7 us (28%)
  starting transfers between devices  46.5 us (27%)
    ppermute x12, waiting for transfers between devices, moved(): lax.ppermute(edge[:, :blocks * width], ('site', 'sector'), pairs)  74.1 us
    pallas_call x22, Pallas kernels, step(): pl.pallas_call(kernel, in_specs=specs, out_specs=[VMEM_SPEC] * len(outs),...  38.3 us
    ppermute x10, starting transfers between devices, per_device(): mains[c] = lax.ppermute(mains[c], 'site', up)  27.3 us
    ppermute x12, starting transfers between devices, moved(): lax.ppermute(edge[:, :blocks * width], ('site', 'sector'), pairs)  15.7 us
    pallas_call x1, Pallas kernels, opened(): pl.pallas_call(functools.partial(open_kernel, dims, ticks), in_specs=[pl....  7.98 us
    ppermute x3, starting transfers between devices, partner(): return lax.ppermute(term, 'sector', [(d, d ^ mask) for d in range(sectors)])  3.49 us
  transfers between devices with their start and end apart: 25, of which 10 were waited for; matrix products, arithmetic and copies ran while one was open for 0% of the time, Pallas kernels for 26%

profile of v5, /device:TPU:1, one launch (start us, length us, event | category | flops | bytes accessed | tf_op | source)
XLA Modules:
  0.0 172.9 jit_solution(8230508494823019350)
XLA Ops:
  1.8 1.3 collective-permute-start
  3.1 1.3 collective-permute-start.11
  4.4 8.0 %opened.1 = (bf16[4,4,512,512]{3,2,1,0:T(8,128)(2,1)S(1)}, bf16[4,4,512,512]{3,2,1,0:T(8,128)(2,1)S(1)}, f32[128,2048]{1,0:T(8,128)S(1)}, f32[16,128]{1,0:T(8,128)S(1)}, f32[128,128]{1,0:T(8,128)S(1)}) custom-call(f32[4,4,512,512]{3,2,1,0:T(8,128)} %bitcast.1, f32[1,128,2048]{2,1,0:T(8,128)} %rows_ref.3, s32[6,1,128]{2,1,0:T(1,128)} %outcome_ref.1, ...), custom_call_target="tpu_custom_call" | custom-call | flops 1610612736 | bytes 16777216 | tf_op jit(solution)/shard_map/opened/pallas_call | solution.py:153
  12.4 2.2 %collective-permute-done.refs_5_ = f32[64,1536]{1,0:T(8,128)S(1)} collective-permute-done((f32[64,1536]{1,0:T(8,128)S(1)}, f32[64,1536]{1,0:T(8,128)S(1)}, u32[]{:S(2)}, u32[]{:S(2)}) %collective-permute-start) | collective-permute-done | bytes 393248 | tf_op jit(solution)/shard_map/ppermute | solution.py:405
  14.5 1.4 shard_map.68
  15.9 5.7 %collective-permute-start.1 = (f32[1040,128]{1,0:T(8,128)S(1)}, f32[1040,128]{1,0:T(8,128)S(1)}, u32[]{:S(2)}, u32[]{:S(2)}) collective-permute-start(f32[1040,128]{1,0:T(8,128)S(1)} %get-tuple-element.59), channel_id=1, source_target_pairs={{0,4},{4,8},{8,12},{12,16},{16,20},{20,24},{24,28},{1,5},{5,9},{9,... | collective-permute-start | bytes 1597448 | tf_op jit(solution)/shard_map/ppermute | solution.py:423
  21.6 1.3 collective-permute-done.11.refs_5_
  22.9 1.5 shard_map.79
  24.4 4.6 %collective-permute-start.12 = (f32[1040,128]{1,0:T(8,128)S(1)}, f32[1040,128]{1,0:T(8,128)S(1)}, u32[]{:S(2)}, u32[]{:S(2)}) collective-permute-start(f32[1040,128]{1,0:T(8,128)S(1)} %get-tuple-element.81), channel_id=1, source_target_pairs={{0,4},{4,8},{8,12},{12,16},{16,20},{20,24},{24,28},{1,5},{5,9},{9,... | collective-permute-start | bytes 1597448 | tf_op jit(solution)/shard_map/ppermute | solution.py:423
  29.0 1.3 collective-permute-start.2
  30.3 1.3 collective-permute-start.13
  31.6 2.2 %shard_map.69 = (f32[64,2048]{1,0:T(8,128)S(1)}, f32[16,64]{1,0:T(8,128)S(1)}) custom-call(f32[128,128]{1,0:T(8,128)S(1)} %get-tuple-element.53.refs_0_, bf16[4,4,512,512]{3,2,1,0:T(8,128)(2,1)S(1)} %get-tuple-element.54.refs_1_, bf16[4,4,512,512]{3,2,1,0:T(8,128)(2,1)S(1)} %get-tuple-element.55.refs_2_, f32[1040,128]{1,0:T(8,128)S(1)} %collective-permute-done.1.refs_3_, ...), custom_call_target="tpu_custom_call" | custom-call | flops 1006632960 | bytes 524288 | tf_op jit(solution)/shard_map/pallas_call | solution.py:289
  33.8 12.7 %collective-permute-done.2.refs_5_ = f32[64,1536]{1,0:T(8,128)S(1)} collective-permute-done((f32[64,1536]{1,0:T(8,128)S(1)}, f32[64,1536]{1,0:T(8,128)S(1)}, u32[]{:S(2)}, u32[]{:S(2)}) %collective-permute-start.2) | collective-permute-done | bytes 393248 | tf_op jit(solution)/shard_map/ppermute | solution.py:405
  46.6 1.3 shard_map.70
  47.9 1.9 %collective-permute-start.3 = (f32[1040,128]{1,0:T(8,128)S(1)}, f32[1040,128]{1,0:T(8,128)S(1)}, u32[]{:S(2)}, u32[]{:S(2)}) collective-permute-start(f32[1040,128]{1,0:T(8,128)S(1)} %get-tuple-element.63), channel_id=1, source_target_pairs={{0,4},{4,8},{8,12},{12,16},{16,20},{20,24},{24,28},{1,5},{5,9},{9,... | collective-permute-start | bytes 1597448 | tf_op jit(solution)/shard_map/ppermute | solution.py:423
  49.9 2.2 %shard_map.80 = (f32[64,2048]{1,0:T(8,128)S(1)}, f32[16,64]{1,0:T(8,128)S(1)}) custom-call(f32[128,128]{1,0:T(8,128)S(1)} %get-tuple-element.53.refs_0_, bf16[4,4,512,512]{3,2,1,0:T(8,128)(2,1)S(1)} %get-tuple-element.54.refs_1_, bf16[4,4,512,512]{3,2,1,0:T(8,128)(2,1)S(1)} %get-tuple-element.55.refs_2_, f32[1040,128]{1,0:T(8,128)S(1)} %collective-permute-done.12.refs_3_, ...), custom_call_target="tpu_custom_call" | custom-call | flops 1006632960 | bytes 524288 | tf_op jit(solution)/shard_map/pallas_call | solution.py:289
  52.0 1.3 shard_map.81
  53.4 3.6 %collective-permute-start.14 = (f32[1040,128]{1,0:T(8,128)S(1)}, f32[1040,128]{1,0:T(8,128)S(1)}, u32[]{:S(2)}, u32[]{:S(2)}) collective-permute-start(f32[1040,128]{1,0:T(8,128)S(1)} %get-tuple-element.85), channel_id=1, source_target_pairs={{0,4},{4,8},{8,12},{12,16},{16,20},{20,24},{24,28},{1,5},{5,9},{9,... | collective-permute-start | bytes 1597448 | tf_op jit(solution)/shard_map/ppermute | solution.py:423
  57.0 1.5 collective-permute-start.4
  58.5 1.3 collective-permute-start.15
  59.8 2.2 %shard_map.71 = (f32[64,2048]{1,0:T(8,128)S(1)}, f32[16,64]{1,0:T(8,128)S(1)}) custom-call(f32[128,128]{1,0:T(8,128)S(1)} %get-tuple-element.53.refs_0_, bf16[4,4,512,512]{3,2,1,0:T(8,128)(2,1)S(1)} %get-tuple-element.54.refs_1_, bf16[4,4,512,512]{3,2,1,0:T(8,128)(2,1)S(1)} %get-tuple-element.55.refs_2_, f32[1040,128]{1,0:T(8,128)S(1)} %collective-permute-done.3.refs_3_, ...), custom_call_target="tpu_custom_call" | custom-call | flops 1006632960 | bytes 524288 | tf_op jit(solution)/shard_map/pallas_call | solution.py:289
  62.0 13.2 %collective-permute-done.4.refs_5_ = f32[64,1536]{1,0:T(8,128)S(1)} collective-permute-done((f32[64,1536]{1,0:T(8,128)S(1)}, f32[64,1536]{1,0:T(8,128)S(1)}, u32[]{:S(2)}, u32[]{:S(2)}) %collective-permute-start.4) | collective-permute-done | bytes 393248 | tf_op jit(solution)/shard_map/ppermute | solution.py:405
  75.2 1.4 shard_map.72
  76.5 1.9 %collective-permute-start.5 = (f32[1040,128]{1,0:T(8,128)S(1)}, f32[1040,128]{1,0:T(8,128)S(1)}, u32[]{:S(2)}, u32[]{:S(2)}) collective-permute-start(f32[1040,128]{1,0:T(8,128)S(1)} %get-tuple-element.67), channel_id=1, source_target_pairs={{0,4},{4,8},{8,12},{12,16},{16,20},{20,24},{24,28},{1,5},{5,9},{9,... | collective-permute-start | bytes 1597448 | tf_op jit(solution)/shard_map/ppermute | solution.py:423
  78.5 2.2 %shard_map.82 = (f32[64,2048]{1,0:T(8,128)S(1)}, f32[16,64]{1,0:T(8,128)S(1)}) custom-call(f32[128,128]{1,0:T(8,128)S(1)} %get-tuple-element.53.refs_0_, bf16[4,4,512,512]{3,2,1,0:T(8,128)(2,1)S(1)} %get-tuple-element.54.refs_1_, bf16[4,4,512,512]{3,2,1,0:T(8,128)(2,1)S(1)} %get-tuple-element.55.refs_2_, f32[1040,128]{1,0:T(8,128)S(1)} %collective-permute-done.14.refs_3_, ...), custom_call_target="tpu_custom_call" | custom-call | flops 1006632960 | bytes 524288 | tf_op jit(solution)/shard_map/pallas_call | solution.py:289
  80.6 1.4 shard_map.83
  82.0 1.9 %collective-permute-start.16 = (f32[1040,128]{1,0:T(8,128)S(1)}, f32[1040,128]{1,0:T(8,128)S(1)}, u32[]{:S(2)}, u32[]{:S(2)}) collective-permute-start(f32[1040,128]{1,0:T(8,128)S(1)} %get-tuple-element.89), channel_id=1, source_target_pairs={{0,4},{4,8},{8,12},{12,16},{16,20},{20,24},{24,28},{1,5},{5,9},{9,... | collective-permute-start | bytes 1597448 | tf_op jit(solution)/shard_map/ppermute | solution.py:423
  86.5 2.2 %shard_map.73 = (f32[64,2048]{1,0:T(8,128)S(1)}, f32[16,64]{1,0:T(8,128)S(1)}) custom-call(f32[128,128]{1,0:T(8,128)S(1)} %get-tuple-element.53.refs_0_, bf16[4,4,512,512]{3,2,1,0:T(8,128)(2,1)S(1)} %get-tuple-element.54.refs_1_, bf16[4,4,512,512]{3,2,1,0:T(8,128)(2,1)S(1)} %get-tuple-element.55.refs_2_, f32[1040,128]{1,0:T(8,128)S(1)} %collective-permute-done.5.refs_3_, ...), custom_call_target="tpu_custom_call" | custom-call | flops 1006632960 | bytes 524288 | tf_op jit(solution)/shard_map/pallas_call | solution.py:289
  88.7 15.1 %collective-permute-done.6.refs_5_ = f32[64,1536]{1,0:T(8,128)S(1)} collective-permute-done((f32[64,1536]{1,0:T(8,128)S(1)}, f32[64,1536]{1,0:T(8,128)S(1)}, u32[]{:S(2)}, u32[]{:S(2)}) %collective-permute-start.6) | collective-permute-done | bytes 393248 | tf_op jit(solution)/shard_map/ppermute | solution.py:405
  103.8 1.4 shard_map.74
  105.2 1.9 %collective-permute-start.7 = (f32[1040,128]{1,0:T(8,128)S(1)}, f32[1040,128]{1,0:T(8,128)S(1)}, u32[]{:S(2)}, u32[]{:S(2)}) collective-permute-start(f32[1040,128]{1,0:T(8,128)S(1)} %get-tuple-element.71), channel_id=1, source_target_pairs={{0,4},{4,8},{8,12},{12,16},{16,20},{20,24},{24,28},{1,5},{5,9},{9,... | collective-permute-start | bytes 1597448 | tf_op jit(solution)/shard_map/ppermute | solution.py:423
  107.1 2.2 %shard_map.84 = (f32[64,2048]{1,0:T(8,128)S(1)}, f32[16,64]{1,0:T(8,128)S(1)}) custom-call(f32[128,128]{1,0:T(8,128)S(1)} %get-tuple-element.53.refs_0_, bf16[4,4,512,512]{3,2,1,0:T(8,128)(2,1)S(1)} %get-tuple-element.54.refs_1_, bf16[4,4,512,512]{3,2,1,0:T(8,128)(2,1)S(1)} %get-tuple-element.55.refs_2_, f32[1040,128]{1,0:T(8,128)S(1)} %collective-permute-done.16.refs_3_, ...), custom_call_target="tpu_custom_call" | custom-call | flops 1006632960 | bytes 524288 | tf_op jit(solution)/shard_map/pallas_call | solution.py:289
  109.3 1.4 shard_map.85
  110.7 1.9 %collective-permute-start.18 = (f32[1040,128]{1,0:T(8,128)S(1)}, f32[1040,128]{1,0:T(8,128)S(1)}, u32[]{:S(2)}, u32[]{:S(2)}) collective-permute-start(f32[1040,128]{1,0:T(8,128)S(1)} %get-tuple-element.93), channel_id=1, source_target_pairs={{0,4},{4,8},{8,12},{12,16},{16,20},{20,24},{24,28},{1,5},{5,9},{9,... | collective-permute-start | bytes 1597448 | tf_op jit(solution)/shard_map/ppermute | solution.py:423
  115.2 2.4 %shard_map.75 = (f32[64,2048]{1,0:T(8,128)S(1)}, f32[16,64]{1,0:T(8,128)S(1)}) custom-call(f32[128,128]{1,0:T(8,128)S(1)} %get-tuple-element.53.refs_0_, bf16[4,4,512,512]{3,2,1,0:T(8,128)(2,1)S(1)} %get-tuple-element.54.refs_1_, bf16[4,4,512,512]{3,2,1,0:T(8,128)(2,1)S(1)} %get-tuple-element.55.refs_2_, f32[1040,128]{1,0:T(8,128)S(1)} %collective-permute-done.7.refs_3_, ...), custom_call_target="tpu_custom_call" | custom-call | flops 1006632960 | bytes 524288 | tf_op jit(solution)/shard_map/pallas_call | solution.py:289
  117.6 15.1 %collective-permute-done.8.refs_5_ = f32[64,1536]{1,0:T(8,128)S(1)} collective-permute-done((f32[64,1536]{1,0:T(8,128)S(1)}, f32[64,1536]{1,0:T(8,128)S(1)}, u32[]{:S(2)}, u32[]{:S(2)}) %collective-permute-start.8) | collective-permute-done | bytes 393248 | tf_op jit(solution)/shard_map/ppermute | solution.py:405
  132.7 1.4 shard_map.76
  134.1 1.9 %collective-permute-start.9 = (f32[1040,128]{1,0:T(8,128)S(1)}, f32[1040,128]{1,0:T(8,128)S(1)}, u32[]{:S(2)}, u32[]{:S(2)}) collective-permute-start(f32[1040,128]{1,0:T(8,128)S(1)} %get-tuple-element.75), channel_id=1, source_target_pairs={{0,4},{4,8},{8,12},{12,16},{16,20},{20,24},{24,28},{1,5},{5,9},{9,... | collective-permute-start | bytes 1597448 | tf_op jit(solution)/shard_map/ppermute | solution.py:423
  136.0 2.2 %shard_map.86 = (f32[64,2048]{1,0:T(8,128)S(1)}, f32[16,64]{1,0:T(8,128)S(1)}) custom-call(f32[128,128]{1,0:T(8,128)S(1)} %get-tuple-element.53.refs_0_, bf16[4,4,512,512]{3,2,1,0:T(8,128)(2,1)S(1)} %get-tuple-element.54.refs_1_, bf16[4,4,512,512]{3,2,1,0:T(8,128)(2,1)S(1)} %get-tuple-element.55.refs_2_, f32[1040,128]{1,0:T(8,128)S(1)} %collective-permute-done.18.refs_3_, ...), custom_call_target="tpu_custom_call" | custom-call | flops 1006632960 | bytes 524288 | tf_op jit(solution)/shard_map/pallas_call | solution.py:289
  138.2 1.4 shard_map.87
  139.6 1.9 %collective-permute-start.20 = (f32[1040,128]{1,0:T(8,128)S(1)}, f32[1040,128]{1,0:T(8,128)S(1)}, u32[]{:S(2)}, u32[]{:S(2)}) collective-permute-start(f32[1040,128]{1,0:T(8,128)S(1)} %get-tuple-element.97), channel_id=1, source_target_pairs={{0,4},{4,8},{8,12},{12,16},{16,20},{20,24},{24,28},{1,5},{5,9},{9,... | collective-permute-start | bytes 1597448 | tf_op jit(solution)/shard_map/ppermute | solution.py:423
  144.1 2.2 %shard_map.77 = (f32[64,2048]{1,0:T(8,128)S(1)}, f32[16,64]{1,0:T(8,128)S(1)}) custom-call(f32[128,128]{1,0:T(8,128)S(1)} %get-tuple-element.53.refs_0_, bf16[4,4,512,512]{3,2,1,0:T(8,128)(2,1)S(1)} %get-tuple-element.54.refs_1_, bf16[4,4,512,512]{3,2,1,0:T(8,128)(2,1)S(1)} %get-tuple-element.55.refs_2_, f32[1040,128]{1,0:T(8,128)S(1)} %collective-permute-done.9.refs_3_, ...), custom_call_target="tpu_custom_call" | custom-call | flops 1006632960 | bytes 524288 | tf_op jit(solution)/shard_map/pallas_call | solution.py:289
  146.3 13.8 %collective-permute-done.10.refs_5_ = f32[64,1536]{1,0:T(8,128)S(1)} collective-permute-done((f32[64,1536]{1,0:T(8,128)S(1)}, f32[64,1536]{1,0:T(8,128)S(1)}, u32[]{:S(2)}, u32[]{:S(2)}) %collective-permute-start.10) | collective-permute-done | bytes 393248 | tf_op jit(solution)/shard_map/ppermute | solution.py:405
  160.0 1.3 shard_map.78
  161.4 2.2 %shard_map.88 = (f32[64,2048]{1,0:T(8,128)S(1)}, f32[16,64]{1,0:T(8,128)S(1)}) custom-call(f32[128,128]{1,0:T(8,128)S(1)} %get-tuple-element.53.refs_0_, bf16[4,4,512,512]{3,2,1,0:T(8,128)(2,1)S(1)} %get-tuple-element.54.refs_1_, bf16[4,4,512,512]{3,2,1,0:T(8,128)(2,1)S(1)} %get-tuple-element.55.refs_2_, f32[1040,128]{1,0:T(8,128)S(1)} %collective-permute-done.20.refs_3_, ...), custom_call_target="tpu_custom_call" | custom-call | flops 1006632960 | bytes 524288 | tf_op jit(solution)/shard_map/pallas_call | solution.py:289
  164.2 1.4 shard_map.89
  165.6 3.5 %collective-permute-start.23 = (f32[16,128]{1,0:T(8,128)S(1)}, f32[16,128]{1,0:T(8,128)S(1)}, u32[]{:S(2)}, u32[]{:S(2)}) collective-permute-start(f32[16,128]{1,0:T(8,128)S(1)} %get-tuple-element.103.refs_2_), channel_id=1, source_target_pairs={{0,2},{1,3},{2,0},{3,1},{4,6},{5,7},{6,4},{7,5},{8,10},{9,11},{10,... | collective-permute-start | bytes 24584 | tf_op jit(solution)/shard_map/ppermute | solution.py:372
  170.2 1.5 collective-permute-done.22.refs_3_
  (27 shorter events, 11.9 us)
Async XLA Ops:
  1.8 12.7 %collective-permute-start = (f32[64,1536]{1,0:T(8,128)S(1)}, f32[64,1536]{1,0:T(8,128)S(1)}, u32[]{:S(2)}, u32[]{:S(2)}) collective-permute-start(f32[64,1536]{1,0:T(8,128)S(1)} %get-tuple-element.58), channel_id=1, source_target_pairs={{1,0},{2,1},{3,2},{5,4},{6,5},{7,6},{9,8},{10,9},{11,10},{13,12},{... | collective-permute-start | bytes 1179656 | tf_op jit(solution)/shard_map/ppermute | solution.py:405
  3.1 19.9 %collective-permute-start.11 = (f32[64,1536]{1,0:T(8,128)S(1)}, f32[64,1536]{1,0:T(8,128)S(1)}, u32[]{:S(2)}, u32[]{:S(2)}) collective-permute-start(f32[64,1536]{1,0:T(8,128)S(1)} %get-tuple-element.80), channel_id=1, source_target_pairs={{1,0},{2,1},{3,2},{5,4},{6,5},{7,6},{9,8},{10,9},{11,10},{13,12},{... | collective-permute-start | bytes 1179656 | tf_op jit(solution)/shard_map/ppermute | solution.py:405
  15.9 15.8 %collective-permute-start.1 = (f32[1040,128]{1,0:T(8,128)S(1)}, f32[1040,128]{1,0:T(8,128)S(1)}, u32[]{:S(2)}, u32[]{:S(2)}) collective-permute-start(f32[1040,128]{1,0:T(8,128)S(1)} %get-tuple-element.59), channel_id=1, source_target_pairs={{0,4},{4,8},{8,12},{12,16},{16,20},{20,24},{24,28},{1,5},{5,9},{9,... | collective-permute-start | bytes 1597448 | tf_op jit(solution)/shard_map/ppermute | solution.py:423
  24.4 25.4 %collective-permute-start.12 = (f32[1040,128]{1,0:T(8,128)S(1)}, f32[1040,128]{1,0:T(8,128)S(1)}, u32[]{:S(2)}, u32[]{:S(2)}) collective-permute-start(f32[1040,128]{1,0:T(8,128)S(1)} %get-tuple-element.81), channel_id=1, source_target_pairs={{0,4},{4,8},{8,12},{12,16},{16,20},{20,24},{24,28},{1,5},{5,9},{9,... | collective-permute-start | bytes 1597448 | tf_op jit(solution)/shard_map/ppermute | solution.py:423
  29.0 17.5 %collective-permute-start.2 = (f32[64,1536]{1,0:T(8,128)S(1)}, f32[64,1536]{1,0:T(8,128)S(1)}, u32[]{:S(2)}, u32[]{:S(2)}) collective-permute-start(f32[64,1536]{1,0:T(8,128)S(1)} %get-tuple-element.62), channel_id=1, source_target_pairs={{1,4},{2,5},{3,6},{5,8},{6,9},{7,10},{9,12},{10,13},{11,14},{13,16... | collective-permute-start | bytes 1179656 | tf_op jit(solution)/shard_map/ppermute | solution.py:405
  30.3 21.7 %collective-permute-start.13 = (f32[64,1536]{1,0:T(8,128)S(1)}, f32[64,1536]{1,0:T(8,128)S(1)}, u32[]{:S(2)}, u32[]{:S(2)}) collective-permute-start(f32[64,1536]{1,0:T(8,128)S(1)} %get-tuple-element.84), channel_id=1, source_target_pairs={{1,4},{2,5},{3,6},{5,8},{6,9},{7,10},{9,12},{10,13},{11,14},{13,16... | collective-permute-start | bytes 1179656 | tf_op jit(solution)/shard_map/ppermute | solution.py:405
  47.9 11.9 %collective-permute-start.3 = (f32[1040,128]{1,0:T(8,128)S(1)}, f32[1040,128]{1,0:T(8,128)S(1)}, u32[]{:S(2)}, u32[]{:S(2)}) collective-permute-start(f32[1040,128]{1,0:T(8,128)S(1)} %get-tuple-element.63), channel_id=1, source_target_pairs={{0,4},{4,8},{8,12},{12,16},{16,20},{20,24},{24,28},{1,5},{5,9},{9,... | collective-permute-start | bytes 1597448 | tf_op jit(solution)/shard_map/ppermute | solution.py:423
  53.4 25.0 %collective-permute-start.14 = (f32[1040,128]{1,0:T(8,128)S(1)}, f32[1040,128]{1,0:T(8,128)S(1)}, u32[]{:S(2)}, u32[]{:S(2)}) collective-permute-start(f32[1040,128]{1,0:T(8,128)S(1)} %get-tuple-element.85), channel_id=1, source_target_pairs={{0,4},{4,8},{8,12},{12,16},{16,20},{20,24},{24,28},{1,5},{5,9},{9,... | collective-permute-start | bytes 1597448 | tf_op jit(solution)/shard_map/ppermute | solution.py:423
  57.0 18.1 %collective-permute-start.4 = (f32[64,1536]{1,0:T(8,128)S(1)}, f32[64,1536]{1,0:T(8,128)S(1)}, u32[]{:S(2)}, u32[]{:S(2)}) collective-permute-start(f32[64,1536]{1,0:T(8,128)S(1)} %get-tuple-element.66), channel_id=1, source_target_pairs={{1,4},{2,5},{3,6},{5,8},{6,9},{7,10},{9,12},{10,13},{11,14},{13,16... | collective-permute-start | bytes 1179656 | tf_op jit(solution)/shard_map/ppermute | solution.py:405
  58.5 22.1 %collective-permute-start.15 = (f32[64,1536]{1,0:T(8,128)S(1)}, f32[64,1536]{1,0:T(8,128)S(1)}, u32[]{:S(2)}, u32[]{:S(2)}) collective-permute-start(f32[64,1536]{1,0:T(8,128)S(1)} %get-tuple-element.88), channel_id=1, source_target_pairs={{1,4},{2,5},{3,6},{5,8},{6,9},{7,10},{9,12},{10,13},{11,14},{13,16... | collective-permute-start | bytes 1179656 | tf_op jit(solution)/shard_map/ppermute | solution.py:405
  76.5 10.0 %collective-permute-start.5 = (f32[1040,128]{1,0:T(8,128)S(1)}, f32[1040,128]{1,0:T(8,128)S(1)}, u32[]{:S(2)}, u32[]{:S(2)}) collective-permute-start(f32[1040,128]{1,0:T(8,128)S(1)} %get-tuple-element.67), channel_id=1, source_target_pairs={{0,4},{4,8},{8,12},{12,16},{16,20},{20,24},{24,28},{1,5},{5,9},{9,... | collective-permute-start | bytes 1597448 | tf_op jit(solution)/shard_map/ppermute | solution.py:423
  82.0 25.1 %collective-permute-start.16 = (f32[1040,128]{1,0:T(8,128)S(1)}, f32[1040,128]{1,0:T(8,128)S(1)}, u32[]{:S(2)}, u32[]{:S(2)}) collective-permute-start(f32[1040,128]{1,0:T(8,128)S(1)} %get-tuple-element.89), channel_id=1, source_target_pairs={{0,4},{4,8},{8,12},{12,16},{16,20},{20,24},{24,28},{1,5},{5,9},{9,... | collective-permute-start | bytes 1597448 | tf_op jit(solution)/shard_map/ppermute | solution.py:423
  83.9 19.9 %collective-permute-start.6 = (f32[64,1536]{1,0:T(8,128)S(1)}, f32[64,1536]{1,0:T(8,128)S(1)}, u32[]{:S(2)}, u32[]{:S(2)}) collective-permute-start(f32[64,1536]{1,0:T(8,128)S(1)} %get-tuple-element.70), channel_id=1, source_target_pairs={{1,4},{2,5},{3,6},{5,8},{6,9},{7,10},{9,12},{10,13},{11,14},{13,16... | collective-permute-start | bytes 1179656 | tf_op jit(solution)/shard_map/ppermute | solution.py:405
  85.2 24.1 %collective-permute-start.17 = (f32[64,1536]{1,0:T(8,128)S(1)}, f32[64,1536]{1,0:T(8,128)S(1)}, u32[]{:S(2)}, u32[]{:S(2)}) collective-permute-start(f32[64,1536]{1,0:T(8,128)S(1)} %get-tuple-element.92), channel_id=1, source_target_pairs={{1,4},{2,5},{3,6},{5,8},{6,9},{7,10},{9,12},{10,13},{11,14},{13,16... | collective-permute-start | bytes 1179656 | tf_op jit(solution)/shard_map/ppermute | solution.py:405
  105.2 10.0 %collective-permute-start.7 = (f32[1040,128]{1,0:T(8,128)S(1)}, f32[1040,128]{1,0:T(8,128)S(1)}, u32[]{:S(2)}, u32[]{:S(2)}) collective-permute-start(f32[1040,128]{1,0:T(8,128)S(1)} %get-tuple-element.71), channel_id=1, source_target_pairs={{0,4},{4,8},{8,12},{12,16},{16,20},{20,24},{24,28},{1,5},{5,9},{9,... | collective-permute-start | bytes 1597448 | tf_op jit(solution)/shard_map/ppermute | solution.py:423
  110.7 25.3 %collective-permute-start.18 = (f32[1040,128]{1,0:T(8,128)S(1)}, f32[1040,128]{1,0:T(8,128)S(1)}, u32[]{:S(2)}, u32[]{:S(2)}) collective-permute-start(f32[1040,128]{1,0:T(8,128)S(1)} %get-tuple-element.93), channel_id=1, source_target_pairs={{0,4},{4,8},{8,12},{12,16},{16,20},{20,24},{24,28},{1,5},{5,9},{9,... | collective-permute-start | bytes 1597448 | tf_op jit(solution)/shard_map/ppermute | solution.py:423
  112.6 20.1 %collective-permute-start.8 = (f32[64,1536]{1,0:T(8,128)S(1)}, f32[64,1536]{1,0:T(8,128)S(1)}, u32[]{:S(2)}, u32[]{:S(2)}) collective-permute-start(f32[64,1536]{1,0:T(8,128)S(1)} %get-tuple-element.74), channel_id=1, source_target_pairs={{1,4},{2,5},{3,6},{5,8},{6,9},{7,10},{9,12},{10,13},{11,14},{13,16... | collective-permute-start | bytes 1179656 | tf_op jit(solution)/shard_map/ppermute | solution.py:405
  113.9 24.3 %collective-permute-start.19 = (f32[64,1536]{1,0:T(8,128)S(1)}, f32[64,1536]{1,0:T(8,128)S(1)}, u32[]{:S(2)}, u32[]{:S(2)}) collective-permute-start(f32[64,1536]{1,0:T(8,128)S(1)} %get-tuple-element.96), channel_id=1, source_target_pairs={{1,4},{2,5},{3,6},{5,8},{6,9},{7,10},{9,12},{10,13},{11,14},{13,16... | collective-permute-start | bytes 1179656 | tf_op jit(solution)/shard_map/ppermute | solution.py:405
  134.1 10.0 %collective-permute-start.9 = (f32[1040,128]{1,0:T(8,128)S(1)}, f32[1040,128]{1,0:T(8,128)S(1)}, u32[]{:S(2)}, u32[]{:S(2)}) collective-permute-start(f32[1040,128]{1,0:T(8,128)S(1)} %get-tuple-element.75), channel_id=1, source_target_pairs={{0,4},{4,8},{8,12},{12,16},{16,20},{20,24},{24,28},{1,5},{5,9},{9,... | collective-permute-start | bytes 1597448 | tf_op jit(solution)/shard_map/ppermute | solution.py:423
  139.6 21.8 %collective-permute-start.20 = (f32[1040,128]{1,0:T(8,128)S(1)}, f32[1040,128]{1,0:T(8,128)S(1)}, u32[]{:S(2)}, u32[]{:S(2)}) collective-permute-start(f32[1040,128]{1,0:T(8,128)S(1)} %get-tuple-element.97), channel_id=1, source_target_pairs={{0,4},{4,8},{8,12},{12,16},{16,20},{20,24},{24,28},{1,5},{5,9},{9,... | collective-permute-start | bytes 1597448 | tf_op jit(solution)/shard_map/ppermute | solution.py:423
  141.5 18.6 %collective-permute-start.10 = (f32[64,1536]{1,0:T(8,128)S(1)}, f32[64,1536]{1,0:T(8,128)S(1)}, u32[]{:S(2)}, u32[]{:S(2)}) collective-permute-start(f32[64,1536]{1,0:T(8,128)S(1)} %get-tuple-element.78), channel_id=1, source_target_pairs={{1,4},{2,5},{3,6},{5,8},{6,9},{7,10},{9,12},{10,13},{11,14},{13,16... | collective-permute-start | bytes 1179656 | tf_op jit(solution)/shard_map/ppermute | solution.py:405
  142.8 21.5 %collective-permute-start.21 = (f32[64,1536]{1,0:T(8,128)S(1)}, f32[64,1536]{1,0:T(8,128)S(1)}, u32[]{:S(2)}, u32[]{:S(2)}) collective-permute-start(f32[64,1536]{1,0:T(8,128)S(1)} %get-tuple-element.100), channel_id=1, source_target_pairs={{1,4},{2,5},{3,6},{5,8},{6,9},{7,10},{9,12},{10,13},{11,14},{13,16... | collective-permute-start | bytes 1179656 | tf_op jit(solution)/shard_map/ppermute | solution.py:405
  165.6 3.5 %collective-permute-start.24 = (f32[16,128]{1,0:T(8,128)S(1)}, f32[16,128]{1,0:T(8,128)S(1)}, u32[]{:S(2)}, u32[]{:S(2)}) collective-permute-start(f32[16,128]{1,0:T(8,128)S(1)} %get-tuple-element.103.refs_2_), channel_id=1, source_target_pairs={{0,3},{1,2},{2,1},{3,0},{4,7},{5,6},{6,5},{7,4},{8,11},{9,10},{10,... | collective-permute-start | bytes 24584 | tf_op jit(solution)/shard_map/ppermute | solution.py:372
  165.6 4.5 %collective-permute-start.23 = (f32[16,128]{1,0:T(8,128)S(1)}, f32[16,128]{1,0:T(8,128)S(1)}, u32[]{:S(2)}, u32[]{:S(2)}) collective-permute-start(f32[16,128]{1,0:T(8,128)S(1)} %get-tuple-element.103.refs_2_), channel_id=1, source_target_pairs={{0,2},{1,3},{2,0},{3,1},{4,6},{5,7},{6,4},{7,5},{8,10},{9,11},{10,... | collective-permute-start | bytes 24584 | tf_op jit(solution)/shard_map/ppermute | solution.py:372
  169.1 2.5 %collective-permute-start.22 = (f32[16,128]{1,0:T(8,128)S(1)}, f32[16,128]{1,0:T(8,128)S(1)}, u32[]{:S(2)}, u32[]{:S(2)}) collective-permute-start(f32[16,128]{1,0:T(8,128)S(1)} %get-tuple-element.103.refs_2_), channel_id=1, source_target_pairs={{0,1},{1,0},{2,3},{3,2},{4,5},{5,4},{6,7},{7,6},{8,9},{9,8},{10,11... | collective-permute-start | bytes 24584 | tf_op jit(solution)/shard_map/ppermute | solution.py:372

commit v6 on v5

--- a/solution.py
+++ b/solution.py
@@ -105,7 +105,7 @@
         pltpu.make_async_copy(rows_ref, row_buffer, sems.at[depth + 1]),
         pltpu.make_async_copy(prior_ref, prior_buffer, sems.at[depth + 2]),
     ]
-    for copy in inputs + copies[:depth]:
+    for copy in copies[:depth] + inputs:
         copy.start()
 
     def split(i):
@@ -193,8 +193,11 @@
         copy = pltpu.make_async_copy(source, fresh, sem)
         copy.start()
         copy.wait()
-        for q in range(local):
-            put(stack, q, 0, fresh[:, q * width : (q + 1) * width] * SCALE)
+
+        @pl.loop(0, local)
+        def _(q):
+            cols = pl.ds(pl.multiple_of(q * width, LANES), width)
+            put(stack, q, 0, fresh[:, cols] * SCALE)
 
     @pl.when(jnp.logical_not(at_start))
     def _():
@@ -236,8 +239,8 @@
             index += 1
     at_end = lax.axis_index("site") == lax.axis_size("site") - 1
     if not last:
-        cols = edge_ref.shape[1]
-        source = entering_ref.at[tick, pl.ds(own.start, rows), pl.ds(0, cols)]
+        cols_sent = edge_ref.shape[1]
+        source = entering_ref.at[tick, pl.ds(own.start, rows), pl.ds(0, cols_sent)]
         copy = pltpu.make_async_copy(source, fresh, sem)
         pl.when(at_end)(copy.start)
     choice = choice_ref[own, tick : tick + 1]
@@ -264,7 +267,11 @@
         @pl.when(at_end)
         def _():
             copy.wait()
-            edge_ref[...] = fresh[...] * SCALE
+
+            @pl.loop(0, cols_sent // LANES)
+            def _(group):
+                cols = pl.ds(pl.multiple_of(group * LANES, LANES), LANES)
+                edge_ref[:, cols] = fresh[:, cols] * SCALE
 
     depth = base_sums_ref.shape[0]
     sums = base_sums_ref[:, base] + as_row(2 * tick + 1, total, depth)

time: 174 us -> 174 us (level)
  no operation moved by 1% of the time
where the time goes in v6:
time: 174 us; the launch traced here: 173 us
  waiting for transfers between devices  76.3 us (44%)
  Pallas kernels  49.2 us (28%)
  starting transfers between devices  46.4 us (27%)
    ppermute x12, waiting for transfers between devices, moved(): lax.ppermute(edge[:, :blocks * width], ('site', 'sector'), pairs)  73.8 us
    pallas_call x22, Pallas kernels, step(): pl.pallas_call(kernel, in_specs=specs, out_specs=[VMEM_SPEC] * len(outs),...  38.5 us
    ppermute x10, starting transfers between devices, per_device(): mains[c] = lax.ppermute(mains[c], 'site', up)  27.3 us
    ppermute x12, starting transfers between devices, moved(): lax.ppermute(edge[:, :blocks * width], ('site', 'sector'), pairs)  15.5 us
    pallas_call x1, Pallas kernels, opened(): pl.pallas_call(functools.partial(open_kernel, dims, ticks), in_specs=[pl....  8.39 us
    ppermute x3, starting transfers between devices, partner(): return lax.ppermute(term, 'sector', [(d, d ^ mask) for d in range(sectors)])  3.59 us
  transfers between devices with their start and end apart: 25, of which 10 were waited for; matrix products, arithmetic and copies ran while one was open for 0% of the time, Pallas kernels for 26%

profile of v6, /device:TPU:1, one launch (start us, length us, event | category | flops | bytes accessed | tf_op | source)
XLA Modules:
  0.0 173.1 jit_solution(5351555437191247640)
XLA Ops:
  1.8 1.3 collective-permute-start
  3.1 1.3 collective-permute-start.11
  4.4 8.4 %opened.1 = (bf16[4,4,512,512]{3,2,1,0:T(8,128)(2,1)S(1)}, bf16[4,4,512,512]{3,2,1,0:T(8,128)(2,1)S(1)}, f32[128,2048]{1,0:T(8,128)S(1)}, f32[16,128]{1,0:T(8,128)S(1)}, f32[128,128]{1,0:T(8,128)S(1)}) custom-call(f32[4,4,512,512]{3,2,1,0:T(8,128)} %bitcast.1, f32[1,128,2048]{2,1,0:T(8,128)} %rows_ref.3, s32[6,1,128]{2,1,0:T(1,128)} %outcome_ref.1, ...), custom_call_target="tpu_custom_call" | custom-call | flops 1610612736 | bytes 16777216 | tf_op jit(solution)/shard_map/opened/pallas_call | solution.py:153
  12.8 1.8 %collective-permute-done.refs_5_ = f32[64,1536]{1,0:T(8,128)S(1)} collective-permute-done((f32[64,1536]{1,0:T(8,128)S(1)}, f32[64,1536]{1,0:T(8,128)S(1)}, u32[]{:S(2)}, u32[]{:S(2)}) %collective-permute-start) | collective-permute-done | bytes 393248 | tf_op jit(solution)/shard_map/ppermute | solution.py:412
  14.5 1.4 shard_map.68
  15.9 5.7 %collective-permute-start.1 = (f32[1040,128]{1,0:T(8,128)S(1)}, f32[1040,128]{1,0:T(8,128)S(1)}, u32[]{:S(2)}, u32[]{:S(2)}) collective-permute-start(f32[1040,128]{1,0:T(8,128)S(1)} %get-tuple-element.59), channel_id=1, source_target_pairs={{0,4},{4,8},{8,12},{12,16},{16,20},{20,24},{24,28},{1,5},{5,9},{9,... | collective-permute-start | bytes 1597448 | tf_op jit(solution)/shard_map/ppermute | solution.py:430
  21.6 1.3 collective-permute-done.11.refs_5_
  22.9 1.5 shard_map.79
  24.4 4.6 %collective-permute-start.12 = (f32[1040,128]{1,0:T(8,128)S(1)}, f32[1040,128]{1,0:T(8,128)S(1)}, u32[]{:S(2)}, u32[]{:S(2)}) collective-permute-start(f32[1040,128]{1,0:T(8,128)S(1)} %get-tuple-element.81), channel_id=1, source_target_pairs={{0,4},{4,8},{8,12},{12,16},{16,20},{20,24},{24,28},{1,5},{5,9},{9,... | collective-permute-start | bytes 1597448 | tf_op jit(solution)/shard_map/ppermute | solution.py:430
  31.6 2.2 %shard_map.69 = (f32[64,2048]{1,0:T(8,128)S(1)}, f32[16,64]{1,0:T(8,128)S(1)}) custom-call(f32[128,128]{1,0:T(8,128)S(1)} %get-tuple-element.53.refs_0_, bf16[4,4,512,512]{3,2,1,0:T(8,128)(2,1)S(1)} %get-tuple-element.54.refs_1_, bf16[4,4,512,512]{3,2,1,0:T(8,128)(2,1)S(1)} %get-tuple-element.55.refs_2_, f32[1040,128]{1,0:T(8,128)S(1)} %collective-permute-done.1.refs_3_, ...), custom_call_target="tpu_custom_call" | custom-call | flops 1006632960 | bytes 524288 | tf_op jit(solution)/shard_map/pallas_call | solution.py:296
  33.8 12.7 %collective-permute-done.2.refs_5_ = f32[64,1536]{1,0:T(8,128)S(1)} collective-permute-done((f32[64,1536]{1,0:T(8,128)S(1)}, f32[64,1536]{1,0:T(8,128)S(1)}, u32[]{:S(2)}, u32[]{:S(2)}) %collective-permute-start.2) | collective-permute-done | bytes 393248 | tf_op jit(solution)/shard_map/ppermute | solution.py:412
  46.6 1.3 shard_map.70
  47.9 1.9 %collective-permute-start.3 = (f32[1040,128]{1,0:T(8,128)S(1)}, f32[1040,128]{1,0:T(8,128)S(1)}, u32[]{:S(2)}, u32[]{:S(2)}) collective-permute-start(f32[1040,128]{1,0:T(8,128)S(1)} %get-tuple-element.63), channel_id=1, source_target_pairs={{0,4},{4,8},{8,12},{12,16},{16,20},{20,24},{24,28},{1,5},{5,9},{9,... | collective-permute-start | bytes 1597448 | tf_op jit(solution)/shard_map/ppermute | solution.py:430
  49.9 2.2 %shard_map.80 = (f32[64,2048]{1,0:T(8,128)S(1)}, f32[16,64]{1,0:T(8,128)S(1)}) custom-call(f32[128,128]{1,0:T(8,128)S(1)} %get-tuple-element.53.refs_0_, bf16[4,4,512,512]{3,2,1,0:T(8,128)(2,1)S(1)} %get-tuple-element.54.refs_1_, bf16[4,4,512,512]{3,2,1,0:T(8,128)(2,1)S(1)} %get-tuple-element.55.refs_2_, f32[1040,128]{1,0:T(8,128)S(1)} %collective-permute-done.12.refs_3_, ...), custom_call_target="tpu_custom_call" | custom-call | flops 1006632960 | bytes 524288 | tf_op jit(solution)/shard_map/pallas_call | solution.py:296
  52.0 1.3 shard_map.81
  53.4 3.6 %collective-permute-start.14 = (f32[1040,128]{1,0:T(8,128)S(1)}, f32[1040,128]{1,0:T(8,128)S(1)}, u32[]{:S(2)}, u32[]{:S(2)}) collective-permute-start(f32[1040,128]{1,0:T(8,128)S(1)} %get-tuple-element.85), channel_id=1, source_target_pairs={{0,4},{4,8},{8,12},{12,16},{16,20},{20,24},{24,28},{1,5},{5,9},{9,... | collective-permute-start | bytes 1597448 | tf_op jit(solution)/shard_map/ppermute | solution.py:430
  57.0 1.3 collective-permute-start.4
  58.3 1.3 collective-permute-start.15
  59.6 2.4 %shard_map.71 = (f32[64,2048]{1,0:T(8,128)S(1)}, f32[16,64]{1,0:T(8,128)S(1)}) custom-call(f32[128,128]{1,0:T(8,128)S(1)} %get-tuple-element.53.refs_0_, bf16[4,4,512,512]{3,2,1,0:T(8,128)(2,1)S(1)} %get-tuple-element.54.refs_1_, bf16[4,4,512,512]{3,2,1,0:T(8,128)(2,1)S(1)} %get-tuple-element.55.refs_2_, f32[1040,128]{1,0:T(8,128)S(1)} %collective-permute-done.3.refs_3_, ...), custom_call_target="tpu_custom_call" | custom-call | flops 1006632960 | bytes 524288 | tf_op jit(solution)/shard_map/pallas_call | solution.py:296
  62.0 13.0 %collective-permute-done.4.refs_5_ = f32[64,1536]{1,0:T(8,128)S(1)} collective-permute-done((f32[64,1536]{1,0:T(8,128)S(1)}, f32[64,1536]{1,0:T(8,128)S(1)}, u32[]{:S(2)}, u32[]{:S(2)}) %collective-permute-start.4) | collective-permute-done | bytes 393248 | tf_op jit(solution)/shard_map/ppermute | solution.py:412
  75.0 1.3 shard_map.72
  76.3 1.9 %collective-permute-start.5 = (f32[1040,128]{1,0:T(8,128)S(1)}, f32[1040,128]{1,0:T(8,128)S(1)}, u32[]{:S(2)}, u32[]{:S(2)}) collective-permute-start(f32[1040,128]{1,0:T(8,128)S(1)} %get-tuple-element.67), channel_id=1, source_target_pairs={{0,4},{4,8},{8,12},{12,16},{16,20},{20,24},{24,28},{1,5},{5,9},{9,... | collective-permute-start | bytes 1597448 | tf_op jit(solution)/shard_map/ppermute | solution.py:430
  78.3 2.2 %shard_map.82 = (f32[64,2048]{1,0:T(8,128)S(1)}, f32[16,64]{1,0:T(8,128)S(1)}) custom-call(f32[128,128]{1,0:T(8,128)S(1)} %get-tuple-element.53.refs_0_, bf16[4,4,512,512]{3,2,1,0:T(8,128)(2,1)S(1)} %get-tuple-element.54.refs_1_, bf16[4,4,512,512]{3,2,1,0:T(8,128)(2,1)S(1)} %get-tuple-element.55.refs_2_, f32[1040,128]{1,0:T(8,128)S(1)} %collective-permute-done.14.refs_3_, ...), custom_call_target="tpu_custom_call" | custom-call | flops 1006632960 | bytes 524288 | tf_op jit(solution)/shard_map/pallas_call | solution.py:296
  80.5 1.4 shard_map.83
  81.8 1.9 %collective-permute-start.16 = (f32[1040,128]{1,0:T(8,128)S(1)}, f32[1040,128]{1,0:T(8,128)S(1)}, u32[]{:S(2)}, u32[]{:S(2)}) collective-permute-start(f32[1040,128]{1,0:T(8,128)S(1)} %get-tuple-element.89), channel_id=1, source_target_pairs={{0,4},{4,8},{8,12},{12,16},{16,20},{20,24},{24,28},{1,5},{5,9},{9,... | collective-permute-start | bytes 1597448 | tf_op jit(solution)/shard_map/ppermute | solution.py:430
  86.4 2.2 %shard_map.73 = (f32[64,2048]{1,0:T(8,128)S(1)}, f32[16,64]{1,0:T(8,128)S(1)}) custom-call(f32[128,128]{1,0:T(8,128)S(1)} %get-tuple-element.53.refs_0_, bf16[4,4,512,512]{3,2,1,0:T(8,128)(2,1)S(1)} %get-tuple-element.54.refs_1_, bf16[4,4,512,512]{3,2,1,0:T(8,128)(2,1)S(1)} %get-tuple-element.55.refs_2_, f32[1040,128]{1,0:T(8,128)S(1)} %collective-permute-done.5.refs_3_, ...), custom_call_target="tpu_custom_call" | custom-call | flops 1006632960 | bytes 524288 | tf_op jit(solution)/shard_map/pallas_call | solution.py:296
  88.6 15.3 %collective-permute-done.6.refs_5_ = f32[64,1536]{1,0:T(8,128)S(1)} collective-permute-done((f32[64,1536]{1,0:T(8,128)S(1)}, f32[64,1536]{1,0:T(8,128)S(1)}, u32[]{:S(2)}, u32[]{:S(2)}) %collective-permute-start.6) | collective-permute-done | bytes 393248 | tf_op jit(solution)/shard_map/ppermute | solution.py:412
  103.9 1.4 shard_map.74
  105.2 1.9 %collective-permute-start.7 = (f32[1040,128]{1,0:T(8,128)S(1)}, f32[1040,128]{1,0:T(8,128)S(1)}, u32[]{:S(2)}, u32[]{:S(2)}) collective-permute-start(f32[1040,128]{1,0:T(8,128)S(1)} %get-tuple-element.71), channel_id=1, source_target_pairs={{0,4},{4,8},{8,12},{12,16},{16,20},{20,24},{24,28},{1,5},{5,9},{9,... | collective-permute-start | bytes 1597448 | tf_op jit(solution)/shard_map/ppermute | solution.py:430
  107.2 2.2 %shard_map.84 = (f32[64,2048]{1,0:T(8,128)S(1)}, f32[16,64]{1,0:T(8,128)S(1)}) custom-call(f32[128,128]{1,0:T(8,128)S(1)} %get-tuple-element.53.refs_0_, bf16[4,4,512,512]{3,2,1,0:T(8,128)(2,1)S(1)} %get-tuple-element.54.refs_1_, bf16[4,4,512,512]{3,2,1,0:T(8,128)(2,1)S(1)} %get-tuple-element.55.refs_2_, f32[1040,128]{1,0:T(8,128)S(1)} %collective-permute-done.16.refs_3_, ...), custom_call_target="tpu_custom_call" | custom-call | flops 1006632960 | bytes 524288 | tf_op jit(solution)/shard_map/pallas_call | solution.py:296
  109.3 1.4 shard_map.85
  110.7 1.9 %collective-permute-start.18 = (f32[1040,128]{1,0:T(8,128)S(1)}, f32[1040,128]{1,0:T(8,128)S(1)}, u32[]{:S(2)}, u32[]{:S(2)}) collective-permute-start(f32[1040,128]{1,0:T(8,128)S(1)} %get-tuple-element.93), channel_id=1, source_target_pairs={{0,4},{4,8},{8,12},{12,16},{16,20},{20,24},{24,28},{1,5},{5,9},{9,... | collective-permute-start | bytes 1597448 | tf_op jit(solution)/shard_map/ppermute | solution.py:430
  112.6 1.3 collective-permute-start.8
  113.9 1.3 collective-permute-start.19
  115.2 2.4 %shard_map.75 = (f32[64,2048]{1,0:T(8,128)S(1)}, f32[16,64]{1,0:T(8,128)S(1)}) custom-call(f32[128,128]{1,0:T(8,128)S(1)} %get-tuple-element.53.refs_0_, bf16[4,4,512,512]{3,2,1,0:T(8,128)(2,1)S(1)} %get-tuple-element.54.refs_1_, bf16[4,4,512,512]{3,2,1,0:T(8,128)(2,1)S(1)} %get-tuple-element.55.refs_2_, f32[1040,128]{1,0:T(8,128)S(1)} %collective-permute-done.7.refs_3_, ...), custom_call_target="tpu_custom_call" | custom-call | flops 1006632960 | bytes 524288 | tf_op jit(solution)/shard_map/pallas_call | solution.py:296
  117.7 15.1 %collective-permute-done.8.refs_5_ = f32[64,1536]{1,0:T(8,128)S(1)} collective-permute-done((f32[64,1536]{1,0:T(8,128)S(1)}, f32[64,1536]{1,0:T(8,128)S(1)}, u32[]{:S(2)}, u32[]{:S(2)}) %collective-permute-start.8) | collective-permute-done | bytes 393248 | tf_op jit(solution)/shard_map/ppermute | solution.py:412
  132.7 1.4 shard_map.76
  134.1 1.9 %collective-permute-start.9 = (f32[1040,128]{1,0:T(8,128)S(1)}, f32[1040,128]{1,0:T(8,128)S(1)}, u32[]{:S(2)}, u32[]{:S(2)}) collective-permute-start(f32[1040,128]{1,0:T(8,128)S(1)} %get-tuple-element.75), channel_id=1, source_target_pairs={{0,4},{4,8},{8,12},{12,16},{16,20},{20,24},{24,28},{1,5},{5,9},{9,... | collective-permute-start | bytes 1597448 | tf_op jit(solution)/shard_map/ppermute | solution.py:430
  136.0 2.2 %shard_map.86 = (f32[64,2048]{1,0:T(8,128)S(1)}, f32[16,64]{1,0:T(8,128)S(1)}) custom-call(f32[128,128]{1,0:T(8,128)S(1)} %get-tuple-element.53.refs_0_, bf16[4,4,512,512]{3,2,1,0:T(8,128)(2,1)S(1)} %get-tuple-element.54.refs_1_, bf16[4,4,512,512]{3,2,1,0:T(8,128)(2,1)S(1)} %get-tuple-element.55.refs_2_, f32[1040,128]{1,0:T(8,128)S(1)} %collective-permute-done.18.refs_3_, ...), custom_call_target="tpu_custom_call" | custom-call | flops 1006632960 | bytes 524288 | tf_op jit(solution)/shard_map/pallas_call | solution.py:296
  138.2 1.4 shard_map.87
  139.6 1.9 %collective-permute-start.20 = (f32[1040,128]{1,0:T(8,128)S(1)}, f32[1040,128]{1,0:T(8,128)S(1)}, u32[]{:S(2)}, u32[]{:S(2)}) collective-permute-start(f32[1040,128]{1,0:T(8,128)S(1)} %get-tuple-element.97), channel_id=1, source_target_pairs={{0,4},{4,8},{8,12},{12,16},{16,20},{20,24},{24,28},{1,5},{5,9},{9,... | collective-permute-start | bytes 1597448 | tf_op jit(solution)/shard_map/ppermute | solution.py:430
  144.1 2.2 %shard_map.77 = (f32[64,2048]{1,0:T(8,128)S(1)}, f32[16,64]{1,0:T(8,128)S(1)}) custom-call(f32[128,128]{1,0:T(8,128)S(1)} %get-tuple-element.53.refs_0_, bf16[4,4,512,512]{3,2,1,0:T(8,128)(2,1)S(1)} %get-tuple-element.54.refs_1_, bf16[4,4,512,512]{3,2,1,0:T(8,128)(2,1)S(1)} %get-tuple-element.55.refs_2_, f32[1040,128]{1,0:T(8,128)S(1)} %collective-permute-done.9.refs_3_, ...), custom_call_target="tpu_custom_call" | custom-call | flops 1006632960 | bytes 524288 | tf_op jit(solution)/shard_map/pallas_call | solution.py:296
  146.3 13.9 %collective-permute-done.10.refs_5_ = f32[64,1536]{1,0:T(8,128)S(1)} collective-permute-done((f32[64,1536]{1,0:T(8,128)S(1)}, f32[64,1536]{1,0:T(8,128)S(1)}, u32[]{:S(2)}, u32[]{:S(2)}) %collective-permute-start.10) | collective-permute-done | bytes 393248 | tf_op jit(solution)/shard_map/ppermute | solution.py:412
  160.2 1.3 shard_map.78
  161.5 2.2 %shard_map.88 = (f32[64,2048]{1,0:T(8,128)S(1)}, f32[16,64]{1,0:T(8,128)S(1)}) custom-call(f32[128,128]{1,0:T(8,128)S(1)} %get-tuple-element.53.refs_0_, bf16[4,4,512,512]{3,2,1,0:T(8,128)(2,1)S(1)} %get-tuple-element.54.refs_1_, bf16[4,4,512,512]{3,2,1,0:T(8,128)(2,1)S(1)} %get-tuple-element.55.refs_2_, f32[1040,128]{1,0:T(8,128)S(1)} %collective-permute-done.20.refs_3_, ...), custom_call_target="tpu_custom_call" | custom-call | flops 1006632960 | bytes 524288 | tf_op jit(solution)/shard_map/pallas_call | solution.py:296
  164.4 1.4 shard_map.89
  165.8 3.6 %collective-permute-start.23 = (f32[16,128]{1,0:T(8,128)S(1)}, f32[16,128]{1,0:T(8,128)S(1)}, u32[]{:S(2)}, u32[]{:S(2)}) collective-permute-start(f32[16,128]{1,0:T(8,128)S(1)} %get-tuple-element.103.refs_2_), channel_id=1, source_target_pairs={{0,2},{1,3},{2,0},{3,1},{4,6},{5,7},{6,4},{7,5},{8,10},{9,11},{10,... | collective-permute-start | bytes 24584 | tf_op jit(solution)/shard_map/ppermute | solution.py:379
  170.4 1.5 collective-permute-done.22.refs_3_
  (27 shorter events, 11.9 us)
Async XLA Ops:
  1.8 12.7 %collective-permute-start = (f32[64,1536]{1,0:T(8,128)S(1)}, f32[64,1536]{1,0:T(8,128)S(1)}, u32[]{:S(2)}, u32[]{:S(2)}) collective-permute-start(f32[64,1536]{1,0:T(8,128)S(1)} %get-tuple-element.58), channel_id=1, source_target_pairs={{1,0},{2,1},{3,2},{5,4},{6,5},{7,6},{9,8},{10,9},{11,10},{13,12},{... | collective-permute-start | bytes 1179656 | tf_op jit(solution)/shard_map/ppermute | solution.py:412
  3.1 19.9 %collective-permute-start.11 = (f32[64,1536]{1,0:T(8,128)S(1)}, f32[64,1536]{1,0:T(8,128)S(1)}, u32[]{:S(2)}, u32[]{:S(2)}) collective-permute-start(f32[64,1536]{1,0:T(8,128)S(1)} %get-tuple-element.80), channel_id=1, source_target_pairs={{1,0},{2,1},{3,2},{5,4},{6,5},{7,6},{9,8},{10,9},{11,10},{13,12},{... | collective-permute-start | bytes 1179656 | tf_op jit(solution)/shard_map/ppermute | solution.py:412
  15.9 15.8 %collective-permute-start.1 = (f32[1040,128]{1,0:T(8,128)S(1)}, f32[1040,128]{1,0:T(8,128)S(1)}, u32[]{:S(2)}, u32[]{:S(2)}) collective-permute-start(f32[1040,128]{1,0:T(8,128)S(1)} %get-tuple-element.59), channel_id=1, source_target_pairs={{0,4},{4,8},{8,12},{12,16},{16,20},{20,24},{24,28},{1,5},{5,9},{9,... | collective-permute-start | bytes 1597448 | tf_op jit(solution)/shard_map/ppermute | solution.py:430
  24.4 25.4 %collective-permute-start.12 = (f32[1040,128]{1,0:T(8,128)S(1)}, f32[1040,128]{1,0:T(8,128)S(1)}, u32[]{:S(2)}, u32[]{:S(2)}) collective-permute-start(f32[1040,128]{1,0:T(8,128)S(1)} %get-tuple-element.81), channel_id=1, source_target_pairs={{0,4},{4,8},{8,12},{12,16},{16,20},{20,24},{24,28},{1,5},{5,9},{9,... | collective-permute-start | bytes 1597448 | tf_op jit(solution)/shard_map/ppermute | solution.py:430
  29.0 17.5 %collective-permute-start.2 = (f32[64,1536]{1,0:T(8,128)S(1)}, f32[64,1536]{1,0:T(8,128)S(1)}, u32[]{:S(2)}, u32[]{:S(2)}) collective-permute-start(f32[64,1536]{1,0:T(8,128)S(1)} %get-tuple-element.62), channel_id=1, source_target_pairs={{1,4},{2,5},{3,6},{5,8},{6,9},{7,10},{9,12},{10,13},{11,14},{13,16... | collective-permute-start | bytes 1179656 | tf_op jit(solution)/shard_map/ppermute | solution.py:412
  30.3 21.7 %collective-permute-start.13 = (f32[64,1536]{1,0:T(8,128)S(1)}, f32[64,1536]{1,0:T(8,128)S(1)}, u32[]{:S(2)}, u32[]{:S(2)}) collective-permute-start(f32[64,1536]{1,0:T(8,128)S(1)} %get-tuple-element.84), channel_id=1, source_target_pairs={{1,4},{2,5},{3,6},{5,8},{6,9},{7,10},{9,12},{10,13},{11,14},{13,16... | collective-permute-start | bytes 1179656 | tf_op jit(solution)/shard_map/ppermute | solution.py:412
  47.9 11.7 %collective-permute-start.3 = (f32[1040,128]{1,0:T(8,128)S(1)}, f32[1040,128]{1,0:T(8,128)S(1)}, u32[]{:S(2)}, u32[]{:S(2)}) collective-permute-start(f32[1040,128]{1,0:T(8,128)S(1)} %get-tuple-element.63), channel_id=1, source_target_pairs={{0,4},{4,8},{8,12},{12,16},{16,20},{20,24},{24,28},{1,5},{5,9},{9,... | collective-permute-start | bytes 1597448 | tf_op jit(solution)/shard_map/ppermute | solution.py:430
  53.4 24.9 %collective-permute-start.14 = (f32[1040,128]{1,0:T(8,128)S(1)}, f32[1040,128]{1,0:T(8,128)S(1)}, u32[]{:S(2)}, u32[]{:S(2)}) collective-permute-start(f32[1040,128]{1,0:T(8,128)S(1)} %get-tuple-element.85), channel_id=1, source_target_pairs={{0,4},{4,8},{8,12},{12,16},{16,20},{20,24},{24,28},{1,5},{5,9},{9,... | collective-permute-start | bytes 1597448 | tf_op jit(solution)/shard_map/ppermute | solution.py:430
  57.0 18.0 %collective-permute-start.4 = (f32[64,1536]{1,0:T(8,128)S(1)}, f32[64,1536]{1,0:T(8,128)S(1)}, u32[]{:S(2)}, u32[]{:S(2)}) collective-permute-start(f32[64,1536]{1,0:T(8,128)S(1)} %get-tuple-element.66), channel_id=1, source_target_pairs={{1,4},{2,5},{3,6},{5,8},{6,9},{7,10},{9,12},{10,13},{11,14},{13,16... | collective-permute-start | bytes 1179656 | tf_op jit(solution)/shard_map/ppermute | solution.py:412
  58.3 22.2 %collective-permute-start.15 = (f32[64,1536]{1,0:T(8,128)S(1)}, f32[64,1536]{1,0:T(8,128)S(1)}, u32[]{:S(2)}, u32[]{:S(2)}) collective-permute-start(f32[64,1536]{1,0:T(8,128)S(1)} %get-tuple-element.88), channel_id=1, source_target_pairs={{1,4},{2,5},{3,6},{5,8},{6,9},{7,10},{9,12},{10,13},{11,14},{13,16... | collective-permute-start | bytes 1179656 | tf_op jit(solution)/shard_map/ppermute | solution.py:412
  76.3 10.0 %collective-permute-start.5 = (f32[1040,128]{1,0:T(8,128)S(1)}, f32[1040,128]{1,0:T(8,128)S(1)}, u32[]{:S(2)}, u32[]{:S(2)}) collective-permute-start(f32[1040,128]{1,0:T(8,128)S(1)} %get-tuple-element.67), channel_id=1, source_target_pairs={{0,4},{4,8},{8,12},{12,16},{16,20},{20,24},{24,28},{1,5},{5,9},{9,... | collective-permute-start | bytes 1597448 | tf_op jit(solution)/shard_map/ppermute | solution.py:430
  81.8 25.3 %collective-permute-start.16 = (f32[1040,128]{1,0:T(8,128)S(1)}, f32[1040,128]{1,0:T(8,128)S(1)}, u32[]{:S(2)}, u32[]{:S(2)}) collective-permute-start(f32[1040,128]{1,0:T(8,128)S(1)} %get-tuple-element.89), channel_id=1, source_target_pairs={{0,4},{4,8},{8,12},{12,16},{16,20},{20,24},{24,28},{1,5},{5,9},{9,... | collective-permute-start | bytes 1597448 | tf_op jit(solution)/shard_map/ppermute | solution.py:430
  83.8 20.1 %collective-permute-start.6 = (f32[64,1536]{1,0:T(8,128)S(1)}, f32[64,1536]{1,0:T(8,128)S(1)}, u32[]{:S(2)}, u32[]{:S(2)}) collective-permute-start(f32[64,1536]{1,0:T(8,128)S(1)} %get-tuple-element.70), channel_id=1, source_target_pairs={{1,4},{2,5},{3,6},{5,8},{6,9},{7,10},{9,12},{10,13},{11,14},{13,16... | collective-permute-start | bytes 1179656 | tf_op jit(solution)/shard_map/ppermute | solution.py:412
  85.1 24.3 %collective-permute-start.17 = (f32[64,1536]{1,0:T(8,128)S(1)}, f32[64,1536]{1,0:T(8,128)S(1)}, u32[]{:S(2)}, u32[]{:S(2)}) collective-permute-start(f32[64,1536]{1,0:T(8,128)S(1)} %get-tuple-element.92), channel_id=1, source_target_pairs={{1,4},{2,5},{3,6},{5,8},{6,9},{7,10},{9,12},{10,13},{11,14},{13,16... | collective-permute-start | bytes 1179656 | tf_op jit(solution)/shard_map/ppermute | solution.py:412
  105.2 10.0 %collective-permute-start.7 = (f32[1040,128]{1,0:T(8,128)S(1)}, f32[1040,128]{1,0:T(8,128)S(1)}, u32[]{:S(2)}, u32[]{:S(2)}) collective-permute-start(f32[1040,128]{1,0:T(8,128)S(1)} %get-tuple-element.71), channel_id=1, source_target_pairs={{0,4},{4,8},{8,12},{12,16},{16,20},{20,24},{24,28},{1,5},{5,9},{9,... | collective-permute-start | bytes 1597448 | tf_op jit(solution)/shard_map/ppermute | solution.py:430
  110.7 25.3 %collective-permute-start.18 = (f32[1040,128]{1,0:T(8,128)S(1)}, f32[1040,128]{1,0:T(8,128)S(1)}, u32[]{:S(2)}, u32[]{:S(2)}) collective-permute-start(f32[1040,128]{1,0:T(8,128)S(1)} %get-tuple-element.93), channel_id=1, source_target_pairs={{0,4},{4,8},{8,12},{12,16},{16,20},{20,24},{24,28},{1,5},{5,9},{9,... | collective-permute-start | bytes 1597448 | tf_op jit(solution)/shard_map/ppermute | solution.py:430
  112.6 20.1 %collective-permute-start.8 = (f32[64,1536]{1,0:T(8,128)S(1)}, f32[64,1536]{1,0:T(8,128)S(1)}, u32[]{:S(2)}, u32[]{:S(2)}) collective-permute-start(f32[64,1536]{1,0:T(8,128)S(1)} %get-tuple-element.74), channel_id=1, source_target_pairs={{1,4},{2,5},{3,6},{5,8},{6,9},{7,10},{9,12},{10,13},{11,14},{13,16... | collective-permute-start | bytes 1179656 | tf_op jit(solution)/shard_map/ppermute | solution.py:412
  113.9 24.3 %collective-permute-start.19 = (f32[64,1536]{1,0:T(8,128)S(1)}, f32[64,1536]{1,0:T(8,128)S(1)}, u32[]{:S(2)}, u32[]{:S(2)}) collective-permute-start(f32[64,1536]{1,0:T(8,128)S(1)} %get-tuple-element.96), channel_id=1, source_target_pairs={{1,4},{2,5},{3,6},{5,8},{6,9},{7,10},{9,12},{10,13},{11,14},{13,16... | collective-permute-start | bytes 1179656 | tf_op jit(solution)/shard_map/ppermute | solution.py:412
  134.1 10.0 %collective-permute-start.9 = (f32[1040,128]{1,0:T(8,128)S(1)}, f32[1040,128]{1,0:T(8,128)S(1)}, u32[]{:S(2)}, u32[]{:S(2)}) collective-permute-start(f32[1040,128]{1,0:T(8,128)S(1)} %get-tuple-element.75), channel_id=1, source_target_pairs={{0,4},{4,8},{8,12},{12,16},{16,20},{20,24},{24,28},{1,5},{5,9},{9,... | collective-permute-start | bytes 1597448 | tf_op jit(solution)/shard_map/ppermute | solution.py:430
  139.6 21.9 %collective-permute-start.20 = (f32[1040,128]{1,0:T(8,128)S(1)}, f32[1040,128]{1,0:T(8,128)S(1)}, u32[]{:S(2)}, u32[]{:S(2)}) collective-permute-start(f32[1040,128]{1,0:T(8,128)S(1)} %get-tuple-element.97), channel_id=1, source_target_pairs={{0,4},{4,8},{8,12},{12,16},{16,20},{20,24},{24,28},{1,5},{5,9},{9,... | collective-permute-start | bytes 1597448 | tf_op jit(solution)/shard_map/ppermute | solution.py:430
  141.5 18.7 %collective-permute-start.10 = (f32[64,1536]{1,0:T(8,128)S(1)}, f32[64,1536]{1,0:T(8,128)S(1)}, u32[]{:S(2)}, u32[]{:S(2)}) collective-permute-start(f32[64,1536]{1,0:T(8,128)S(1)} %get-tuple-element.78), channel_id=1, source_target_pairs={{1,4},{2,5},{3,6},{5,8},{6,9},{7,10},{9,12},{10,13},{11,14},{13,16... | collective-permute-start | bytes 1179656 | tf_op jit(solution)/shard_map/ppermute | solution.py:412
  142.8 21.6 %collective-permute-start.21 = (f32[64,1536]{1,0:T(8,128)S(1)}, f32[64,1536]{1,0:T(8,128)S(1)}, u32[]{:S(2)}, u32[]{:S(2)}) collective-permute-start(f32[64,1536]{1,0:T(8,128)S(1)} %get-tuple-element.100), channel_id=1, source_target_pairs={{1,4},{2,5},{3,6},{5,8},{6,9},{7,10},{9,12},{10,13},{11,14},{13,16... | collective-permute-start | bytes 1179656 | tf_op jit(solution)/shard_map/ppermute | solution.py:412
  165.8 3.6 %collective-permute-start.24 = (f32[16,128]{1,0:T(8,128)S(1)}, f32[16,128]{1,0:T(8,128)S(1)}, u32[]{:S(2)}, u32[]{:S(2)}) collective-permute-start(f32[16,128]{1,0:T(8,128)S(1)} %get-tuple-element.103.refs_2_), channel_id=1, source_target_pairs={{0,3},{1,2},{2,1},{3,0},{4,7},{5,6},{6,5},{7,4},{8,11},{9,10},{10,... | collective-permute-start | bytes 24584 | tf_op jit(solution)/shard_map/ppermute | solution.py:379
  165.8 4.6 %collective-permute-start.23 = (f32[16,128]{1,0:T(8,128)S(1)}, f32[16,128]{1,0:T(8,128)S(1)}, u32[]{:S(2)}, u32[]{:S(2)}) collective-permute-start(f32[16,128]{1,0:T(8,128)S(1)} %get-tuple-element.103.refs_2_), channel_id=1, source_target_pairs={{0,2},{1,3},{2,0},{3,1},{4,6},{5,7},{6,4},{7,5},{8,10},{9,11},{10,... | collective-permute-start | bytes 24584 | tf_op jit(solution)/shard_map/ppermute | solution.py:379
  169.3 2.5 %collective-permute-start.22 = (f32[16,128]{1,0:T(8,128)S(1)}, f32[16,128]{1,0:T(8,128)S(1)}, u32[]{:S(2)}, u32[]{:S(2)}) collective-permute-start(f32[16,128]{1,0:T(8,128)S(1)} %get-tuple-element.103.refs_2_), channel_id=1, source_target_pairs={{0,1},{1,0},{2,3},{3,2},{4,5},{5,4},{6,7},{7,6},{8,9},{9,8},{10,11... | collective-permute-start | bytes 24584 | tf_op jit(solution)/shard_map/ppermute | solution.py:379
